TPU v7x, 32 devices: a whole 2x2x4 slice. The times are simulated.
32 devices in a mesh: blk: 4 (over x, core), ulysses: 8 (over z, y).
Axes of the slice: x: 2, y: 2, z: 4, core: 2. Of those that a mesh axis runs over, the one named last changes fastest.
Arguments:
- query_rows: bfloat16 [32, 4096, 128], P(None, ('blk', 'ulysses')), may hold values from -160 to 160
- out_grad: bfloat16 [32, 4096, 128], P(None, ('blk', 'ulysses')), may hold values from -6 to 6
- key_rows: bfloat16 [32, 512, 128], P(None, 'blk'), may hold values from -6 to 6
- value_rows: bfloat16 [32, 512, 128], P(None, 'blk'), may hold values from -6 to 6
- routes: int32 [4, 4], replicated, may hold values from 0 to 7
Outputs:
- query_grad: bfloat16 [32, 4096, 128], P(None, ('blk', 'ulysses'))
- key_grad: float32 [32, 512, 128], P(None, ('blk', 'ulysses'))
- value_grad: float32 [32, 512, 128], P(None, ('blk', 'ulysses'))
All inputs are finite; a program needn't handle non-finite values.
Results may differ from a plain program's by a relative error of at most 0.0056.
Values may be sent and summed in bfloat16 or wider, within the bound.
No kernel may reach another device: no remote copies, remote signals or barrier semaphores. Data moves between devices by JAX's collectives and lax.ppermute only.
A program may use at most 64 MiB of HBM per device.

v0:
```python
import functools
import math

import jax
import jax.numpy as jnp
from jax import lax
from jax.experimental import pallas as pl
from jax.experimental.pallas import tpu as pltpu
from jax.sharding import PartitionSpec as P


KB = 16
PLAN = ((20, 12, False, 0), (0, 20, True, 0))
STEP_HEADS = 10
VMEM_SMALL = 8 << 20
VMEM_ATTEND = 24 << 20


def far_masks(groups):
    return [1] + [mask for even in range(2, groups, 2) for mask in (even, even ^ 1)]


def pick_kernel(cuts, groups, routes, query, grad, keys, values, *rest):
    outs, arrived = list(rest[:-1]), rest[-1]
    group = lax.axis_index("blk")
    half = lax.axis_index("ulysses") % 2
    copies = []
    for number, (first_head, heads, paired, _) in enumerate(cuts):
        if paired:
            heads //= 2
            other = first_head + (1 - half) * heads
            first_head = first_head + half * heads
            swapped = outs.pop(0)
            for side, rows in enumerate((query, grad)):
                copies.append(
                    pltpu.make_async_copy(
                        rows.at[pl.ds(other, heads)],
                        swapped.at[side],
                        arrived.at[number, groups - 1, side],
                    )
                )
        for index, mask in enumerate(far_masks(groups)):
            out = outs[(index + 1) // 2]
            out = out if index == 0 else out.at[(index + 1) % 2]
            start = pl.multiple_of(routes[group ^ mask, group] * KB, KB)
            for side, rows in enumerate((keys, values)):
                copies.append(
                    pltpu.make_async_copy(
                        rows.at[pl.ds(first_head, heads), pl.ds(start, KB)],
                        out.at[side],
                        arrived.at[number, index, side],
                    )
                )
        outs = outs[groups // 2 :]
    for copy in copies:
        copy.start()
    for copy in copies:
        copy.wait()


def pick(routes, query, grad, keys, values, groups, cuts):
    _, tokens, head_dim = query.shape
    shapes, counts = [], []
    for _, heads, paired, _ in cuts:
        heads = heads // 2 if paired else heads
        block = (2, heads, KB, head_dim)
        swap = [(2, heads, tokens, head_dim)] if paired else []
        shapes += swap + [block] + [(2,) + block] * (groups // 2 - 1)
        counts.append(len(swap) + groups // 2)
    outs = pl.pallas_call(
        functools.partial(pick_kernel, cuts, groups),
        out_shape=[jax.ShapeDtypeStruct(shape, jnp.bfloat16) for shape in shapes],
        in_specs=[pl.BlockSpec(memory_space=pltpu.SMEM)]
        + [pl.BlockSpec(memory_space=pltpu.HBM)] * 4,
        out_specs=[pl.BlockSpec(memory_space=pltpu.VMEM)] * len(shapes),
        scratch_shapes=[pltpu.SemaphoreType.DMA((len(cuts), groups, 2))],
        compiler_params=pltpu.CompilerParams(vmem_limit_bytes=VMEM_SMALL),
        name="pick",
    )(routes, query, grad, keys, values)
    picked = []
    for count, cut in zip(counts, cuts):
        mine, outs = outs[:count], outs[count:]
        picked.append((mine[0], mine[1:]) if cut[2] else (None, mine))
    return picked


def slot_specs(groups, step_heads, rows, head_dim):
    flat = pl.BlockSpec((2, step_heads) + rows + (head_dim,), lambda i, *_: (0, i) + (0,) * (len(rows) + 1))
    half = pl.BlockSpec(
        (None, 2, step_heads) + rows + (head_dim,), lambda i, *_: (0, 0, i) + (0,) * (len(rows) + 1)
    )
    return [flat] + [half, flat] * (groups // 2 - 1)


def attend_kernel(masks, has_alias, paired, _, query, grad, keys, values, *rest):
    slots = len(masks)
    far_rows = rest[:slots]
    swapped = rest[slots] if paired else None
    rest = rest[slots + has_alias + paired :]
    if paired:
        other_out, rest = rest[0], rest[1:]
    query_out, own_out, near_out = rest[:3]
    pair_outs = rest[3 : 3 + slots // 2]
    far_outs = [near_out] + [out.at[half] for out in pair_outs for half in range(2)]
    score_ref, dweight_ref, half_ref, dscore_ref = rest[3 + slots // 2 :]
    heads, tokens, head_dim = query.shape
    group_keys = keys.shape[1]
    group = lax.axis_index("blk")
    rank = lax.axis_index("ulysses")
    key_stride = tokens * lax.axis_size("ulysses") // group_keys
    score_scale = 1.0 / math.sqrt(head_dim)
    exp_scale = score_scale * math.log2(math.e)
    key_at = lax.broadcasted_iota(jnp.int32, (group_keys, tokens), 0) * key_stride
    token_at = lax.broadcasted_iota(jnp.int32, (group_keys, tokens), 1)
    sources = (rank, rank ^ 1) if paired else (rank,)
    hidden = [
        jnp.concatenate(
            [jnp.where(key_at <= token_at + source * tokens, 0.0, -jnp.inf) for source in sources],
            axis=1,
        )
    ]
    for mask in masks:
        seen = jnp.where((group ^ mask) < group, 0.0, -jnp.inf)
        hidden.append(jnp.full((KB, tokens * len(sources)), seen, jnp.float32))
    hidden = jnp.concatenate(hidden, axis=0)
    nt = (((1,), (1,)), ((), ()))
    tn = (((0,), (0,)), ((), ()))

    def near(rows, side, head):
        return jnp.concatenate([rows[head]] + [far[side, head] for far in far_rows], axis=0)

    def both(rows, side, head):
        if not paired:
            return rows[head]
        return jnp.concatenate([rows[head], swapped[side, head]], axis=0)

    for head in range(heads):
        score_ref[head] = lax.dot_general(
            near(keys, 0, head), both(query, 0, head), nt, preferred_element_type=jnp.float32
        )
        dweight_ref[head] = lax.dot_general(
            near(values, 1, head), both(grad, 1, head), nt, preferred_element_type=jnp.float32
        )
    for head in range(heads):
        scores = score_ref[head] + hidden
        dweights = dweight_ref[head]
        row_max = jnp.max(scores, axis=0, keepdims=True)
        expsum = jnp.exp2((scores - row_max) * exp_scale)
        weights = expsum * (1.0 / jnp.sum(expsum, axis=0, keepdims=True))
        weights_half = weights.astype(jnp.bfloat16)
        delta = jnp.sum(weights_half.astype(jnp.float32) * dweights, axis=0, keepdims=True)
        half_ref[head] = weights_half
        dscore_ref[head] = (weights * (dweights - delta)).astype(jnp.bfloat16)
    for head in range(heads):
        dscore = dscore_ref[head]
        query_grad = lax.dot_general(
            dscore, near(keys, 0, head), tn, preferred_element_type=jnp.float32
        )
        query_grad = (query_grad * score_scale).astype(jnp.bfloat16)
        query_out[head] = query_grad[:tokens]
        if paired:
            other_out[head] = query_grad[tokens:]
        key_part = jnp.dot(dscore, both(query, 0, head), preferred_element_type=jnp.float32)
        value_part = jnp.dot(
            half_ref[head], both(grad, 1, head), preferred_element_type=jnp.float32
        )
        parts = ((key_part * score_scale).astype(jnp.bfloat16), value_part.astype(jnp.bfloat16))
        for side, part in enumerate(parts):
            own_out[side, head] = part[:group_keys]
            for slot, far_out in enumerate(far_outs):
                start = group_keys + slot * KB
                far_out[side, head] = part[start : start + KB]


def step_of(heads, *offsets):
    return max(step for step in range(1, STEP_HEADS + 1) if math.gcd(step, heads, *offsets) == step)


def attend(half, query, grad, keys, values, far, swapped, groups, cut, query_out):
    first_head, heads, paired, _ = cut
    _, tokens, head_dim = query.shape
    group_keys = keys.shape[1]
    masks = far_masks(groups)
    near_keys = group_keys + KB * len(masks)
    if paired:
        heads //= 2
    step_heads = step_of(heads, first_head)
    first_step = first_head // step_heads
    half_steps = heads // step_heads if paired else 0

    def rows(count):
        return pl.BlockSpec(
            (step_heads, count, head_dim),
            lambda i, half: (first_step + half[0] * half_steps + i, 0, 0),
        )

    def pair(count):
        return pl.BlockSpec((2, step_heads, count, head_dim), lambda i, half: (0, i, 0, 0))

    both = pl.BlockSpec((2, 2, step_heads, KB, head_dim), lambda i, half: (0, 0, i, 0, 0))
    block = (2, heads, KB, head_dim)
    shapes = [query.shape, (2, heads, group_keys, head_dim), block]
    shapes += [(2,) + block] * (groups // 2 - 1)
    out_specs = [rows(tokens), pair(group_keys), pair(KB)] + [both] * (groups // 2 - 1)
    operands = [half, query, grad, keys, values, *far]
    in_specs = [rows(tokens), rows(tokens), rows(group_keys), rows(group_keys)]
    in_specs += slot_specs(groups, step_heads, (KB,), head_dim)
    aliases = {}
    if paired:
        operands.append(swapped)
        in_specs.append(pair(tokens))
        shapes.insert(0, (heads, tokens, head_dim))
        out_specs.insert(
            0, pl.BlockSpec((step_heads, tokens, head_dim), lambda i, half: (i, 0, 0))
        )
    if query_out is not None:
        aliases = {len(operands): int(paired)}
        operands.append(query_out)
        in_specs.append(pl.BlockSpec(memory_space=pl.ANY))
    scores = (step_heads, near_keys, tokens * (1 + paired))
    outs = pl.pallas_call(
        functools.partial(attend_kernel, masks, query_out is not None, paired),
        out_shape=[jax.ShapeDtypeStruct(shape, jnp.bfloat16) for shape in shapes],
        grid_spec=pltpu.PrefetchScalarGridSpec(
            num_scalar_prefetch=1,
            grid=(heads // step_heads,),
            in_specs=in_specs,
            out_specs=out_specs,
            scratch_shapes=[pltpu.VMEM(scores, jnp.float32)] * 2
            + [pltpu.VMEM(scores, jnp.bfloat16)] * 2,
        ),
        input_output_aliases=aliases,
        compiler_params=pltpu.CompilerParams(vmem_limit_bytes=VMEM_ATTEND),
        name="attend",
    )(*operands)
    other = None
    if paired:
        other, outs = outs[0], outs[1:]
    return other, outs[0], outs[1], outs[2:]


def merge_kernel(masks, bit, routes, own, *rest):
    slots = len(masks)
    back = rest[:slots]
    sent, kept, total = rest[slots:]
    group = lax.axis_index("blk")
    mine = (lax.axis_index("ulysses") // bit) % 2
    per_block = back[0].shape[2]
    total[...] = own[...].astype(jnp.float32)
    for mask, part in zip(masks, back):
        first = routes[group ^ mask, group] * per_block
        spot = pl.ds(first, per_block)
        total[:, :, spot] = total[:, :, spot] + part[...].astype(jnp.float32)
    for index in range(sent.shape[2]):
        base = index // bit * 2 * bit + index % bit
        for out, side in ((sent, 1 - mine), (kept, mine)):
            out[:, :, index] = total[:, :, base + side * bit].astype(jnp.bfloat16)


def merge(routes, own, back, groups, ranks, bit):
    _, chunk_heads, group_keys, head_dim = own.shape
    rank_keys = group_keys // ranks
    step_heads = step_of(chunk_heads)
    masks = far_masks(groups)
    rows = (KB // rank_keys, rank_keys)

    def blocks(count):
        return pl.BlockSpec(
            (2, step_heads, count, rank_keys, head_dim), lambda i: (0, i, 0, 0, 0)
        )

    half = jax.ShapeDtypeStruct((2, chunk_heads, ranks // 2, rank_keys, head_dim), jnp.bfloat16)
    return pl.pallas_call(
        functools.partial(merge_kernel, masks, bit),
        out_shape=[half, half],
        grid=(chunk_heads // step_heads,),
        in_specs=[pl.BlockSpec(memory_space=pltpu.SMEM), blocks(ranks)]
        + slot_specs(groups, step_heads, rows, head_dim),
        out_specs=[blocks(ranks // 2)] * 2,
        scratch_shapes=[
            pltpu.VMEM((2, step_heads, ranks, rank_keys, head_dim), jnp.float32)
        ],
        compiler_params=pltpu.CompilerParams(vmem_limit_bytes=VMEM_ATTEND),
        name="merge",
    )(
        routes,
        own.reshape(2, chunk_heads, ranks, rank_keys, head_dim),
        *(part.reshape(part.shape[:-2] + rows + (head_dim,)) for part in back),
    )


def body(query_rows, out_grad, key_rows, value_rows, routes):
    head_count, _, head_dim = query_rows.shape
    query_rows, out_grad, key_rows, value_rows, routes = (
        pltpu.with_memory_space_constraint(rows, pltpu.HBM)
        for rows in (query_rows, out_grad, key_rows, value_rows, routes)
    )
    group_keys = key_rows.shape[1]
    groups = lax.axis_size("blk")
    ranks = lax.axis_size("ulysses")
    my_rank = lax.axis_index("ulysses")
    rank_keys = group_keys // ranks
    half = my_rank % 2
    bits = [1 << b for b in range(ranks.bit_length() - 1)]
    whole = sum(parts for _, parts, _, _ in PLAN)
    cuts = [
        (head_count * first // whole, head_count * parts // whole, paired, order)
        for first, parts, paired, order in PLAN
    ]

    def exchange(near, pairs, forward):
        def hop(rows, mask, both=False):
            links = [
                (g, g ^ mask) for g in range(groups) if both or ((g ^ mask) > g) == forward
            ]
            return lax.ppermute(rows, "blk", links)

        crossed = [hop(pair, 2 * i) for i, pair in enumerate(pairs, 1)]
        slots = [hop(near, 1, both=True)]
        for pair in crossed:
            slots += [pair, hop(pair[1], 1, both=True)]
        return slots

    def scatter(sent, kept, order):
        left = list(reversed(bits))
        for step, bit in enumerate(order):
            left.remove(bit)
            if step:
                axis = 2 + sum(b > bit for b in left)
                mine = (my_rank // bit) % 2
                sent = lax.dynamic_index_in_dim(total, 1 - mine, axis, keepdims=False)
                kept = lax.dynamic_index_in_dim(total, mine, axis, keepdims=False)
            came = lax.ppermute(sent, "ulysses", [(r, r ^ bit) for r in range(ranks)])
            total = kept.astype(jnp.float32) + came.astype(jnp.float32)
            total = total.reshape(kept.shape[:2] + (2,) * len(left) + (rank_keys, head_dim))
            if step + 1 < len(order):
                total = total.astype(jnp.bfloat16)
        return total

    def trade(rows):
        return lax.ppermute(rows, "ulysses", [(r, r ^ 1) for r in range(ranks)])

    def join(total):
        mine = lax.dynamic_index_in_dim(total, half, 2, keepdims=False)
        away = lax.dynamic_index_in_dim(total, 1 - half, 2, keepdims=False)
        came = trade(away.astype(jnp.bfloat16)).astype(jnp.float32)
        low = jnp.where(half == 0, mine, came)
        high = jnp.where(half == 0, came, mine)
        return jnp.concatenate([low, high], axis=1)

    half_operand = half.astype(jnp.int32).reshape(1)
    picked = pick(routes, query_rows, out_grad, key_rows, value_rows, groups, cuts)
    query_out = None
    results = []
    others = []
    fetched = []
    for swapped, parts in picked:
        if swapped is not None:
            swapped = trade(swapped)
        fetched.append((swapped, exchange(parts[0], parts[1:], True)))
    for number, cut in enumerate(cuts):
        swapped, far = fetched[number]
        other, query_out, own, parts = attend(
            half_operand, query_rows, out_grad, key_rows, value_rows, far, swapped,
            groups, cut, query_out,
        )
        back = exchange(parts[0], parts[1:], False)
        if other is not None:
            others.append((cut, trade(other)))
        order = [bit for bit in bits if not (cut[2] and bit == 1)]
        if cut[3]:
            order[0], order[1] = order[1], order[0]
        sent, kept = merge(routes, own, back, groups, ranks, order[0])
        total = scatter(sent, kept, order)
        results.append(join(total) if cut[2] else total)
    for cut, rows in others:
        first = cut[0] + (1 - half) * (cut[1] // 2)
        query_out = lax.dynamic_update_slice_in_dim(query_out, rows, first, 0)
    placed = [results[number] for number in sorted(range(len(cuts)), key=lambda n: cuts[n][0])]
    key_grad = jnp.concatenate([total[0] for total in placed], axis=0)
    value_grad = jnp.concatenate([total[1] for total in placed], axis=0)
    return (query_out, key_grad, value_grad)


def solution(mesh):
    return jax.shard_map(
        body,
        mesh=mesh,
        in_specs=(
            P(None, ("blk", "ulysses"), None),
            P(None, ("blk", "ulysses"), None),
            P(None, "blk", None),
            P(None, "blk", None),
            P(),
        ),
        out_specs=(
            P(None, ("blk", "ulysses"), None),
            P(None, ("blk", "ulysses"), None),
            P(None, ("blk", "ulysses"), None),
        ),
        check_vma=False,
    )
```

profile of v0, /device:TPU:0, one launch (start us, length us, event | category | flops | bytes accessed | tf_op | source)
XLA Modules:
  0.0 80.1 jit_solution(16472514848951803367)
XLA Ops:
  0.6 2.1 %pick.1 = (bf16[2,12,16,128]{3,2,1,0:T(8,128)(2,1)S(1)}, bf16[2,2,12,16,128]{4,3,2,1,0:T(8,128)(2,1)S(1)}, bf16[2,10,128,128]{3,2,1,0:T(8,128)(2,1)S(1)}, bf16[2...) custom-call(s32[4,4]{1,0:T(4,128)} %routes.5, bf16[32,128,128]{2,1,0:T(8,128)(2,1)} %query.5, ...), custom_call_target="tpu_custom_call" | custom-call | tf_op jit(solution)/shard_map/pick/pallas_call | solution.py:70
  2.7 4.9 %collective-permute-start.5 = (bf16[2,2,12,16,128]{4,3,2,1,0:T(8,128)(2,1)S(1)}, bf16[2,2,12,16,128]{4,3,2,1,0:T(8,128)(2,1)S(1)}, u32[]{:S(2)}, u32[]{:S(2)}) collective-permute-start(bf16[2,2,12,16,128]{4,3,2,1,0:T(8,128)(2,1)S(1)} %get-tuple-element.25), channel_id=1, source_target_pairs={{0,16},{8,24},{1,17},{9,25},{2,18},{10,26},{3,19},{11,27},{4,20},{... | collective-permute-start | bytes 589832 | tf_op jit(solution)/shard_map/ppermute | solution.py:316
  7.6 0.1 collective-permute-start.4
  7.7 4.1 %collective-permute-done.5.rest_1_ = bf16[2,2,12,16,128]{4,3,2,1,0:T(8,128)(2,1)S(1)} collective-permute-done((bf16[2,2,12,16,128]{4,3,2,1,0:T(8,128)(2,1)S(1)}, bf16[2,2,12,16,128]{4,3,2,1,0:T(8,128)(2,1)S(1)}, u32[]{:S(2)}, u32[]{:S(2)}) %collective-permute-start.5) | collective-permute-done | bytes 196640 | tf_op jit(solution)/shard_map/ppermute | solution.py:316
  11.8 0.0 collective-permute-start.6
  11.8 0.0 collective-permute-done.4.rest_0_
  11.8 1.3 %collective-permute-done.6.rest_2_ = bf16[2,12,16,128]{3,2,1,0:T(8,128)(2,1)S(1)} collective-permute-done((bf16[2,12,16,128]{3,2,1,0:T(8,128)(2,1)S(1)}, bf16[2,12,16,128]{3,2,1,0:T(8,128)(2,1)S(1)}, u32[]{:S(2)}, u32[]{:S(2)}) %collective-permute-start.6) | collective-permute-done | bytes 98336 | tf_op jit(solution)/shard_map/ppermute | solution.py:316
  13.1 4.4 %attend.2 = (bf16[32,128,128]{2,1,0:T(8,128)(2,1)}, bf16[2,12,128,128]{3,2,1,0:T(8,128)(2,1)S(1)}, bf16[2,12,16,128]{3,2,1,0:T(8,128)(2,1)S(1)}, bf16[2,2,12,16,128]{4,3,2,1,0:T(8,128)(2,1)S(1)}) custom-call(s32[1]{0:T(128)} %bitcast._, bf16[32,128,128]{2,1,0:T(8,128)(2,1)} %query.5, bf16[32,128,128]{2,1,0:T(8,128)(2,1)} %grad.5, ...), custom_call_target="tpu_custom_call" | custom-call | tf_op jit(solution)/shard_map/attend/pallas_call | solution.py:221
  17.4 1.3 %collective-permute-start.15 = (bf16[2,2,12,16,128]{4,3,2,1,0:T(8,128)(2,1)S(1)}, bf16[2,2,12,16,128]{4,3,2,1,0:T(8,128)(2,1)S(1)}, u32[]{:S(2)}, u32[]{:S(2)}) collective-permute-start(bf16[2,2,12,16,128]{4,3,2,1,0:T(8,128)(2,1)S(1)} %get-tuple-element.36), channel_id=1, source_target_pairs={{16,0},{24,8},{17,1},{25,9},{18,2},{26,10},{19,3},{27,11},{20,4},{... | collective-permute-start | bytes 589832 | tf_op jit(solution)/shard_map/ppermute | solution.py:316
  18.7 1.6 %collective-permute-start.3 = (bf16[2,10,128,128]{3,2,1,0:T(8,128)(2,1)S(1)}, bf16[2,10,128,128]{3,2,1,0:T(8,128)(2,1)S(1)}, u32[]{:S(2)}, u32[]{:S(2)}) collective-permute-start(bf16[2,10,128,128]{3,2,1,0:T(8,128)(2,1)S(1)} %get-tuple-element.23), channel_id=1, source_target_pairs={{0,1},{1,0},{2,3},{3,2},{4,5},{5,4},{6,7},{7,6},{8,9},{9,8},{10,11... | collective-permute-start | bytes 1966088 | tf_op jit(solution)/shard_map/ppermute | solution.py:341
  20.3 0.0 collective-permute-start
  20.3 4.6 %collective-permute-start.1 = (bf16[2,2,10,16,128]{4,3,2,1,0:T(8,128)(2,1)S(1)}, bf16[2,2,10,16,128]{4,3,2,1,0:T(8,128)(2,1)S(1)}, u32[]{:S(2)}, u32[]{:S(2)}) collective-permute-start(bf16[2,2,10,16,128]{4,3,2,1,0:T(8,128)(2,1)S(1)} %get-tuple-element.22), channel_id=1, source_target_pairs={{0,16},{8,24},{1,17},{9,25},{2,18},{10,26},{3,19},{11,27},{4,20},{... | collective-permute-start | bytes 491528 | tf_op jit(solution)/shard_map/ppermute | solution.py:316
  24.9 0.3 collective-permute-start.14
  25.2 1.3 %collective-permute-done.15 = bf16[2,2,12,16,128]{4,3,2,1,0:T(8,128)(2,1)S(1)} collective-permute-done((bf16[2,2,12,16,128]{4,3,2,1,0:T(8,128)(2,1)S(1)}, bf16[2,2,12,16,128]{4,3,2,1,0:T(8,128)(2,1)S(1)}, u32[]{:S(2)}, u32[]{:S(2)}) %collective-permute-start.15) | collective-permute-done | bytes 196640 | tf_op jit(solution)/shard_map/ppermute | solution.py:316
  26.5 0.1 collective-permute-start.16
  26.5 2.4 %collective-permute-done.1.rest_1_ = bf16[2,2,10,16,128]{4,3,2,1,0:T(8,128)(2,1)S(1)} collective-permute-done((bf16[2,2,10,16,128]{4,3,2,1,0:T(8,128)(2,1)S(1)}, bf16[2,2,10,16,128]{4,3,2,1,0:T(8,128)(2,1)S(1)}, u32[]{:S(2)}, u32[]{:S(2)}) %collective-permute-start.1) | collective-permute-done | bytes 163872 | tf_op jit(solution)/shard_map/ppermute | solution.py:316
  29.0 0.0 collective-permute-start.2
  29.0 0.0 collective-permute-done.14
  29.0 0.0 collective-permute-done.16
  29.0 1.1 %merge.3 = (bf16[2,12,4,16,128]{4,3,2,1,0:T(8,128)(2,1)S(1)}, bf16[2,12,4,16,128]{4,3,2,1,0:T(8,128)(2,1)S(1)}) custom-call(s32[4,4]{1,0:T(4,128)} %routes.5, bf16[2,12,8,16,128]{4,3,2,1,0:T(8,128)(2,1)S(1)} %bitcast.57, bf16[2,12,1,16,128]{4,3,2,1,0:T(8,128)(2,1)S(1)} %bitcast.61, bf16[2,2,12,1,16,128]{5,4,3,2,1,0:T(8,128)(2,1)S(1)} %bitcast.59, ...), custom_call_target="tpu_custom_call" | custom-call | tf_op jit(solution)/shard_map/merge/pallas_call | solution.py:273
  30.2 0.6 collective-permute-start.17
  30.7 0.0 collective-permute-done.rest_0_
  30.7 0.0 collective-permute-done.2.rest_2_
  30.7 5.6 %collective-permute-done.3.rest_3_ = bf16[2,10,128,128]{3,2,1,0:T(8,128)(2,1)S(1)} collective-permute-done((bf16[2,10,128,128]{3,2,1,0:T(8,128)(2,1)S(1)}, bf16[2,10,128,128]{3,2,1,0:T(8,128)(2,1)S(1)}, u32[]{:S(2)}, u32[]{:S(2)}) %collective-permute-start.3) | collective-permute-done | bytes 655392 | tf_op jit(solution)/shard_map/ppermute | solution.py:341
  36.4 4.0 %attend.3 = (bf16[10,128,128]{2,1,0:T(8,128)(2,1)S(1)}, bf16[32,128,128]{2,1,0:T(8,128)(2,1)}, bf16[2,10,128,128]{3,2,1,0:T(8,128)(2,1)S(1)}, bf16[2,10,16,128]{...) custom-call(s32[1]{0:T(128)} %bitcast._, bf16[32,128,128]{2,1,0:T(8,128)(2,1)} %query.5, ...), custom_call_target="tpu_custom_call", output_to_operand_aliasing={{1}: (9, {})} | custom-call | tf_op jit(solution)/shard_map/attend/pallas_call | solution.py:221
  40.4 1.3 %collective-permute-start.9 = (bf16[2,2,10,16,128]{4,3,2,1,0:T(8,128)(2,1)S(1)}, bf16[2,2,10,16,128]{4,3,2,1,0:T(8,128)(2,1)S(1)}, u32[]{:S(2)}, u32[]{:S(2)}) collective-permute-start(bf16[2,2,10,16,128]{4,3,2,1,0:T(8,128)(2,1)S(1)} %get-tuple-element.31), channel_id=1, source_target_pairs={{16,0},{24,8},{17,1},{25,9},{18,2},{26,10},{19,3},{27,11},{20,4},{... | collective-permute-start | bytes 491528 | tf_op jit(solution)/shard_map/ppermute | solution.py:316
  41.7 0.1 collective-permute-start.8
  41.8 1.6 %collective-permute-start.7 = (bf16[10,128,128]{2,1,0:T(8,128)(2,1)S(1)}, bf16[10,128,128]{2,1,0:T(8,128)(2,1)S(1)}, u32[]{:S(2)}, u32[]{:S(2)}) collective-permute-start(bf16[10,128,128]{2,1,0:T(8,128)(2,1)S(1)} %get-tuple-element.28), channel_id=1, source_target_pairs={{0,1},{1,0},{2,3},{3,2},{4,5},{5,4},{6,7},{7,6},{8,9},{9,8},{10,11... | collective-permute-start | bytes 983048 | tf_op jit(solution)/shard_map/ppermute | solution.py:341
  43.3 4.2 %collective-permute-done.9 = bf16[2,2,10,16,128]{4,3,2,1,0:T(8,128)(2,1)S(1)} collective-permute-done((bf16[2,2,10,16,128]{4,3,2,1,0:T(8,128)(2,1)S(1)}, bf16[2,2,10,16,128]{4,3,2,1,0:T(8,128)(2,1)S(1)}, u32[]{:S(2)}, u32[]{:S(2)}) %collective-permute-start.9) | collective-permute-done | bytes 163872 | tf_op jit(solution)/shard_map/ppermute | solution.py:316
  47.6 0.0 collective-permute-start.10
  47.6 0.0 collective-permute-done.17
  47.6 0.1 add_convert_fusion
  47.8 1.6 %collective-permute-start.18 = (bf16[2,12,2,16,128]{4,3,1,0,2:T(8,128)(2,1)S(1)}, bf16[2,12,2,16,128]{4,3,1,0,2:T(8,128)(2,1)S(1)}, u32[]{:S(2)}, u32[]{:S(2)}) collective-permute-start(bf16[2,12,2,16,128]{4,3,1,0,2:T(8,128)(2,1)S(1)} %bitcast.67), channel_id=1, source_target_pairs={{0,2},{1,3},{2,0},{3,1},{4,6},{5,7},{6,4},{7,5},{8,10},{9,11},{10,... | collective-permute-start | bytes 589832 | tf_op jit(solution)/shard_map/ppermute | solution.py:333
  49.4 0.0 collective-permute-done.8
  49.4 0.9 %merge.2 = (bf16[2,10,4,16,128]{4,3,2,1,0:T(8,128)(2,1)S(1)}, bf16[2,10,4,16,128]{4,3,2,1,0:T(8,128)(2,1)S(1)}) custom-call(s32[4,4]{1,0:T(4,128)} %routes.5, bf16[2,10,8,16,128]{4,3,2,1,0:T(8,128)(2,1)S(1)} %bitcast.58, bf16[2,10,1,16,128]{4,3,2,1,0:T(8,128)(2,1)S(1)} %bitcast.63, bf16[2,2,10,1,16,128]{5,4,3,2,1,0:T(8,128)(2,1)S(1)} %bitcast.60, ...), custom_call_target="tpu_custom_call" | custom-call | tf_op jit(solution)/shard_map/merge/pallas_call | solution.py:273
  50.4 1.1 %collective-permute-start.11 = (bf16[2,10,4,16,128]{4,3,2,1,0:T(8,128)(2,1)S(1)}, bf16[2,10,4,16,128]{4,3,2,1,0:T(8,128)(2,1)S(1)}, u32[]{:S(2)}, u32[]{:S(2)}) collective-permute-start(bf16[2,10,4,16,128]{4,3,2,1,0:T(8,128)(2,1)S(1)} %get-tuple-element.33), channel_id=1, source_target_pairs={{0,2},{1,3},{2,0},{3,1},{4,6},{5,7},{6,4},{7,5},{8,10},{9,11},{10,... | collective-permute-start | bytes 983048 | tf_op jit(solution)/shard_map/ppermute | solution.py:333
  51.4 0.5 collective-permute-done.7
  51.9 0.7 constant_dynamic-update-slice_fusion
  52.6 3.0 %collective-permute-done.18 = bf16[2,12,2,16,128]{4,3,1,0,2:T(8,128)(2,1)S(1)} collective-permute-done((bf16[2,12,2,16,128]{4,3,1,0,2:T(8,128)(2,1)S(1)}, bf16[2,12,2,16,128]{4,3,1,0,2:T(8,128)(2,1)S(1)}, u32[]{:S(2)}, u32[]{:S(2)}) %collective-permute-start.18) | collective-permute-done | bytes 196640 | tf_op jit(solution)/shard_map/ppermute | solution.py:333
  55.6 0.1 fusion
  55.7 2.6 %collective-permute-start.19 = (bf16[2,12,16,128]{3,2,1,0:T(8,128)(2,1)S(1)}, bf16[2,12,16,128]{3,2,1,0:T(8,128)(2,1)S(1)}, u32[]{:S(2)}, u32[]{:S(2)}) collective-permute-start(bf16[2,12,16,128]{3,2,1,0:T(8,128)(2,1)S(1)} %dynamic-slice_bitcast_fusion), channel_id=1, source_target_pairs={{0,4},{1,5},{2,6},{3,7},{4,0},{5,1},{6,2},{7,3},{8,12},{9,13},{10,... | collective-permute-start | bytes 294920 | tf_op jit(solution)/shard_map/ppermute | solution.py:333
  58.4 5.9 %collective-permute-done.11 = bf16[2,10,4,16,128]{4,3,2,1,0:T(8,128)(2,1)S(1)} collective-permute-done((bf16[2,10,4,16,128]{4,3,2,1,0:T(8,128)(2,1)S(1)}, bf16[2,10,4,16,128]{4,3,2,1,0:T(8,128)(2,1)S(1)}, u32[]{:S(2)}, u32[]{:S(2)}) %collective-permute-start.11) | collective-permute-done | bytes 327712 | tf_op jit(solution)/shard_map/ppermute | solution.py:333
  64.3 0.1 add_convert_fusion.1
  64.4 1.7 %collective-permute-start.12 = (bf16[2,10,2,16,128]{4,3,1,0,2:T(8,128)(2,1)S(1)}, bf16[2,10,2,16,128]{4,3,1,0,2:T(8,128)(2,1)S(1)}, u32[]{:S(2)}, u32[]{:S(2)}) collective-permute-start(bf16[2,10,2,16,128]{4,3,1,0,2:T(8,128)(2,1)S(1)} %bitcast.68), channel_id=1, source_target_pairs={{0,4},{1,5},{2,6},{3,7},{4,0},{5,1},{6,2},{7,3},{8,12},{9,13},{10,... | collective-permute-start | bytes 491528 | tf_op jit(solution)/shard_map/ppermute | solution.py:333
  66.2 8.4 %collective-permute-done.12 = bf16[2,10,2,16,128]{4,3,1,0,2:T(8,128)(2,1)S(1)} collective-permute-done((bf16[2,10,2,16,128]{4,3,1,0,2:T(8,128)(2,1)S(1)}, bf16[2,10,2,16,128]{4,3,1,0,2:T(8,128)(2,1)S(1)}, u32[]{:S(2)}, u32[]{:S(2)}) %collective-permute-start.12) | collective-permute-done | bytes 163872 | tf_op jit(solution)/shard_map/ppermute | solution.py:333
  74.7 1.6 %collective-permute-start.13 = (bf16[2,10,16,128]{3,2,1,0:T(8,128)(2,1)S(1)}, bf16[2,10,16,128]{3,2,1,0:T(8,128)(2,1)S(1)}, u32[]{:S(2)}, u32[]{:S(2)}) collective-permute-start(bf16[2,10,16,128]{3,2,1,0:T(8,128)(2,1)S(1)} %fusion.4), channel_id=1, source_target_pairs={{0,1},{1,0},{2,3},{3,2},{4,5},{5,4},{6,7},{7,6},{8,9},{9,8},{10,11... | collective-permute-start | bytes 245768 | tf_op jit(solution)/shard_map/ppermute | solution.py:341
  76.3 2.9 %collective-permute-done.13 = bf16[2,10,16,128]{3,2,1,0:T(8,128)(2,1)S(1)} collective-permute-done((bf16[2,10,16,128]{3,2,1,0:T(8,128)(2,1)S(1)}, bf16[2,10,16,128]{3,2,1,0:T(8,128)(2,1)S(1)}, u32[]{:S(2)}, u32[]{:S(2)}) %collective-permute-start.13) | collective-permute-done | bytes 81952 | tf_op jit(solution)/shard_map/ppermute | solution.py:341
  79.3 0.8 %pad_maximum_fusion = (f32[32,16,128]{2,1,0:T(8,128)}, f32[32,16,128]{2,1,0:T(8,128)}) fusion(f32[12,16,128]{2,1,0:T(8,128)S(1)} %get-tuple-element.48, f32[20,16,128]{2,1,0:T(8,128)S(1)} %get-tuple-element.44, f32[12,16,128]{2,1,0:T(8,128)S(1)} %get-tuple-element.47, f32[20,16,128]{2,1,0:T(8,128)S(1)} %get-tuple-element.43), kind=kLoop, calls=%fused_computation.7 | loop fusion | flops 131072 | bytes 1048576 | tf_op jit(solution)/shard_map/concatenate | solution.py:380
  (17 shorter events, 0.3 us)
Async XLA Ops:
  2.7 9.0 %collective-permute-start.5 = (bf16[2,2,12,16,128]{4,3,2,1,0:T(8,128)(2,1)S(1)}, bf16[2,2,12,16,128]{4,3,2,1,0:T(8,128)(2,1)S(1)}, u32[]{:S(2)}, u32[]{:S(2)}) collective-permute-start(bf16[2,2,12,16,128]{4,3,2,1,0:T(8,128)(2,1)S(1)} %get-tuple-element.25), channel_id=1, source_target_pairs={{0,16},{8,24},{1,17},{9,25},{2,18},{10,26},{3,19},{11,27},{4,20},{... | collective-permute-start | bytes 589832 | tf_op jit(solution)/shard_map/ppermute | solution.py:316
  7.6 4.2 %collective-permute-start.4 = (bf16[2,12,16,128]{3,2,1,0:T(8,128)(2,1)S(1)}, bf16[2,12,16,128]{3,2,1,0:T(8,128)(2,1)S(1)}, u32[]{:S(2)}, u32[]{:S(2)}) collective-permute-start(bf16[2,12,16,128]{3,2,1,0:T(8,128)(2,1)S(1)} %get-tuple-element.24), channel_id=1, source_target_pairs={{0,8},{8,0},{16,24},{24,16},{1,9},{9,1},{17,25},{25,17},{2,10},{10... | collective-permute-start | bytes 294920 | tf_op jit(solution)/shard_map/ppermute | solution.py:316
  11.8 1.3 %collective-permute-start.6 = (bf16[2,12,16,128]{3,2,1,0:T(8,128)(2,1)S(1)}, bf16[2,12,16,128]{3,2,1,0:T(8,128)(2,1)S(1)}, u32[]{:S(2)}, u32[]{:S(2)}) collective-permute-start(bf16[2,12,16,128]{3,2,1,0:T(8,128)(2,1)S(1)} %slice_bitcast_fusion.3), channel_id=1, source_target_pairs={{0,8},{8,0},{16,24},{24,16},{1,9},{9,1},{17,25},{25,17},{2,10},{10... | collective-permute-start | bytes 294920 | tf_op jit(solution)/shard_map/ppermute | solution.py:316
  17.4 9.0 %collective-permute-start.15 = (bf16[2,2,12,16,128]{4,3,2,1,0:T(8,128)(2,1)S(1)}, bf16[2,2,12,16,128]{4,3,2,1,0:T(8,128)(2,1)S(1)}, u32[]{:S(2)}, u32[]{:S(2)}) collective-permute-start(bf16[2,2,12,16,128]{4,3,2,1,0:T(8,128)(2,1)S(1)} %get-tuple-element.36), channel_id=1, source_target_pairs={{16,0},{24,8},{17,1},{25,9},{18,2},{26,10},{19,3},{27,11},{20,4},{... | collective-permute-start | bytes 589832 | tf_op jit(solution)/shard_map/ppermute | solution.py:316
  18.7 17.7 %collective-permute-start.3 = (bf16[2,10,128,128]{3,2,1,0:T(8,128)(2,1)S(1)}, bf16[2,10,128,128]{3,2,1,0:T(8,128)(2,1)S(1)}, u32[]{:S(2)}, u32[]{:S(2)}) collective-permute-start(bf16[2,10,128,128]{3,2,1,0:T(8,128)(2,1)S(1)} %get-tuple-element.23), channel_id=1, source_target_pairs={{0,1},{1,0},{2,3},{3,2},{4,5},{5,4},{6,7},{7,6},{8,9},{9,8},{10,11... | collective-permute-start | bytes 1966088 | tf_op jit(solution)/shard_map/ppermute | solution.py:341
  20.3 10.4 %collective-permute-start = (bf16[2,10,16,128]{3,2,1,0:T(8,128)(2,1)S(1)}, bf16[2,10,16,128]{3,2,1,0:T(8,128)(2,1)S(1)}, u32[]{:S(2)}, u32[]{:S(2)}) collective-permute-start(bf16[2,10,16,128]{3,2,1,0:T(8,128)(2,1)S(1)} %get-tuple-element.21), channel_id=1, source_target_pairs={{0,8},{8,0},{16,24},{24,16},{1,9},{9,1},{17,25},{25,17},{2,10},{10... | collective-permute-start | bytes 245768 | tf_op jit(solution)/shard_map/ppermute | solution.py:316
  20.3 8.7 %collective-permute-start.1 = (bf16[2,2,10,16,128]{4,3,2,1,0:T(8,128)(2,1)S(1)}, bf16[2,2,10,16,128]{4,3,2,1,0:T(8,128)(2,1)S(1)}, u32[]{:S(2)}, u32[]{:S(2)}) collective-permute-start(bf16[2,2,10,16,128]{4,3,2,1,0:T(8,128)(2,1)S(1)} %get-tuple-element.22), channel_id=1, source_target_pairs={{0,16},{8,24},{1,17},{9,25},{2,18},{10,26},{3,19},{11,27},{4,20},{... | collective-permute-start | bytes 491528 | tf_op jit(solution)/shard_map/ppermute | solution.py:316
  24.9 4.1 %collective-permute-start.14 = (bf16[2,12,16,128]{3,2,1,0:T(8,128)(2,1)S(1)}, bf16[2,12,16,128]{3,2,1,0:T(8,128)(2,1)S(1)}, u32[]{:S(2)}, u32[]{:S(2)}) collective-permute-start(bf16[2,12,16,128]{3,2,1,0:T(8,128)(2,1)S(1)} %get-tuple-element.35), channel_id=1, source_target_pairs={{0,8},{8,0},{16,24},{24,16},{1,9},{9,1},{17,25},{25,17},{2,10},{10... | collective-permute-start | bytes 294920 | tf_op jit(solution)/shard_map/ppermute | solution.py:316
  26.5 2.5 %collective-permute-start.16 = (bf16[2,12,16,128]{3,2,1,0:T(8,128)(2,1)S(1)}, bf16[2,12,16,128]{3,2,1,0:T(8,128)(2,1)S(1)}, u32[]{:S(2)}, u32[]{:S(2)}) collective-permute-start(bf16[2,12,16,128]{3,2,1,0:T(8,128)(2,1)S(1)} %slice_bitcast_fusion.2), channel_id=1, source_target_pairs={{0,8},{8,0},{16,24},{24,16},{1,9},{9,1},{17,25},{25,17},{2,10},{10... | collective-permute-start | bytes 294920 | tf_op jit(solution)/shard_map/ppermute | solution.py:316
  29.0 1.8 %collective-permute-start.2 = (bf16[2,10,16,128]{3,2,1,0:T(8,128)(2,1)S(1)}, bf16[2,10,16,128]{3,2,1,0:T(8,128)(2,1)S(1)}, u32[]{:S(2)}, u32[]{:S(2)}) collective-permute-start(bf16[2,10,16,128]{3,2,1,0:T(8,128)(2,1)S(1)} %slice_bitcast_fusion.5), channel_id=1, source_target_pairs={{0,8},{8,0},{16,24},{24,16},{1,9},{9,1},{17,25},{25,17},{2,10},{10... | collective-permute-start | bytes 245768 | tf_op jit(solution)/shard_map/ppermute | solution.py:316
  30.2 17.4 %collective-permute-start.17 = (bf16[2,12,4,16,128]{4,3,2,1,0:T(8,128)(2,1)S(1)}, bf16[2,12,4,16,128]{4,3,2,1,0:T(8,128)(2,1)S(1)}, u32[]{:S(2)}, u32[]{:S(2)}) collective-permute-start(bf16[2,12,4,16,128]{4,3,2,1,0:T(8,128)(2,1)S(1)} %get-tuple-element.38), channel_id=1, source_target_pairs={{0,1},{1,0},{2,3},{3,2},{4,5},{5,4},{6,7},{7,6},{8,9},{9,8},{10,11... | collective-permute-start | bytes 1179656 | tf_op jit(solution)/shard_map/ppermute | solution.py:333
  40.4 7.2 %collective-permute-start.9 = (bf16[2,2,10,16,128]{4,3,2,1,0:T(8,128)(2,1)S(1)}, bf16[2,2,10,16,128]{4,3,2,1,0:T(8,128)(2,1)S(1)}, u32[]{:S(2)}, u32[]{:S(2)}) collective-permute-start(bf16[2,2,10,16,128]{4,3,2,1,0:T(8,128)(2,1)S(1)} %get-tuple-element.31), channel_id=1, source_target_pairs={{16,0},{24,8},{17,1},{25,9},{18,2},{26,10},{19,3},{27,11},{20,4},{... | collective-permute-start | bytes 491528 | tf_op jit(solution)/shard_map/ppermute | solution.py:316
  41.7 7.8 %collective-permute-start.8 = (bf16[2,10,16,128]{3,2,1,0:T(8,128)(2,1)S(1)}, bf16[2,10,16,128]{3,2,1,0:T(8,128)(2,1)S(1)}, u32[]{:S(2)}, u32[]{:S(2)}) collective-permute-start(bf16[2,10,16,128]{3,2,1,0:T(8,128)(2,1)S(1)} %get-tuple-element.30), channel_id=1, source_target_pairs={{0,8},{8,0},{16,24},{24,16},{1,9},{9,1},{17,25},{25,17},{2,10},{10... | collective-permute-start | bytes 245768 | tf_op jit(solution)/shard_map/ppermute | solution.py:316
  41.8 10.1 %collective-permute-start.7 = (bf16[10,128,128]{2,1,0:T(8,128)(2,1)S(1)}, bf16[10,128,128]{2,1,0:T(8,128)(2,1)S(1)}, u32[]{:S(2)}, u32[]{:S(2)}) collective-permute-start(bf16[10,128,128]{2,1,0:T(8,128)(2,1)S(1)} %get-tuple-element.28), channel_id=1, source_target_pairs={{0,1},{1,0},{2,3},{3,2},{4,5},{5,4},{6,7},{7,6},{8,9},{9,8},{10,11... | collective-permute-start | bytes 983048 | tf_op jit(solution)/shard_map/ppermute | solution.py:341
  47.6 1.9 %collective-permute-start.10 = (bf16[2,10,16,128]{3,2,1,0:T(8,128)(2,1)S(1)}, bf16[2,10,16,128]{3,2,1,0:T(8,128)(2,1)S(1)}, u32[]{:S(2)}, u32[]{:S(2)}) collective-permute-start(bf16[2,10,16,128]{3,2,1,0:T(8,128)(2,1)S(1)} %slice_bitcast_fusion.4), channel_id=1, source_target_pairs={{0,8},{8,0},{16,24},{24,16},{1,9},{9,1},{17,25},{25,17},{2,10},{10... | collective-permute-start | bytes 245768 | tf_op jit(solution)/shard_map/ppermute | solution.py:316
  47.8 7.8 %collective-permute-start.18 = (bf16[2,12,2,16,128]{4,3,1,0,2:T(8,128)(2,1)S(1)}, bf16[2,12,2,16,128]{4,3,1,0,2:T(8,128)(2,1)S(1)}, u32[]{:S(2)}, u32[]{:S(2)}) collective-permute-start(bf16[2,12,2,16,128]{4,3,1,0,2:T(8,128)(2,1)S(1)} %bitcast.67), channel_id=1, source_target_pairs={{0,2},{1,3},{2,0},{3,1},{4,6},{5,7},{6,4},{7,5},{8,10},{9,11},{10,... | collective-permute-start | bytes 589832 | tf_op jit(solution)/shard_map/ppermute | solution.py:333
  50.4 13.9 %collective-permute-start.11 = (bf16[2,10,4,16,128]{4,3,2,1,0:T(8,128)(2,1)S(1)}, bf16[2,10,4,16,128]{4,3,2,1,0:T(8,128)(2,1)S(1)}, u32[]{:S(2)}, u32[]{:S(2)}) collective-permute-start(bf16[2,10,4,16,128]{4,3,2,1,0:T(8,128)(2,1)S(1)} %get-tuple-element.33), channel_id=1, source_target_pairs={{0,2},{1,3},{2,0},{3,1},{4,6},{5,7},{6,4},{7,5},{8,10},{9,11},{10,... | collective-permute-start | bytes 983048 | tf_op jit(solution)/shard_map/ppermute | solution.py:333
  55.7 10.5 %collective-permute-start.19 = (bf16[2,12,16,128]{3,2,1,0:T(8,128)(2,1)S(1)}, bf16[2,12,16,128]{3,2,1,0:T(8,128)(2,1)S(1)}, u32[]{:S(2)}, u32[]{:S(2)}) collective-permute-start(bf16[2,12,16,128]{3,2,1,0:T(8,128)(2,1)S(1)} %dynamic-slice_bitcast_fusion), channel_id=1, source_target_pairs={{0,4},{1,5},{2,6},{3,7},{4,0},{5,1},{6,2},{7,3},{8,12},{9,13},{10,... | collective-permute-start | bytes 294920 | tf_op jit(solution)/shard_map/ppermute | solution.py:333
  64.4 10.2 %collective-permute-start.12 = (bf16[2,10,2,16,128]{4,3,1,0,2:T(8,128)(2,1)S(1)}, bf16[2,10,2,16,128]{4,3,1,0,2:T(8,128)(2,1)S(1)}, u32[]{:S(2)}, u32[]{:S(2)}) collective-permute-start(bf16[2,10,2,16,128]{4,3,1,0,2:T(8,128)(2,1)S(1)} %bitcast.68), channel_id=1, source_target_pairs={{0,4},{1,5},{2,6},{3,7},{4,0},{5,1},{6,2},{7,3},{8,12},{9,13},{10,... | collective-permute-start | bytes 491528 | tf_op jit(solution)/shard_map/ppermute | solution.py:333
  74.7 4.5 %collective-permute-start.13 = (bf16[2,10,16,128]{3,2,1,0:T(8,128)(2,1)S(1)}, bf16[2,10,16,128]{3,2,1,0:T(8,128)(2,1)S(1)}, u32[]{:S(2)}, u32[]{:S(2)}) collective-permute-start(bf16[2,10,16,128]{3,2,1,0:T(8,128)(2,1)S(1)} %fusion.4), channel_id=1, source_target_pairs={{0,1},{1,0},{2,3},{3,2},{4,5},{5,4},{6,7},{7,6},{8,9},{9,8},{10,11... | collective-permute-start | bytes 245768 | tf_op jit(solution)/shard_map/ppermute | solution.py:341
where the time goes:
time: 80.5 us; the launch traced here: 80.1 us
  waiting for transfers between devices  39.7 us (49%)
  starting transfers between devices  24.9 us (31%)
  Pallas kernels  12.5 us (16%)
  other arithmetic  1.2 us (1%)
  local copies, waits for them, and re-layouts  0.92 us (1%)
  between operations  0.92 us (1%)
    ppermute x5, waiting for transfers between devices, scatter(): came = lax.ppermute(sent, 'ulysses', [(r, r ^ bit) for r in range(ranks)])  17.4 us
    ppermute x12, waiting for transfers between devices, hop(): return lax.ppermute(rows, 'blk', links)  13.3 us
    ppermute x12, starting transfers between devices, hop(): return lax.ppermute(rows, 'blk', links)  12.5 us
    ppermute x3, waiting for transfers between devices, trade(): return lax.ppermute(rows, 'ulysses', [(r, r ^ 1) for r in range(ranks)])  9 us
    pallas_call x2, Pallas kernels, attend(): pl.pallas_call(functools.partial(attend_kernel, masks, query_out is not N...  8.32 us
    ppermute x5, starting transfers between devices, scatter(): came = lax.ppermute(sent, 'ulysses', [(r, r ^ bit) for r in range(ranks)])  7.67 us
    ppermute x3, starting transfers between devices, trade(): return lax.ppermute(rows, 'ulysses', [(r, r ^ 1) for r in range(ranks)])  4.76 us
    pallas_call x1, Pallas kernels, pick(): pl.pallas_call(functools.partial(pick_kernel, cuts, groups), out_shape=[j...  2.11 us
  transfers between devices with their start and end apart: 20, of which 11 were waited for; matrix products, arithmetic and copies ran while one was open for 1% of the time, Pallas kernels for 8%

commit v1 on v0

--- a/solution.py
+++ b/solution.py
@@ -10,8 +10,8 @@
 
 
 KB = 16
-PLAN = ((20, 12, False, 0), (0, 20, True, 0))
-STEP_HEADS = 10
+PLAN = ((16, 16, False, (1, 2)), (0, 16, True, (2,)))
+STEP_HEADS = 8
 VMEM_SMALL = 8 << 20
 VMEM_ATTEND = 24 << 20
 
@@ -239,25 +239,33 @@
     return other, outs[0], outs[1], outs[2:]
 
 
-def merge_kernel(masks, bit, routes, own, *rest):
+def mixes(bits):
+    found = [0]
+    for bit in bits:
+        found += [mask | bit for mask in found]
+    return found
+
+
+def merge_kernel(masks, bits, routes, own, *rest):
     slots = len(masks)
     back = rest[:slots]
-    sent, kept, total = rest[slots:]
+    outs, total = rest[slots:-1], rest[-1]
     group = lax.axis_index("blk")
-    mine = (lax.axis_index("ulysses") // bit) % 2
+    rank = lax.axis_index("ulysses")
     per_block = back[0].shape[2]
     total[...] = own[...].astype(jnp.float32)
     for mask, part in zip(masks, back):
         first = routes[group ^ mask, group] * per_block
         spot = pl.ds(first, per_block)
         total[:, :, spot] = total[:, :, spot] + part[...].astype(jnp.float32)
-    for index in range(sent.shape[2]):
-        base = index // bit * 2 * bit + index % bit
-        for out, side in ((sent, 1 - mine), (kept, mine)):
-            out[:, :, index] = total[:, :, base + side * bit].astype(jnp.bfloat16)
-
-
-def merge(routes, own, back, groups, ranks, bit):
+    chosen = sum(bits)
+    bases = [index for index in range(own.shape[2]) if index & chosen == 0]
+    for mix, out in zip(mixes(bits), outs):
+        for index, base in enumerate(bases):
+            out[:, :, index] = total[:, :, base + ((rank ^ mix) & chosen)].astype(jnp.bfloat16)
+
+
+def merge(routes, own, back, groups, ranks, bits):
     _, chunk_heads, group_keys, head_dim = own.shape
     rank_keys = group_keys // ranks
     step_heads = step_of(chunk_heads)
@@ -269,14 +277,15 @@
             (2, step_heads, count, rank_keys, head_dim), lambda i: (0, i, 0, 0, 0)
         )
 
-    half = jax.ShapeDtypeStruct((2, chunk_heads, ranks // 2, rank_keys, head_dim), jnp.bfloat16)
+    pieces = 1 << len(bits)
+    piece = (2, chunk_heads, ranks // pieces, rank_keys, head_dim)
     return pl.pallas_call(
-        functools.partial(merge_kernel, masks, bit),
-        out_shape=[half, half],
+        functools.partial(merge_kernel, masks, bits),
+        out_shape=[jax.ShapeDtypeStruct(piece, jnp.bfloat16)] * pieces,
         grid=(chunk_heads // step_heads,),
         in_specs=[pl.BlockSpec(memory_space=pltpu.SMEM), blocks(ranks)]
         + slot_specs(groups, step_heads, rows, head_dim),
-        out_specs=[blocks(ranks // 2)] * 2,
+        out_specs=[blocks(ranks // pieces)] * pieces,
         scratch_shapes=[
             pltpu.VMEM((2, step_heads, ranks, rank_keys, head_dim), jnp.float32)
         ],
@@ -321,21 +330,32 @@
             slots += [pair, hop(pair[1], 1, both=True)]
         return slots
 
-    def scatter(sent, kept, order):
-        left = list(reversed(bits))
-        for step, bit in enumerate(order):
-            left.remove(bit)
-            if step:
-                axis = 2 + sum(b > bit for b in left)
-                mine = (my_rank // bit) % 2
-                sent = lax.dynamic_index_in_dim(total, 1 - mine, axis, keepdims=False)
-                kept = lax.dynamic_index_in_dim(total, mine, axis, keepdims=False)
-            came = lax.ppermute(sent, "ulysses", [(r, r ^ bit) for r in range(ranks)])
-            total = kept.astype(jnp.float32) + came.astype(jnp.float32)
-            total = total.reshape(kept.shape[:2] + (2,) * len(left) + (rank_keys, head_dim))
-            if step + 1 < len(order):
-                total = total.astype(jnp.bfloat16)
-        return total
+    def scatter(pieces, stages):
+        left = [bit for bit in bits]
+        for step, stage in enumerate(stages):
+            left = [bit for bit in left if bit not in stage]
+            shape = (2, pieces[0].shape[1]) + (2,) * len(left) + (rank_keys, head_dim)
+            came = [
+                lax.ppermute(piece.reshape(shape), "ulysses", [(r, r ^ mix) for r in range(ranks)])
+                for mix, piece in zip(mixes(stage)[1:], pieces[1:])
+            ]
+            total = pieces[0].reshape(shape).astype(jnp.float32)
+            for part in came:
+                total = total + part.astype(jnp.float32)
+            if step + 1 == len(stages):
+                return total
+            total = total.astype(jnp.bfloat16)
+            after = stages[step + 1]
+            rest = [bit for bit in left if bit not in after]
+            axes = [2 + sum(b > bit for b in rest + list(after)) for bit in after]
+            pieces = []
+            for mix in mixes(after):
+                starts = [0] * total.ndim
+                sizes = list(total.shape)
+                for bit, axis in zip(after, axes):
+                    starts[axis] = ((my_rank ^ mix) // bit) % 2
+                    sizes[axis] = 1
+                pieces.append(lax.dynamic_slice(total, starts, sizes))
 
     def trade(rows):
         return lax.ppermute(rows, "ulysses", [(r, r ^ 1) for r in range(ranks)])
@@ -367,11 +387,14 @@
         back = exchange(parts[0], parts[1:], False)
         if other is not None:
             others.append((cut, trade(other)))
-        order = [bit for bit in bits if not (cut[2] and bit == 1)]
-        if cut[3]:
-            order[0], order[1] = order[1], order[0]
-        sent, kept = merge(routes, own, back, groups, ranks, order[0])
-        total = scatter(sent, kept, order)
+        wanted = [bit for bit in bits if not (cut[2] and bit == 1)]
+        stages = []
+        for size in cut[3] + (1,) * len(bits):
+            if wanted:
+                stages.append(tuple(wanted[:size]))
+                wanted = wanted[size:]
+        pieces = merge(routes, own, back, groups, ranks, stages[0])
+        total = scatter(pieces, stages)
         results.append(join(total) if cut[2] else total)
     for cut, rows in others:
         first = cut[0] + (1 - half) * (cut[1] // 2)

time: 80.5 us -> 70.7 us (0.88)
  waiting for transfers between devices: 39.7 us -> 27.8 us
  starting transfers between devices: 24.9 us -> 27.9 us
    ppermute x3, waiting for transfers between devices: 9 us -> 0.01 us  [trade(): return lax.ppermute(rows, 'ulysses', [(r, r ^ 1) for r in range(ranks)])]
    ppermute x12, waiting for transfers between devices: 13.3 us -> 9.09 us  [hop(): return lax.ppermute(rows, 'blk', links)]
    ppermute x5 -> x7, starting transfers between devices: 7.67 us -> 10.9 us  [scatter(): lax.ppermute(piece.reshape(shape), 'ulysses', [(r, r ^ mix) for r in rang...]
    ppermute x5 -> x7, waiting for transfers between devices: 17.4 us -> 18.7 us  [scatter(): lax.ppermute(piece.reshape(shape), 'ulysses', [(r, r ^ mix) for r in rang...]
    ppermute x3, starting transfers between devices: 4.76 us -> 3.69 us  [trade(): return lax.ppermute(rows, 'ulysses', [(r, r ^ 1) for r in range(ranks)])]
  transfers between devices with their start and end apart: 20 -> 22, of which waited for: 11 -> 8; matrix products, arithmetic and copies ran while one was open for 1% -> 2% of each run, Pallas kernels for 8% -> 14%
where the time goes in v1:
time: 70.7 us; the launch traced here: 70.3 us
  starting transfers between devices  27.9 us (39%)
  waiting for transfers between devices  27.8 us (39%)
  Pallas kernels  11.8 us (17%)
  other arithmetic  1.14 us (2%)
  local copies, waits for them, and re-layouts  0.87 us (1%)
  between operations  0.83 us (1%)
    ppermute x7, waiting for transfers between devices, scatter(): lax.ppermute(piece.reshape(shape), 'ulysses', [(r, r ^ mix) for r in rang...  18.7 us
    ppermute x12, starting transfers between devices, hop(): return lax.ppermute(rows, 'blk', links)  13.3 us
    ppermute x7, starting transfers between devices, scatter(): lax.ppermute(piece.reshape(shape), 'ulysses', [(r, r ^ mix) for r in rang...  10.9 us
    ppermute x12, waiting for transfers between devices, hop(): return lax.ppermute(rows, 'blk', links)  9.09 us
    pallas_call x2, Pallas kernels, attend(): pl.pallas_call(functools.partial(attend_kernel, masks, query_out is not N...  7.54 us
    ppermute x3, starting transfers between devices, trade(): return lax.ppermute(rows, 'ulysses', [(r, r ^ 1) for r in range(ranks)])  3.69 us
    pallas_call x2, Pallas kernels, merge(): pl.pallas_call(functools.partial(merge_kernel, masks, bits), out_shape=[j...  2.13 us
    pallas_call x1, Pallas kernels, pick(): pl.pallas_call(functools.partial(pick_kernel, cuts, groups), out_shape=[j...  2.11 us
  transfers between devices with their start and end apart: 22, of which 8 were waited for; matrix products, arithmetic and copies ran while one was open for 2% of the time, Pallas kernels for 14%

profile of v1, /device:TPU:0, one launch (start us, length us, event | category | flops | bytes accessed | tf_op | source)
XLA Modules:
  0.0 70.3 jit_solution(12084076391787885938)
XLA Ops:
  0.6 2.1 %pick.1 = (bf16[2,16,16,128]{3,2,1,0:T(8,128)(2,1)S(1)}, bf16[2,2,16,16,128]{4,3,2,1,0:T(8,128)(2,1)S(1)}, bf16[2,8,128,128]{3,2,1,0:T(8,128)(2,1)S(1)}, bf16[2,...) custom-call(s32[4,4]{1,0:T(4,128)} %routes.5, bf16[32,128,128]{2,1,0:T(8,128)(2,1)} %query.5, ...), custom_call_target="tpu_custom_call" | custom-call | tf_op jit(solution)/shard_map/pick/pallas_call | solution.py:70
  2.7 4.9 %collective-permute-start.5 = (bf16[2,2,16,16,128]{4,3,2,1,0:T(8,128)(2,1)S(1)}, bf16[2,2,16,16,128]{4,3,2,1,0:T(8,128)(2,1)S(1)}, u32[]{:S(2)}, u32[]{:S(2)}) collective-permute-start(bf16[2,2,16,16,128]{4,3,2,1,0:T(8,128)(2,1)S(1)} %get-tuple-element.27), channel_id=1, source_target_pairs={{0,16},{8,24},{1,17},{9,25},{2,18},{10,26},{3,19},{11,27},{4,20},{... | collective-permute-start | bytes 786440 | tf_op jit(solution)/shard_map/ppermute | solution.py:325
  7.6 0.1 collective-permute-start.4
  7.7 1.6 %collective-permute-start.3 = (bf16[2,8,128,128]{3,2,1,0:T(8,128)(2,1)S(1)}, bf16[2,8,128,128]{3,2,1,0:T(8,128)(2,1)S(1)}, u32[]{:S(2)}, u32[]{:S(2)}) collective-permute-start(bf16[2,8,128,128]{3,2,1,0:T(8,128)(2,1)S(1)} %get-tuple-element.25), channel_id=1, source_target_pairs={{0,1},{1,0},{2,3},{3,2},{4,5},{5,4},{6,7},{7,6},{8,9},{9,8},{10,11... | collective-permute-start | bytes 1572872 | tf_op jit(solution)/shard_map/ppermute | solution.py:361
  9.3 3.9 %collective-permute-done.5.rest_1_ = bf16[2,2,16,16,128]{4,3,2,1,0:T(8,128)(2,1)S(1)} collective-permute-done((bf16[2,2,16,16,128]{4,3,2,1,0:T(8,128)(2,1)S(1)}, bf16[2,2,16,16,128]{4,3,2,1,0:T(8,128)(2,1)S(1)}, u32[]{:S(2)}, u32[]{:S(2)}) %collective-permute-start.5) | collective-permute-done | bytes 262176 | tf_op jit(solution)/shard_map/ppermute | solution.py:325
  13.2 0.1 collective-permute-start.6
  13.3 4.4 %collective-permute-start.1 = (bf16[2,2,8,16,128]{4,3,2,1,0:T(8,128)(2,1)S(1)}, bf16[2,2,8,16,128]{4,3,2,1,0:T(8,128)(2,1)S(1)}, u32[]{:S(2)}, u32[]{:S(2)}) collective-permute-start(bf16[2,2,8,16,128]{4,3,2,1,0:T(8,128)(2,1)S(1)} %get-tuple-element.24), channel_id=1, source_target_pairs={{0,16},{8,24},{1,17},{9,25},{2,18},{10,26},{3,19},{11,27},{4,20},{... | collective-permute-start | bytes 393224 | tf_op jit(solution)/shard_map/ppermute | solution.py:325
  17.7 0.3 collective-permute-start
  17.9 0.0 collective-permute-done.4.rest_0_
  17.9 4.2 %attend.2 = (bf16[32,128,128]{2,1,0:T(8,128)(2,1)}, bf16[2,16,128,128]{3,2,1,0:T(8,128)(2,1)S(1)}, bf16[2,16,16,128]{3,2,1,0:T(8,128)(2,1)S(1)}, bf16[2,2,16,16,128]{4,3,2,1,0:T(8,128)(2,1)S(1)}) custom-call(s32[1]{0:T(128)} %bitcast._, bf16[32,128,128]{2,1,0:T(8,128)(2,1)} %query.5, bf16[32,128,128]{2,1,0:T(8,128)(2,1)} %grad.5, ...), custom_call_target="tpu_custom_call" | custom-call | tf_op jit(solution)/shard_map/attend/pallas_call | solution.py:221
  22.1 1.3 %collective-permute-start.16 = (bf16[2,2,16,16,128]{4,3,2,1,0:T(8,128)(2,1)S(1)}, bf16[2,2,16,16,128]{4,3,2,1,0:T(8,128)(2,1)S(1)}, u32[]{:S(2)}, u32[]{:S(2)}) collective-permute-start(bf16[2,2,16,16,128]{4,3,2,1,0:T(8,128)(2,1)S(1)} %get-tuple-element.40), channel_id=1, source_target_pairs={{16,0},{24,8},{17,1},{25,9},{18,2},{26,10},{19,3},{27,11},{20,4},{... | collective-permute-start | bytes 786440 | tf_op jit(solution)/shard_map/ppermute | solution.py:325
  23.4 0.0 collective-permute-done.1.rest_1_
  23.4 0.4 collective-permute-start.2
  23.8 0.2 collective-permute-start.15
  24.0 0.7 %collective-permute-done.2.rest_2_ = bf16[2,8,16,128]{3,2,1,0:T(8,128)(2,1)S(1)} collective-permute-done((bf16[2,8,16,128]{3,2,1,0:T(8,128)(2,1)S(1)}, bf16[2,8,16,128]{3,2,1,0:T(8,128)(2,1)S(1)}, u32[]{:S(2)}, u32[]{:S(2)}) %collective-permute-start.2) | collective-permute-done | bytes 65568 | tf_op jit(solution)/shard_map/ppermute | solution.py:325
  24.7 0.0 collective-permute-done.3.rest_3_
  24.7 3.4 %attend.3 = (bf16[8,128,128]{2,1,0:T(8,128)(2,1)S(1)}, bf16[32,128,128]{2,1,0:T(8,128)(2,1)}, bf16[2,8,128,128]{3,2,1,0:T(8,128)(2,1)S(1)}, bf16[2,8,16,128]{3,2...) custom-call(s32[1]{0:T(128)} %bitcast._, bf16[32,128,128]{2,1,0:T(8,128)(2,1)} %query.5, ...), custom_call_target="tpu_custom_call", output_to_operand_aliasing={{1}: (9, {})} | custom-call | tf_op jit(solution)/shard_map/attend/pallas_call | solution.py:221
  28.1 1.3 %collective-permute-start.9 = (bf16[2,2,8,16,128]{4,3,2,1,0:T(8,128)(2,1)S(1)}, bf16[2,2,8,16,128]{4,3,2,1,0:T(8,128)(2,1)S(1)}, u32[]{:S(2)}, u32[]{:S(2)}) collective-permute-start(bf16[2,2,8,16,128]{4,3,2,1,0:T(8,128)(2,1)S(1)} %get-tuple-element.33), channel_id=1, source_target_pairs={{16,0},{24,8},{17,1},{25,9},{18,2},{26,10},{19,3},{27,11},{20,4},{... | collective-permute-start | bytes 393224 | tf_op jit(solution)/shard_map/ppermute | solution.py:325
  29.4 0.4 collective-permute-start.8
  29.8 1.5 %collective-permute-start.7 = (bf16[8,128,128]{2,1,0:T(8,128)(2,1)S(1)}, bf16[8,128,128]{2,1,0:T(8,128)(2,1)S(1)}, u32[]{:S(2)}, u32[]{:S(2)}) collective-permute-start(bf16[8,128,128]{2,1,0:T(8,128)(2,1)S(1)} %get-tuple-element.30), channel_id=1, source_target_pairs={{0,1},{1,0},{2,3},{3,2},{4,5},{5,4},{6,7},{7,6},{8,9},{9,8},{10,11... | collective-permute-start | bytes 786440 | tf_op jit(solution)/shard_map/ppermute | solution.py:361
  31.3 1.2 %collective-permute-done.16 = bf16[2,2,16,16,128]{4,3,2,1,0:T(8,128)(2,1)S(1)} collective-permute-done((bf16[2,2,16,16,128]{4,3,2,1,0:T(8,128)(2,1)S(1)}, bf16[2,2,16,16,128]{4,3,2,1,0:T(8,128)(2,1)S(1)}, u32[]{:S(2)}, u32[]{:S(2)}) %collective-permute-start.16) | collective-permute-done | bytes 262176 | tf_op jit(solution)/shard_map/ppermute | solution.py:325
  32.5 0.1 collective-permute-start.17
  32.6 3.3 %collective-permute-done.9 = bf16[2,2,8,16,128]{4,3,2,1,0:T(8,128)(2,1)S(1)} collective-permute-done((bf16[2,2,8,16,128]{4,3,2,1,0:T(8,128)(2,1)S(1)}, bf16[2,2,8,16,128]{4,3,2,1,0:T(8,128)(2,1)S(1)}, u32[]{:S(2)}, u32[]{:S(2)}) %collective-permute-start.9) | collective-permute-done | bytes 131104 | tf_op jit(solution)/shard_map/ppermute | solution.py:325
  35.9 0.0 collective-permute-start.10
  35.9 0.0 collective-permute-done.15
  35.9 0.0 collective-permute-done.17
  35.9 1.3 %merge.3 = (bf16[2,16,4,16,128]{4,3,2,1,0:T(8,128)(2,1)S(1)}, bf16[2,16,4,16,128]{4,3,2,1,0:T(8,128)(2,1)S(1)}) custom-call(s32[4,4]{1,0:T(4,128)} %routes.5, bf16[2,16,8,16,128]{4,3,2,1,0:T(8,128)(2,1)S(1)} %bitcast.46, bf16[2,16,1,16,128]{4,3,2,1,0:T(8,128)(2,1)S(1)} %bitcast.52, bf16[2,2,16,1,16,128]{5,4,3,2,1,0:T(8,128)(2,1)S(1)} %bitcast.47, ...), custom_call_target="tpu_custom_call" | custom-call | tf_op jit(solution)/shard_map/merge/pallas_call | solution.py:282
  37.2 1.6 %collective-permute-start.18 = (bf16[2,16,2,2,16,128]{5,4,1,0,3,2:T(8,128)(2,1)S(1)}, bf16[2,16,2,2,16,128]{5,4,1,0,3,2:T(8,128)(2,1)S(1)}, u32[]{:S(2)}, u32[]{:S(2)}) collective-permute-start(bf16[2,16,2,2,16,128]{5,4,1,0,3,2:T(8,128)(2,1)S(1)} %copy.11), channel_id=1, source_target_pairs={{0,1},{1,0},{2,3},{3,2},{4,5},{5,4},{6,7},{7,6},{8,9},{9,8},{10,11... | collective-permute-start | bytes 1572872 | tf_op jit(solution)/shard_map/ppermute | solution.py:339
  38.8 0.9 %merge.2 = (bf16[2,8,2,16,128]{4,3,2,1,0:T(8,128)(2,1)S(1)}, bf16[2,8,2,16,128]{4,3,2,1,0:T(8,128)(2,1)S(1)}, bf16[2,8,2,16,128]{4,3,2,1,0:T(8,128)(2,1)S(1)}, bf16[2,8,2,16,128]{4,3,2,1,0:T(8,128)(2,1)S(1)}) custom-call(s32[4,4]{1,0:T(4,128)} %routes.5, bf16[2,8,8,16,128]{4,3,2,1,0:T(8,128)(2,1)S(1)} %bitcast.49, bf16[2,8,1,16,128]{4,3,2,1,0:T(8,128)(2,1)S(1)} %bitcast.54, ...), custom_call_target="tpu_custom_call" | custom-call | tf_op jit(solution)/shard_map/merge/pallas_call | solution.py:282
  39.7 1.6 %collective-permute-start.11 = (bf16[2,8,2,16,128]{4,3,2,1,0:T(8,128)(2,1)S(1)}, bf16[2,8,2,16,128]{4,3,2,1,0:T(8,128)(2,1)S(1)}, u32[]{:S(2)}, u32[]{:S(2)}) collective-permute-start(bf16[2,8,2,16,128]{4,3,2,1,0:T(8,128)(2,1)S(1)} %get-tuple-element.35), channel_id=1, source_target_pairs={{0,2},{1,3},{2,0},{3,1},{4,6},{5,7},{6,4},{7,5},{8,10},{9,11},{10,... | collective-permute-start | bytes 393224 | tf_op jit(solution)/shard_map/ppermute | solution.py:339
  41.3 2.6 %collective-permute-start.12 = (bf16[2,8,2,16,128]{4,3,2,1,0:T(8,128)(2,1)S(1)}, bf16[2,8,2,16,128]{4,3,2,1,0:T(8,128)(2,1)S(1)}, u32[]{:S(2)}, u32[]{:S(2)}) collective-permute-start(bf16[2,8,2,16,128]{4,3,2,1,0:T(8,128)(2,1)S(1)} %get-tuple-element.36), channel_id=1, source_target_pairs={{0,4},{1,5},{2,6},{3,7},{4,0},{5,1},{6,2},{7,3},{8,12},{9,13},{10,... | collective-permute-start | bytes 393224 | tf_op jit(solution)/shard_map/ppermute | solution.py:339
  43.9 0.2 collective-permute-start.13
  44.1 0.7 %constant_dynamic-update-slice_fusion = bf16[32,128,128]{2,1,0:T(8,128)(2,1)} fusion(bf16[32,128,128]{2,1,0:T(8,128)(2,1)} %get-tuple-element.29, bf16[8,128,128]{2,1,0:T(8,128)(2,1)S(1)} %collective-permute-done.7, s32[]{:T(128)S(6)} %select_n.111), kind=kLoop, calls=%fused_computation.27 | loop fusion | bytes 524292 | tf_op jit(solution)/shard_map/dynamic_update_slice | solution.py:401
  44.8 2.5 %collective-permute-done.11 = bf16[2,8,2,16,128]{4,3,2,1,0:T(8,128)(2,1)S(1)} collective-permute-done((bf16[2,8,2,16,128]{4,3,2,1,0:T(8,128)(2,1)S(1)}, bf16[2,8,2,16,128]{4,3,2,1,0:T(8,128)(2,1)S(1)}, u32[]{:S(2)}, u32[]{:S(2)}) %collective-permute-start.11) | collective-permute-done | bytes 131104 | tf_op jit(solution)/shard_map/ppermute | solution.py:339
  47.3 6.9 %collective-permute-done.12 = bf16[2,8,2,16,128]{4,3,2,1,0:T(8,128)(2,1)S(1)} collective-permute-done((bf16[2,8,2,16,128]{4,3,2,1,0:T(8,128)(2,1)S(1)}, bf16[2,8,2,16,128]{4,3,2,1,0:T(8,128)(2,1)S(1)}, u32[]{:S(2)}, u32[]{:S(2)}) %collective-permute-start.12) | collective-permute-done | bytes 131104 | tf_op jit(solution)/shard_map/ppermute | solution.py:339
  54.2 0.0 collective-permute-done.13
  54.2 0.1 convert_add_fusion.1
  54.3 0.6 collective-permute-start.14
  54.9 0.1 fusion
  55.1 2.4 %collective-permute-start.19 = (bf16[2,16,16,128]{3,2,1,0:T(8,128)(2,1)S(1)}, bf16[2,16,16,128]{3,2,1,0:T(8,128)(2,1)S(1)}, u32[]{:S(2)}, u32[]{:S(2)}) collective-permute-start(bf16[2,16,16,128]{3,2,1,0:T(8,128)(2,1)S(1)} %get-tuple-element.43), channel_id=1, source_target_pairs={{0,2},{1,3},{2,0},{3,1},{4,6},{5,7},{6,4},{7,5},{8,10},{9,11},{10,... | collective-permute-start | bytes 393224 | tf_op jit(solution)/shard_map/ppermute | solution.py:339
  57.5 1.1 %collective-permute-start.20 = (bf16[2,16,16,128]{3,2,1,0:T(8,128)(2,1)S(1)}, bf16[2,16,16,128]{3,2,1,0:T(8,128)(2,1)S(1)}, u32[]{:S(2)}, u32[]{:S(2)}) collective-permute-start(bf16[2,16,16,128]{3,2,1,0:T(8,128)(2,1)S(1)} %get-tuple-element.45), channel_id=1, source_target_pairs={{0,4},{1,5},{2,6},{3,7},{4,0},{5,1},{6,2},{7,3},{8,12},{9,13},{10,... | collective-permute-start | bytes 393224 | tf_op jit(solution)/shard_map/ppermute | solution.py:339
  58.6 1.4 %collective-permute-start.21 = (bf16[2,16,16,128]{3,2,1,0:T(8,128)(2,1)S(1)}, bf16[2,16,16,128]{3,2,1,0:T(8,128)(2,1)S(1)}, u32[]{:S(2)}, u32[]{:S(2)}) collective-permute-start(bf16[2,16,16,128]{3,2,1,0:T(8,128)(2,1)S(1)} %get-tuple-element.44), channel_id=1, source_target_pairs={{0,6},{1,7},{2,4},{3,5},{4,2},{5,3},{6,0},{7,1},{8,14},{9,15},{10,... | collective-permute-start | bytes 393224 | tf_op jit(solution)/shard_map/ppermute | solution.py:339
  60.0 0.0 collective-permute-done.14
  60.0 1.8 %collective-permute-done.19 = bf16[2,16,16,128]{3,2,1,0:T(8,128)(2,1)S(1)} collective-permute-done((bf16[2,16,16,128]{3,2,1,0:T(8,128)(2,1)S(1)}, bf16[2,16,16,128]{3,2,1,0:T(8,128)(2,1)S(1)}, u32[]{:S(2)}, u32[]{:S(2)}) %collective-permute-start.19) | collective-permute-done | bytes 131104 | tf_op jit(solution)/shard_map/ppermute | solution.py:339
  61.8 7.6 %collective-permute-done.20 = bf16[2,16,16,128]{3,2,1,0:T(8,128)(2,1)S(1)} collective-permute-done((bf16[2,16,16,128]{3,2,1,0:T(8,128)(2,1)S(1)}, bf16[2,16,16,128]{3,2,1,0:T(8,128)(2,1)S(1)}, u32[]{:S(2)}, u32[]{:S(2)}) %collective-permute-start.20) | collective-permute-done | bytes 131104 | tf_op jit(solution)/shard_map/ppermute | solution.py:339
  69.4 0.0 collective-permute-done.21
  69.4 0.1 fusion.2
  69.5 0.8 %pad_maximum_fusion = (f32[32,16,128]{2,1,0:T(8,128)}, f32[32,16,128]{2,1,0:T(8,128)}) fusion(f32[16,16,128]{2,1,0:T(8,128)S(1)} %get-tuple-element.51, f32[16,16,128]{2,1,0:T(8,128)S(1)} %get-tuple-element.49, f32[16,16,128]{2,1,0:T(8,128)S(1)} %get-tuple-element.50, f32[16,16,128]{2,1,0:T(8,128)S(1)} %get-tuple-element.48), kind=kLoop, calls=%fused_computation.4 | loop fusion | flops 131072 | bytes 1048576 | tf_op jit(solution)/shard_map/concatenate | solution.py:403
  (16 shorter events, 0.2 us)
Async XLA Ops:
  2.7 10.4 %collective-permute-start.5 = (bf16[2,2,16,16,128]{4,3,2,1,0:T(8,128)(2,1)S(1)}, bf16[2,2,16,16,128]{4,3,2,1,0:T(8,128)(2,1)S(1)}, u32[]{:S(2)}, u32[]{:S(2)}) collective-permute-start(bf16[2,2,16,16,128]{4,3,2,1,0:T(8,128)(2,1)S(1)} %get-tuple-element.27), channel_id=1, source_target_pairs={{0,16},{8,24},{1,17},{9,25},{2,18},{10,26},{3,19},{11,27},{4,20},{... | collective-permute-start | bytes 786440 | tf_op jit(solution)/shard_map/ppermute | solution.py:325
  7.6 10.3 %collective-permute-start.4 = (bf16[2,16,16,128]{3,2,1,0:T(8,128)(2,1)S(1)}, bf16[2,16,16,128]{3,2,1,0:T(8,128)(2,1)S(1)}, u32[]{:S(2)}, u32[]{:S(2)}) collective-permute-start(bf16[2,16,16,128]{3,2,1,0:T(8,128)(2,1)S(1)} %get-tuple-element.26), channel_id=1, source_target_pairs={{0,8},{8,0},{16,24},{24,16},{1,9},{9,1},{17,25},{25,17},{2,10},{10... | collective-permute-start | bytes 393224 | tf_op jit(solution)/shard_map/ppermute | solution.py:325
  7.7 17.0 %collective-permute-start.3 = (bf16[2,8,128,128]{3,2,1,0:T(8,128)(2,1)S(1)}, bf16[2,8,128,128]{3,2,1,0:T(8,128)(2,1)S(1)}, u32[]{:S(2)}, u32[]{:S(2)}) collective-permute-start(bf16[2,8,128,128]{3,2,1,0:T(8,128)(2,1)S(1)} %get-tuple-element.25), channel_id=1, source_target_pairs={{0,1},{1,0},{2,3},{3,2},{4,5},{5,4},{6,7},{7,6},{8,9},{9,8},{10,11... | collective-permute-start | bytes 1572872 | tf_op jit(solution)/shard_map/ppermute | solution.py:361
  13.2 4.8 %collective-permute-start.6 = (bf16[2,16,16,128]{3,2,1,0:T(8,128)(2,1)S(1)}, bf16[2,16,16,128]{3,2,1,0:T(8,128)(2,1)S(1)}, u32[]{:S(2)}, u32[]{:S(2)}) collective-permute-start(bf16[2,16,16,128]{3,2,1,0:T(8,128)(2,1)S(1)} %slice_bitcast_fusion.3), channel_id=1, source_target_pairs={{0,8},{8,0},{16,24},{24,16},{1,9},{9,1},{17,25},{25,17},{2,10},{10... | collective-permute-start | bytes 393224 | tf_op jit(solution)/shard_map/ppermute | solution.py:325
  13.3 10.1 %collective-permute-start.1 = (bf16[2,2,8,16,128]{4,3,2,1,0:T(8,128)(2,1)S(1)}, bf16[2,2,8,16,128]{4,3,2,1,0:T(8,128)(2,1)S(1)}, u32[]{:S(2)}, u32[]{:S(2)}) collective-permute-start(bf16[2,2,8,16,128]{4,3,2,1,0:T(8,128)(2,1)S(1)} %get-tuple-element.24), channel_id=1, source_target_pairs={{0,16},{8,24},{1,17},{9,25},{2,18},{10,26},{3,19},{11,27},{4,20},{... | collective-permute-start | bytes 393224 | tf_op jit(solution)/shard_map/ppermute | solution.py:325
  17.7 6.3 %collective-permute-start = (bf16[2,8,16,128]{3,2,1,0:T(8,128)(2,1)S(1)}, bf16[2,8,16,128]{3,2,1,0:T(8,128)(2,1)S(1)}, u32[]{:S(2)}, u32[]{:S(2)}) collective-permute-start(bf16[2,8,16,128]{3,2,1,0:T(8,128)(2,1)S(1)} %get-tuple-element.23), channel_id=1, source_target_pairs={{0,8},{8,0},{16,24},{24,16},{1,9},{9,1},{17,25},{25,17},{2,10},{10... | collective-permute-start | bytes 196616 | tf_op jit(solution)/shard_map/ppermute | solution.py:325
  22.1 10.4 %collective-permute-start.16 = (bf16[2,2,16,16,128]{4,3,2,1,0:T(8,128)(2,1)S(1)}, bf16[2,2,16,16,128]{4,3,2,1,0:T(8,128)(2,1)S(1)}, u32[]{:S(2)}, u32[]{:S(2)}) collective-permute-start(bf16[2,2,16,16,128]{4,3,2,1,0:T(8,128)(2,1)S(1)} %get-tuple-element.40), channel_id=1, source_target_pairs={{16,0},{24,8},{17,1},{25,9},{18,2},{26,10},{19,3},{27,11},{20,4},{... | collective-permute-start | bytes 786440 | tf_op jit(solution)/shard_map/ppermute | solution.py:325
  23.4 1.3 %collective-permute-start.2 = (bf16[2,8,16,128]{3,2,1,0:T(8,128)(2,1)S(1)}, bf16[2,8,16,128]{3,2,1,0:T(8,128)(2,1)S(1)}, u32[]{:S(2)}, u32[]{:S(2)}) collective-permute-start(bf16[2,8,16,128]{3,2,1,0:T(8,128)(2,1)S(1)} %slice_bitcast_fusion.5), channel_id=1, source_target_pairs={{0,8},{8,0},{16,24},{24,16},{1,9},{9,1},{17,25},{25,17},{2,10},{10... | collective-permute-start | bytes 196616 | tf_op jit(solution)/shard_map/ppermute | solution.py:325
  23.8 12.1 %collective-permute-start.15 = (bf16[2,16,16,128]{3,2,1,0:T(8,128)(2,1)S(1)}, bf16[2,16,16,128]{3,2,1,0:T(8,128)(2,1)S(1)}, u32[]{:S(2)}, u32[]{:S(2)}) collective-permute-start(bf16[2,16,16,128]{3,2,1,0:T(8,128)(2,1)S(1)} %get-tuple-element.39), channel_id=1, source_target_pairs={{0,8},{8,0},{16,24},{24,16},{1,9},{9,1},{17,25},{25,17},{2,10},{10... | collective-permute-start | bytes 393224 | tf_op jit(solution)/shard_map/ppermute | solution.py:325
  28.1 7.7 %collective-permute-start.9 = (bf16[2,2,8,16,128]{4,3,2,1,0:T(8,128)(2,1)S(1)}, bf16[2,2,8,16,128]{4,3,2,1,0:T(8,128)(2,1)S(1)}, u32[]{:S(2)}, u32[]{:S(2)}) collective-permute-start(bf16[2,2,8,16,128]{4,3,2,1,0:T(8,128)(2,1)S(1)} %get-tuple-element.33), channel_id=1, source_target_pairs={{16,0},{24,8},{17,1},{25,9},{18,2},{26,10},{19,3},{27,11},{20,4},{... | collective-permute-start | bytes 393224 | tf_op jit(solution)/shard_map/ppermute | solution.py:325
  29.4 9.4 %collective-permute-start.8 = (bf16[2,8,16,128]{3,2,1,0:T(8,128)(2,1)S(1)}, bf16[2,8,16,128]{3,2,1,0:T(8,128)(2,1)S(1)}, u32[]{:S(2)}, u32[]{:S(2)}) collective-permute-start(bf16[2,8,16,128]{3,2,1,0:T(8,128)(2,1)S(1)} %get-tuple-element.32), channel_id=1, source_target_pairs={{0,8},{8,0},{16,24},{24,16},{1,9},{9,1},{17,25},{25,17},{2,10},{10... | collective-permute-start | bytes 196616 | tf_op jit(solution)/shard_map/ppermute | solution.py:325
  29.8 14.3 %collective-permute-start.7 = (bf16[8,128,128]{2,1,0:T(8,128)(2,1)S(1)}, bf16[8,128,128]{2,1,0:T(8,128)(2,1)S(1)}, u32[]{:S(2)}, u32[]{:S(2)}) collective-permute-start(bf16[8,128,128]{2,1,0:T(8,128)(2,1)S(1)} %get-tuple-element.30), channel_id=1, source_target_pairs={{0,1},{1,0},{2,3},{3,2},{4,5},{5,4},{6,7},{7,6},{8,9},{9,8},{10,11... | collective-permute-start | bytes 786440 | tf_op jit(solution)/shard_map/ppermute | solution.py:361
  32.5 3.4 %collective-permute-start.17 = (bf16[2,16,16,128]{3,2,1,0:T(8,128)(2,1)S(1)}, bf16[2,16,16,128]{3,2,1,0:T(8,128)(2,1)S(1)}, u32[]{:S(2)}, u32[]{:S(2)}) collective-permute-start(bf16[2,16,16,128]{3,2,1,0:T(8,128)(2,1)S(1)} %slice_bitcast_fusion.2), channel_id=1, source_target_pairs={{0,8},{8,0},{16,24},{24,16},{1,9},{9,1},{17,25},{25,17},{2,10},{10... | collective-permute-start | bytes 393224 | tf_op jit(solution)/shard_map/ppermute | solution.py:325
  35.9 2.9 %collective-permute-start.10 = (bf16[2,8,16,128]{3,2,1,0:T(8,128)(2,1)S(1)}, bf16[2,8,16,128]{3,2,1,0:T(8,128)(2,1)S(1)}, u32[]{:S(2)}, u32[]{:S(2)}) collective-permute-start(bf16[2,8,16,128]{3,2,1,0:T(8,128)(2,1)S(1)} %slice_bitcast_fusion.4), channel_id=1, source_target_pairs={{0,8},{8,0},{16,24},{24,16},{1,9},{9,1},{17,25},{25,17},{2,10},{10... | collective-permute-start | bytes 196616 | tf_op jit(solution)/shard_map/ppermute | solution.py:325
  37.2 17.6 %collective-permute-start.18 = (bf16[2,16,2,2,16,128]{5,4,1,0,3,2:T(8,128)(2,1)S(1)}, bf16[2,16,2,2,16,128]{5,4,1,0,3,2:T(8,128)(2,1)S(1)}, u32[]{:S(2)}, u32[]{:S(2)}) collective-permute-start(bf16[2,16,2,2,16,128]{5,4,1,0,3,2:T(8,128)(2,1)S(1)} %copy.11), channel_id=1, source_target_pairs={{0,1},{1,0},{2,3},{3,2},{4,5},{5,4},{6,7},{7,6},{8,9},{9,8},{10,11... | collective-permute-start | bytes 1572872 | tf_op jit(solution)/shard_map/ppermute | solution.py:339
  39.7 7.6 %collective-permute-start.11 = (bf16[2,8,2,16,128]{4,3,2,1,0:T(8,128)(2,1)S(1)}, bf16[2,8,2,16,128]{4,3,2,1,0:T(8,128)(2,1)S(1)}, u32[]{:S(2)}, u32[]{:S(2)}) collective-permute-start(bf16[2,8,2,16,128]{4,3,2,1,0:T(8,128)(2,1)S(1)} %get-tuple-element.35), channel_id=1, source_target_pairs={{0,2},{1,3},{2,0},{3,1},{4,6},{5,7},{6,4},{7,5},{8,10},{9,11},{10,... | collective-permute-start | bytes 393224 | tf_op jit(solution)/shard_map/ppermute | solution.py:339
  41.3 12.9 %collective-permute-start.12 = (bf16[2,8,2,16,128]{4,3,2,1,0:T(8,128)(2,1)S(1)}, bf16[2,8,2,16,128]{4,3,2,1,0:T(8,128)(2,1)S(1)}, u32[]{:S(2)}, u32[]{:S(2)}) collective-permute-start(bf16[2,8,2,16,128]{4,3,2,1,0:T(8,128)(2,1)S(1)} %get-tuple-element.36), channel_id=1, source_target_pairs={{0,4},{1,5},{2,6},{3,7},{4,0},{5,1},{6,2},{7,3},{8,12},{9,13},{10,... | collective-permute-start | bytes 393224 | tf_op jit(solution)/shard_map/ppermute | solution.py:339
  43.9 10.3 %collective-permute-start.13 = (bf16[2,8,2,16,128]{4,3,2,1,0:T(8,128)(2,1)S(1)}, bf16[2,8,2,16,128]{4,3,2,1,0:T(8,128)(2,1)S(1)}, u32[]{:S(2)}, u32[]{:S(2)}) collective-permute-start(bf16[2,8,2,16,128]{4,3,2,1,0:T(8,128)(2,1)S(1)} %get-tuple-element.37), channel_id=1, source_target_pairs={{0,6},{1,7},{2,4},{3,5},{4,2},{5,3},{6,0},{7,1},{8,14},{9,15},{10,... | collective-permute-start | bytes 393224 | tf_op jit(solution)/shard_map/ppermute | solution.py:339
  54.3 5.7 %collective-permute-start.14 = (bf16[2,8,16,128]{3,2,1,0:T(8,128)(2,1)S(1)}, bf16[2,8,16,128]{3,2,1,0:T(8,128)(2,1)S(1)}, u32[]{:S(2)}, u32[]{:S(2)}) collective-permute-start(bf16[2,8,16,128]{3,2,1,0:T(8,128)(2,1)S(1)} %fusion.6), channel_id=1, source_target_pairs={{0,1},{1,0},{2,3},{3,2},{4,5},{5,4},{6,7},{7,6},{8,9},{9,8},{10,11... | collective-permute-start | bytes 196616 | tf_op jit(solution)/shard_map/ppermute | solution.py:361
  55.1 6.7 %collective-permute-start.19 = (bf16[2,16,16,128]{3,2,1,0:T(8,128)(2,1)S(1)}, bf16[2,16,16,128]{3,2,1,0:T(8,128)(2,1)S(1)}, u32[]{:S(2)}, u32[]{:S(2)}) collective-permute-start(bf16[2,16,16,128]{3,2,1,0:T(8,128)(2,1)S(1)} %get-tuple-element.43), channel_id=1, source_target_pairs={{0,2},{1,3},{2,0},{3,1},{4,6},{5,7},{6,4},{7,5},{8,10},{9,11},{10,... | collective-permute-start | bytes 393224 | tf_op jit(solution)/shard_map/ppermute | solution.py:339
  57.5 11.9 %collective-permute-start.20 = (bf16[2,16,16,128]{3,2,1,0:T(8,128)(2,1)S(1)}, bf16[2,16,16,128]{3,2,1,0:T(8,128)(2,1)S(1)}, u32[]{:S(2)}, u32[]{:S(2)}) collective-permute-start(bf16[2,16,16,128]{3,2,1,0:T(8,128)(2,1)S(1)} %get-tuple-element.45), channel_id=1, source_target_pairs={{0,4},{1,5},{2,6},{3,7},{4,0},{5,1},{6,2},{7,3},{8,12},{9,13},{10,... | collective-permute-start | bytes 393224 | tf_op jit(solution)/shard_map/ppermute | solution.py:339
  58.6 10.8 %collective-permute-start.21 = (bf16[2,16,16,128]{3,2,1,0:T(8,128)(2,1)S(1)}, bf16[2,16,16,128]{3,2,1,0:T(8,128)(2,1)S(1)}, u32[]{:S(2)}, u32[]{:S(2)}) collective-permute-start(bf16[2,16,16,128]{3,2,1,0:T(8,128)(2,1)S(1)} %get-tuple-element.44), channel_id=1, source_target_pairs={{0,6},{1,7},{2,4},{3,5},{4,2},{5,3},{6,0},{7,1},{8,14},{9,15},{10,... | collective-permute-start | bytes 393224 | tf_op jit(solution)/shard_map/ppermute | solution.py:339

commit v2 on v1

--- a/solution.py
+++ b/solution.py
@@ -13,7 +13,7 @@
 PLAN = ((16, 16, False, (1, 2)), (0, 16, True, (2,)))
 STEP_HEADS = 8
 VMEM_SMALL = 8 << 20
-VMEM_ATTEND = 24 << 20
+VMEM_ATTEND = 16 << 20
 
 
 def far_masks(groups):
@@ -176,10 +176,10 @@
     return max(step for step in range(1, STEP_HEADS + 1) if math.gcd(step, heads, *offsets) == step)
 
 
-def attend(half, query, grad, keys, values, far, swapped, groups, cut, query_out):
+def attend(half, rows, far, swapped, groups, cut, query_shape, query_out):
     first_head, heads, paired, _ = cut
-    _, tokens, head_dim = query.shape
-    group_keys = keys.shape[1]
+    _, tokens, head_dim = query_shape
+    group_keys = rows[2].shape[1]
     masks = far_masks(groups)
     near_keys = group_keys + KB * len(masks)
     if paired:
@@ -188,7 +188,7 @@
     first_step = first_head // step_heads
     half_steps = heads // step_heads if paired else 0
 
-    def rows(count):
+    def placed(count):
         return pl.BlockSpec(
             (step_heads, count, head_dim),
             lambda i, half: (first_step + half[0] * half_steps + i, 0, 0),
@@ -199,11 +199,11 @@
 
     both = pl.BlockSpec((2, 2, step_heads, KB, head_dim), lambda i, half: (0, 0, i, 0, 0))
     block = (2, heads, KB, head_dim)
-    shapes = [query.shape, (2, heads, group_keys, head_dim), block]
+    shapes = [query_shape, (2, heads, group_keys, head_dim), block]
     shapes += [(2,) + block] * (groups // 2 - 1)
-    out_specs = [rows(tokens), pair(group_keys), pair(KB)] + [both] * (groups // 2 - 1)
-    operands = [half, query, grad, keys, values, *far]
-    in_specs = [rows(tokens), rows(tokens), rows(group_keys), rows(group_keys)]
+    out_specs = [placed(tokens), pair(group_keys), pair(KB)] + [both] * (groups // 2 - 1)
+    operands = [half, *rows, *far]
+    in_specs = [placed(tokens)] * 2 + [placed(group_keys)] * 2
     in_specs += slot_specs(groups, step_heads, (KB,), head_dim)
     aliases = {}
     if paired:
@@ -317,17 +317,14 @@
         for first, parts, paired, order in PLAN
     ]
 
-    def exchange(near, pairs, forward):
-        def hop(rows, mask, both=False):
-            links = [
-                (g, g ^ mask) for g in range(groups) if both or ((g ^ mask) > g) == forward
-            ]
-            return lax.ppermute(rows, "blk", links)
+    def exchange(near, pairs):
+        def hop(rows, mask):
+            return lax.ppermute(rows, "blk", [(g, g ^ mask) for g in range(groups)])
 
         crossed = [hop(pair, 2 * i) for i, pair in enumerate(pairs, 1)]
-        slots = [hop(near, 1, both=True)]
+        slots = [hop(near, 1)]
         for pair in crossed:
-            slots += [pair, hop(pair[1], 1, both=True)]
+            slots += [pair, hop(pair[1], 1)]
         return slots
 
     def scatter(pieces, stages):
@@ -335,10 +332,13 @@
         for step, stage in enumerate(stages):
             left = [bit for bit in left if bit not in stage]
             shape = (2, pieces[0].shape[1]) + (2,) * len(left) + (rank_keys, head_dim)
-            came = [
-                lax.ppermute(piece.reshape(shape), "ulysses", [(r, r ^ mix) for r in range(ranks)])
-                for mix, piece in zip(mixes(stage)[1:], pieces[1:])
-            ]
+            came = []
+            for mix, piece in zip(mixes(stage)[1:], pieces[1:]):
+                came.append(
+                    lax.ppermute(
+                        piece.reshape(shape), "ulysses", [(r, r ^ mix) for r in range(ranks)]
+                    )
+                )
             total = pieces[0].reshape(shape).astype(jnp.float32)
             for part in came:
                 total = total + part.astype(jnp.float32)
@@ -370,6 +370,7 @@
 
     half_operand = half.astype(jnp.int32).reshape(1)
     picked = pick(routes, query_rows, out_grad, key_rows, value_rows, groups, cuts)
+    local_rows = (query_rows, out_grad, key_rows, value_rows)
     query_out = None
     results = []
     others = []
@@ -377,14 +378,13 @@
     for swapped, parts in picked:
         if swapped is not None:
             swapped = trade(swapped)
-        fetched.append((swapped, exchange(parts[0], parts[1:], True)))
+        fetched.append((swapped, exchange(parts[0], parts[1:])))
     for number, cut in enumerate(cuts):
         swapped, far = fetched[number]
         other, query_out, own, parts = attend(
-            half_operand, query_rows, out_grad, key_rows, value_rows, far, swapped,
-            groups, cut, query_out,
-        )
-        back = exchange(parts[0], parts[1:], False)
+            half_operand, local_rows, far, swapped, groups, cut, query_rows.shape, query_out
+        )
+        back = exchange(parts[0], parts[1:])
         if other is not None:
             others.append((cut, trade(other)))
         wanted = [bit for bit in bits if not (cut[2] and bit == 1)]
@@ -395,13 +395,22 @@
                 wanted = wanted[size:]
         pieces = merge(routes, own, back, groups, ranks, stages[0])
         total = scatter(pieces, stages)
-        results.append(join(total) if cut[2] else total)
+        if cut[2]:
+            total = join(total)
+        results.append(total)
     for cut, rows in others:
         first = cut[0] + (1 - half) * (cut[1] // 2)
         query_out = lax.dynamic_update_slice_in_dim(query_out, rows, first, 0)
-    placed = [results[number] for number in sorted(range(len(cuts)), key=lambda n: cuts[n][0])]
-    key_grad = jnp.concatenate([total[0] for total in placed], axis=0)
-    value_grad = jnp.concatenate([total[1] for total in placed], axis=0)
+    order = sorted(range(len(cuts)), key=lambda number: cuts[number][0])
+    grads = []
+    for side in range(2):
+        base = lax.optimization_barrier(
+            jnp.concatenate(
+                [results[n][side] if n else jnp.zeros_like(results[0][side]) for n in order]
+            )
+        )
+        grads.append(lax.dynamic_update_slice_in_dim(base, results[0][side], cuts[0][0], 0))
+    key_grad, value_grad = grads
     return (query_out, key_grad, value_grad)
 
 

time: 70.7 us -> 64.4 us (0.911)
  starting transfers between devices: 27.9 us -> 22.3 us
  other arithmetic: 1.14 us -> 0.32 us
  local copies, waits for them, and re-layouts: 0.87 us -> 1.68 us
    ppermute x12, starting transfers between devices: 13.3 us -> 7.74 us  [hop(): return lax.ppermute(rows, 'blk', [(g, g ^ mask) for g in range(groups)])]
    concatenate x1 -> x0, other arithmetic: 0.82 us -> none  [body(): key_grad = jnp.concatenate([total[0] for total in placed], axis=0)]
    unnamed x0 -> x4, local copies, waits for them, and re-layouts: none -> 0.78 us
  transfers between devices with their start and end apart: 22 -> 22, of which waited for: 8 -> 8; matrix products, arithmetic and copies ran while one was open for 2% -> 2% of each run, Pallas kernels for 14% -> 15%
where the time goes in v2:
time: 64.4 us; the launch traced here: 64.1 us
  waiting for transfers between devices  27.2 us (42%)
  starting transfers between devices  22.3 us (35%)
  Pallas kernels  11.8 us (18%)
  local copies, waits for them, and re-layouts  1.68 us (3%)
  between operations  0.82 us (1%)
    ppermute x7, waiting for transfers between devices, scatter(): lax.ppermute(piece.reshape(shape), 'ulysses', [(r, r ^ mix) for r in rang...  18.7 us
    ppermute x7, starting transfers between devices, scatter(): lax.ppermute(piece.reshape(shape), 'ulysses', [(r, r ^ mix) for r in rang...  10.9 us
    ppermute x12, waiting for transfers between devices, hop(): return lax.ppermute(rows, 'blk', [(g, g ^ mask) for g in range(groups)])  8.56 us
    ppermute x12, starting transfers between devices, hop(): return lax.ppermute(rows, 'blk', [(g, g ^ mask) for g in range(groups)])  7.74 us
    pallas_call x2, Pallas kernels, attend(): pl.pallas_call(functools.partial(attend_kernel, masks, query_out is not N...  7.54 us
    ppermute x3, starting transfers between devices, trade(): return lax.ppermute(rows, 'ulysses', [(r, r ^ 1) for r in range(ranks)])  3.62 us
    pallas_call x2, Pallas kernels, merge(): pl.pallas_call(functools.partial(merge_kernel, masks, bits), out_shape=[j...  2.13 us
    pallas_call x1, Pallas kernels, pick(): pl.pallas_call(functools.partial(pick_kernel, cuts, groups), out_shape=[j...  2.11 us
  transfers between devices with their start and end apart: 22, of which 8 were waited for; matrix products, arithmetic and copies ran while one was open for 2% of the time, Pallas kernels for 15%

profile of v2, /device:TPU:0, one launch (start us, length us, event | category | flops | bytes accessed | tf_op | source)
XLA Modules:
  0.0 64.1 jit_solution(17493985919645494233)
XLA Ops:
  0.6 2.1 %pick.1 = (bf16[2,16,16,128]{3,2,1,0:T(8,128)(2,1)S(1)}, bf16[2,2,16,16,128]{4,3,2,1,0:T(8,128)(2,1)S(1)}, bf16[2,8,128,128]{3,2,1,0:T(8,128)(2,1)S(1)}, bf16[2,...) custom-call(s32[4,4]{1,0:T(4,128)} %routes.5, bf16[32,128,128]{2,1,0:T(8,128)(2,1)} %query.5, ...), custom_call_target="tpu_custom_call" | custom-call | tf_op jit(solution)/shard_map/pick/pallas_call | solution.py:70
  2.7 3.0 %collective-permute-start.5 = (bf16[2,2,16,16,128]{4,3,2,1,0:T(8,128)(2,1)S(1)}, bf16[2,2,16,16,128]{4,3,2,1,0:T(8,128)(2,1)S(1)}, u32[]{:S(2)}, u32[]{:S(2)}) collective-permute-start(bf16[2,2,16,16,128]{4,3,2,1,0:T(8,128)(2,1)S(1)} %get-tuple-element.27), channel_id=1, source_target_pairs={{0,16},{8,24},{16,0},{24,8},{1,17},{9,25},{17,1},{25,9},{2,18},{10... | collective-permute-start | bytes 786440 | tf_op jit(solution)/shard_map/ppermute | solution.py:322
  5.8 0.0 collective-permute-start.4
  5.8 1.5 %collective-permute-start.3 = (bf16[2,8,128,128]{3,2,1,0:T(8,128)(2,1)S(1)}, bf16[2,8,128,128]{3,2,1,0:T(8,128)(2,1)S(1)}, u32[]{:S(2)}, u32[]{:S(2)}) collective-permute-start(bf16[2,8,128,128]{3,2,1,0:T(8,128)(2,1)S(1)} %get-tuple-element.25), channel_id=1, source_target_pairs={{0,1},{1,0},{2,3},{3,2},{4,5},{5,4},{6,7},{7,6},{8,9},{9,8},{10,11... | collective-permute-start | bytes 1572872 | tf_op jit(solution)/shard_map/ppermute | solution.py:361
  7.3 4.8 %collective-permute-done.5.rest_1_ = bf16[2,2,16,16,128]{4,3,2,1,0:T(8,128)(2,1)S(1)} collective-permute-done((bf16[2,2,16,16,128]{4,3,2,1,0:T(8,128)(2,1)S(1)}, bf16[2,2,16,16,128]{4,3,2,1,0:T(8,128)(2,1)S(1)}, u32[]{:S(2)}, u32[]{:S(2)}) %collective-permute-start.5) | collective-permute-done | bytes 262176 | tf_op jit(solution)/shard_map/ppermute | solution.py:322
  12.1 0.1 collective-permute-start.6
  12.2 1.8 %collective-permute-start.1 = (bf16[2,2,8,16,128]{4,3,2,1,0:T(8,128)(2,1)S(1)}, bf16[2,2,8,16,128]{4,3,2,1,0:T(8,128)(2,1)S(1)}, u32[]{:S(2)}, u32[]{:S(2)}) collective-permute-start(bf16[2,2,8,16,128]{4,3,2,1,0:T(8,128)(2,1)S(1)} %get-tuple-element.24), channel_id=1, source_target_pairs={{0,16},{8,24},{16,0},{24,8},{1,17},{9,25},{17,1},{25,9},{2,18},{10... | collective-permute-start | bytes 393224 | tf_op jit(solution)/shard_map/ppermute | solution.py:322
  14.0 0.2 collective-permute-start
  14.1 0.0 collective-permute-done.4.rest_0_
  14.1 0.0 collective-permute-done.6.rest_2_
  14.1 4.2 %attend.2 = (bf16[32,128,128]{2,1,0:T(8,128)(2,1)}, bf16[2,16,128,128]{3,2,1,0:T(8,128)(2,1)S(1)}, bf16[2,16,16,128]{3,2,1,0:T(8,128)(2,1)S(1)}, bf16[2,2,16,16,128]{4,3,2,1,0:T(8,128)(2,1)S(1)}) custom-call(s32[1]{0:T(128)} %bitcast._, bf16[32,128,128]{2,1,0:T(8,128)(2,1)} %query.5, bf16[32,128,128]{2,1,0:T(8,128)(2,1)} %grad.5, ...), custom_call_target="tpu_custom_call" | custom-call | tf_op jit(solution)/shard_map/attend/pallas_call | solution.py:221
  18.3 1.1 %collective-permute-start.16 = (bf16[2,2,16,16,128]{4,3,2,1,0:T(8,128)(2,1)S(1)}, bf16[2,2,16,16,128]{4,3,2,1,0:T(8,128)(2,1)S(1)}, u32[]{:S(2)}, u32[]{:S(2)}) collective-permute-start(bf16[2,2,16,16,128]{4,3,2,1,0:T(8,128)(2,1)S(1)} %get-tuple-element.40), channel_id=1, source_target_pairs={{0,16},{8,24},{16,0},{24,8},{1,17},{9,25},{17,1},{25,9},{2,18},{10... | collective-permute-start | bytes 786440 | tf_op jit(solution)/shard_map/ppermute | solution.py:322
  19.4 0.0 collective-permute-done.1.rest_1_
  19.4 0.1 collective-permute-start.2
  19.5 0.5 collective-permute-start.15
  20.0 0.0 collective-permute-done.rest_0_
  20.0 0.7 %collective-permute-done.2.rest_2_ = bf16[2,8,16,128]{3,2,1,0:T(8,128)(2,1)S(1)} collective-permute-done((bf16[2,8,16,128]{3,2,1,0:T(8,128)(2,1)S(1)}, bf16[2,8,16,128]{3,2,1,0:T(8,128)(2,1)S(1)}, u32[]{:S(2)}, u32[]{:S(2)}) %collective-permute-start.2) | collective-permute-done | bytes 65568 | tf_op jit(solution)/shard_map/ppermute | solution.py:322
  20.7 3.4 %attend.3 = (bf16[8,128,128]{2,1,0:T(8,128)(2,1)S(1)}, bf16[32,128,128]{2,1,0:T(8,128)(2,1)}, bf16[2,8,128,128]{3,2,1,0:T(8,128)(2,1)S(1)}, bf16[2,8,16,128]{3,2...) custom-call(s32[1]{0:T(128)} %bitcast._, bf16[32,128,128]{2,1,0:T(8,128)(2,1)} %query.5, ...), custom_call_target="tpu_custom_call", output_to_operand_aliasing={{1}: (9, {})} | custom-call | tf_op jit(solution)/shard_map/attend/pallas_call | solution.py:221
  24.1 0.9 %collective-permute-start.9 = (bf16[2,2,8,16,128]{4,3,2,1,0:T(8,128)(2,1)S(1)}, bf16[2,2,8,16,128]{4,3,2,1,0:T(8,128)(2,1)S(1)}, u32[]{:S(2)}, u32[]{:S(2)}) collective-permute-start(bf16[2,2,8,16,128]{4,3,2,1,0:T(8,128)(2,1)S(1)} %get-tuple-element.33), channel_id=1, source_target_pairs={{0,16},{8,24},{16,0},{24,8},{1,17},{9,25},{17,1},{25,9},{2,18},{10... | collective-permute-start | bytes 393224 | tf_op jit(solution)/shard_map/ppermute | solution.py:322
  25.0 0.0 collective-permute-start.8
  25.0 1.5 %collective-permute-start.7 = (bf16[8,128,128]{2,1,0:T(8,128)(2,1)S(1)}, bf16[8,128,128]{2,1,0:T(8,128)(2,1)S(1)}, u32[]{:S(2)}, u32[]{:S(2)}) collective-permute-start(bf16[8,128,128]{2,1,0:T(8,128)(2,1)S(1)} %get-tuple-element.30), channel_id=1, source_target_pairs={{0,1},{1,0},{2,3},{3,2},{4,5},{5,4},{6,7},{7,6},{8,9},{9,8},{10,11... | collective-permute-start | bytes 786440 | tf_op jit(solution)/shard_map/ppermute | solution.py:361
  26.6 0.3 collective-permute-done.16
  26.9 0.1 collective-permute-start.17
  27.0 2.7 %collective-permute-done.9 = bf16[2,2,8,16,128]{4,3,2,1,0:T(8,128)(2,1)S(1)} collective-permute-done((bf16[2,2,8,16,128]{4,3,2,1,0:T(8,128)(2,1)S(1)}, bf16[2,2,8,16,128]{4,3,2,1,0:T(8,128)(2,1)S(1)}, u32[]{:S(2)}, u32[]{:S(2)}) %collective-permute-start.9) | collective-permute-done | bytes 131104 | tf_op jit(solution)/shard_map/ppermute | solution.py:322
  29.7 0.0 collective-permute-start.10
  29.7 0.0 collective-permute-done.15
  29.7 1.3 %merge.3 = (bf16[2,16,4,16,128]{4,3,2,1,0:T(8,128)(2,1)S(1)}, bf16[2,16,4,16,128]{4,3,2,1,0:T(8,128)(2,1)S(1)}) custom-call(s32[4,4]{1,0:T(4,128)} %routes.5, bf16[2,16,8,16,128]{4,3,2,1,0:T(8,128)(2,1)S(1)} %bitcast.50, bf16[2,16,1,16,128]{4,3,2,1,0:T(8,128)(2,1)S(1)} %bitcast.56, bf16[2,2,16,1,16,128]{5,4,3,2,1,0:T(8,128)(2,1)S(1)} %bitcast.51, ...), custom_call_target="tpu_custom_call" | custom-call | tf_op jit(solution)/shard_map/merge/pallas_call | solution.py:282
  31.0 1.6 %collective-permute-start.18 = (bf16[2,16,2,2,16,128]{5,4,1,0,3,2:T(8,128)(2,1)S(1)}, bf16[2,16,2,2,16,128]{5,4,1,0,3,2:T(8,128)(2,1)S(1)}, u32[]{:S(2)}, u32[]{:S(2)}) collective-permute-start(bf16[2,16,2,2,16,128]{5,4,1,0,3,2:T(8,128)(2,1)S(1)} %copy.11), channel_id=1, source_target_pairs={{0,1},{1,0},{2,3},{3,2},{4,5},{5,4},{6,7},{7,6},{8,9},{9,8},{10,11... | collective-permute-start | bytes 1572872 | tf_op jit(solution)/shard_map/ppermute | solution.py:338
  32.6 0.9 %merge.2 = (bf16[2,8,2,16,128]{4,3,2,1,0:T(8,128)(2,1)S(1)}, bf16[2,8,2,16,128]{4,3,2,1,0:T(8,128)(2,1)S(1)}, bf16[2,8,2,16,128]{4,3,2,1,0:T(8,128)(2,1)S(1)}, bf16[2,8,2,16,128]{4,3,2,1,0:T(8,128)(2,1)S(1)}) custom-call(s32[4,4]{1,0:T(4,128)} %routes.5, bf16[2,8,8,16,128]{4,3,2,1,0:T(8,128)(2,1)S(1)} %bitcast.53, bf16[2,8,1,16,128]{4,3,2,1,0:T(8,128)(2,1)S(1)} %bitcast.58, ...), custom_call_target="tpu_custom_call" | custom-call | tf_op jit(solution)/shard_map/merge/pallas_call | solution.py:282
  33.5 1.6 %collective-permute-start.11 = (bf16[2,8,2,16,128]{4,3,2,1,0:T(8,128)(2,1)S(1)}, bf16[2,8,2,16,128]{4,3,2,1,0:T(8,128)(2,1)S(1)}, u32[]{:S(2)}, u32[]{:S(2)}) collective-permute-start(bf16[2,8,2,16,128]{4,3,2,1,0:T(8,128)(2,1)S(1)} %get-tuple-element.35), channel_id=1, source_target_pairs={{0,2},{1,3},{2,0},{3,1},{4,6},{5,7},{6,4},{7,5},{8,10},{9,11},{10,... | collective-permute-start | bytes 393224 | tf_op jit(solution)/shard_map/ppermute | solution.py:338
  35.1 2.6 %collective-permute-start.12 = (bf16[2,8,2,16,128]{4,3,2,1,0:T(8,128)(2,1)S(1)}, bf16[2,8,2,16,128]{4,3,2,1,0:T(8,128)(2,1)S(1)}, u32[]{:S(2)}, u32[]{:S(2)}) collective-permute-start(bf16[2,8,2,16,128]{4,3,2,1,0:T(8,128)(2,1)S(1)} %get-tuple-element.36), channel_id=1, source_target_pairs={{0,4},{1,5},{2,6},{3,7},{4,0},{5,1},{6,2},{7,3},{8,12},{9,13},{10,... | collective-permute-start | bytes 393224 | tf_op jit(solution)/shard_map/ppermute | solution.py:338
  37.7 0.2 collective-permute-start.13
  37.9 0.7 %constant_dynamic-update-slice_fusion = bf16[32,128,128]{2,1,0:T(8,128)(2,1)} fusion(bf16[32,128,128]{2,1,0:T(8,128)(2,1)} %get-tuple-element.29, bf16[8,128,128]{2,1,0:T(8,128)(2,1)S(1)} %collective-permute-done.7, s32[]{:T(128)S(6)} %select_n.111), kind=kLoop, calls=%fused_computation.27 | loop fusion | bytes 524292 | tf_op jit(solution)/shard_map/dynamic_update_slice | solution.py:403
  38.7 2.5 %collective-permute-done.11 = bf16[2,8,2,16,128]{4,3,2,1,0:T(8,128)(2,1)S(1)} collective-permute-done((bf16[2,8,2,16,128]{4,3,2,1,0:T(8,128)(2,1)S(1)}, bf16[2,8,2,16,128]{4,3,2,1,0:T(8,128)(2,1)S(1)}, u32[]{:S(2)}, u32[]{:S(2)}) %collective-permute-start.11) | collective-permute-done | bytes 131104 | tf_op jit(solution)/shard_map/ppermute | solution.py:338
  41.1 6.9 %collective-permute-done.12 = bf16[2,8,2,16,128]{4,3,2,1,0:T(8,128)(2,1)S(1)} collective-permute-done((bf16[2,8,2,16,128]{4,3,2,1,0:T(8,128)(2,1)S(1)}, bf16[2,8,2,16,128]{4,3,2,1,0:T(8,128)(2,1)S(1)}, u32[]{:S(2)}, u32[]{:S(2)}) %collective-permute-start.12) | collective-permute-done | bytes 131104 | tf_op jit(solution)/shard_map/ppermute | solution.py:338
  48.0 0.1 convert_add_fusion.1
  48.1 0.6 collective-permute-start.14
  48.7 0.1 fusion
  48.9 2.4 %collective-permute-start.19 = (bf16[2,16,16,128]{3,2,1,0:T(8,128)(2,1)S(1)}, bf16[2,16,16,128]{3,2,1,0:T(8,128)(2,1)S(1)}, u32[]{:S(2)}, u32[]{:S(2)}) collective-permute-start(bf16[2,16,16,128]{3,2,1,0:T(8,128)(2,1)S(1)} %get-tuple-element.43), channel_id=1, source_target_pairs={{0,2},{1,3},{2,0},{3,1},{4,6},{5,7},{6,4},{7,5},{8,10},{9,11},{10,... | collective-permute-start | bytes 393224 | tf_op jit(solution)/shard_map/ppermute | solution.py:338
  51.3 1.1 %collective-permute-start.20 = (bf16[2,16,16,128]{3,2,1,0:T(8,128)(2,1)S(1)}, bf16[2,16,16,128]{3,2,1,0:T(8,128)(2,1)S(1)}, u32[]{:S(2)}, u32[]{:S(2)}) collective-permute-start(bf16[2,16,16,128]{3,2,1,0:T(8,128)(2,1)S(1)} %get-tuple-element.45), channel_id=1, source_target_pairs={{0,4},{1,5},{2,6},{3,7},{4,0},{5,1},{6,2},{7,3},{8,12},{9,13},{10,... | collective-permute-start | bytes 393224 | tf_op jit(solution)/shard_map/ppermute | solution.py:338
  52.4 1.4 %collective-permute-start.21 = (bf16[2,16,16,128]{3,2,1,0:T(8,128)(2,1)S(1)}, bf16[2,16,16,128]{3,2,1,0:T(8,128)(2,1)S(1)}, u32[]{:S(2)}, u32[]{:S(2)}) collective-permute-start(bf16[2,16,16,128]{3,2,1,0:T(8,128)(2,1)S(1)} %get-tuple-element.44), channel_id=1, source_target_pairs={{0,6},{1,7},{2,4},{3,5},{4,2},{5,3},{6,0},{7,1},{8,14},{9,15},{10,... | collective-permute-start | bytes 393224 | tf_op jit(solution)/shard_map/ppermute | solution.py:338
  53.9 1.7 %collective-permute-done.19 = bf16[2,16,16,128]{3,2,1,0:T(8,128)(2,1)S(1)} collective-permute-done((bf16[2,16,16,128]{3,2,1,0:T(8,128)(2,1)S(1)}, bf16[2,16,16,128]{3,2,1,0:T(8,128)(2,1)S(1)}, u32[]{:S(2)}, u32[]{:S(2)}) %collective-permute-start.19) | collective-permute-done | bytes 131104 | tf_op jit(solution)/shard_map/ppermute | solution.py:338
  55.6 7.6 %collective-permute-done.20 = bf16[2,16,16,128]{3,2,1,0:T(8,128)(2,1)S(1)} collective-permute-done((bf16[2,16,16,128]{3,2,1,0:T(8,128)(2,1)S(1)}, bf16[2,16,16,128]{3,2,1,0:T(8,128)(2,1)S(1)}, u32[]{:S(2)}, u32[]{:S(2)}) %collective-permute-start.20) | collective-permute-done | bytes 131104 | tf_op jit(solution)/shard_map/ppermute | solution.py:338
  63.2 0.1 fusion.2
  63.3 0.0 copy-start
  63.3 0.0 copy-start.1
  63.4 0.7 %copy-done = f32[32,16,128]{2,1,0:T(8,128)} copy-done((f32[32,16,128]{2,1,0:T(8,128)}, f32[32,16,128]{2,1,0:T(8,128)S(1)}, u32[]{:S(2)}) %copy-start) | copy-done | bytes 262168
  64.0 0.1 copy-done.1
  (21 shorter events, 0.3 us)
Async XLA Ops:
  2.7 9.3 %collective-permute-start.5 = (bf16[2,2,16,16,128]{4,3,2,1,0:T(8,128)(2,1)S(1)}, bf16[2,2,16,16,128]{4,3,2,1,0:T(8,128)(2,1)S(1)}, u32[]{:S(2)}, u32[]{:S(2)}) collective-permute-start(bf16[2,2,16,16,128]{4,3,2,1,0:T(8,128)(2,1)S(1)} %get-tuple-element.27), channel_id=1, source_target_pairs={{0,16},{8,24},{16,0},{24,8},{1,17},{9,25},{17,1},{25,9},{2,18},{10... | collective-permute-start | bytes 786440 | tf_op jit(solution)/shard_map/ppermute | solution.py:322
  5.8 8.4 %collective-permute-start.4 = (bf16[2,16,16,128]{3,2,1,0:T(8,128)(2,1)S(1)}, bf16[2,16,16,128]{3,2,1,0:T(8,128)(2,1)S(1)}, u32[]{:S(2)}, u32[]{:S(2)}) collective-permute-start(bf16[2,16,16,128]{3,2,1,0:T(8,128)(2,1)S(1)} %get-tuple-element.26), channel_id=1, source_target_pairs={{0,8},{8,0},{16,24},{24,16},{1,9},{9,1},{17,25},{25,17},{2,10},{10... | collective-permute-start | bytes 393224 | tf_op jit(solution)/shard_map/ppermute | solution.py:322
  5.8 15.0 %collective-permute-start.3 = (bf16[2,8,128,128]{3,2,1,0:T(8,128)(2,1)S(1)}, bf16[2,8,128,128]{3,2,1,0:T(8,128)(2,1)S(1)}, u32[]{:S(2)}, u32[]{:S(2)}) collective-permute-start(bf16[2,8,128,128]{3,2,1,0:T(8,128)(2,1)S(1)} %get-tuple-element.25), channel_id=1, source_target_pairs={{0,1},{1,0},{2,3},{3,2},{4,5},{5,4},{6,7},{7,6},{8,9},{9,8},{10,11... | collective-permute-start | bytes 1572872 | tf_op jit(solution)/shard_map/ppermute | solution.py:361
  12.1 2.0 %collective-permute-start.6 = (bf16[2,16,16,128]{3,2,1,0:T(8,128)(2,1)S(1)}, bf16[2,16,16,128]{3,2,1,0:T(8,128)(2,1)S(1)}, u32[]{:S(2)}, u32[]{:S(2)}) collective-permute-start(bf16[2,16,16,128]{3,2,1,0:T(8,128)(2,1)S(1)} %slice_bitcast_fusion.3), channel_id=1, source_target_pairs={{0,8},{8,0},{16,24},{24,16},{1,9},{9,1},{17,25},{25,17},{2,10},{10... | collective-permute-start | bytes 393224 | tf_op jit(solution)/shard_map/ppermute | solution.py:322
  12.2 7.2 %collective-permute-start.1 = (bf16[2,2,8,16,128]{4,3,2,1,0:T(8,128)(2,1)S(1)}, bf16[2,2,8,16,128]{4,3,2,1,0:T(8,128)(2,1)S(1)}, u32[]{:S(2)}, u32[]{:S(2)}) collective-permute-start(bf16[2,2,8,16,128]{4,3,2,1,0:T(8,128)(2,1)S(1)} %get-tuple-element.24), channel_id=1, source_target_pairs={{0,16},{8,24},{16,0},{24,8},{1,17},{9,25},{17,1},{25,9},{2,18},{10... | collective-permute-start | bytes 393224 | tf_op jit(solution)/shard_map/ppermute | solution.py:322
  14.0 6.0 %collective-permute-start = (bf16[2,8,16,128]{3,2,1,0:T(8,128)(2,1)S(1)}, bf16[2,8,16,128]{3,2,1,0:T(8,128)(2,1)S(1)}, u32[]{:S(2)}, u32[]{:S(2)}) collective-permute-start(bf16[2,8,16,128]{3,2,1,0:T(8,128)(2,1)S(1)} %get-tuple-element.23), channel_id=1, source_target_pairs={{0,8},{8,0},{16,24},{24,16},{1,9},{9,1},{17,25},{25,17},{2,10},{10... | collective-permute-start | bytes 196616 | tf_op jit(solution)/shard_map/ppermute | solution.py:322
  18.3 8.6 %collective-permute-start.16 = (bf16[2,2,16,16,128]{4,3,2,1,0:T(8,128)(2,1)S(1)}, bf16[2,2,16,16,128]{4,3,2,1,0:T(8,128)(2,1)S(1)}, u32[]{:S(2)}, u32[]{:S(2)}) collective-permute-start(bf16[2,2,16,16,128]{4,3,2,1,0:T(8,128)(2,1)S(1)} %get-tuple-element.40), channel_id=1, source_target_pairs={{0,16},{8,24},{16,0},{24,8},{1,17},{9,25},{17,1},{25,9},{2,18},{10... | collective-permute-start | bytes 786440 | tf_op jit(solution)/shard_map/ppermute | solution.py:322
  19.4 1.3 %collective-permute-start.2 = (bf16[2,8,16,128]{3,2,1,0:T(8,128)(2,1)S(1)}, bf16[2,8,16,128]{3,2,1,0:T(8,128)(2,1)S(1)}, u32[]{:S(2)}, u32[]{:S(2)}) collective-permute-start(bf16[2,8,16,128]{3,2,1,0:T(8,128)(2,1)S(1)} %slice_bitcast_fusion.5), channel_id=1, source_target_pairs={{0,8},{8,0},{16,24},{24,16},{1,9},{9,1},{17,25},{25,17},{2,10},{10... | collective-permute-start | bytes 196616 | tf_op jit(solution)/shard_map/ppermute | solution.py:322
  19.5 10.2 %collective-permute-start.15 = (bf16[2,16,16,128]{3,2,1,0:T(8,128)(2,1)S(1)}, bf16[2,16,16,128]{3,2,1,0:T(8,128)(2,1)S(1)}, u32[]{:S(2)}, u32[]{:S(2)}) collective-permute-start(bf16[2,16,16,128]{3,2,1,0:T(8,128)(2,1)S(1)} %get-tuple-element.39), channel_id=1, source_target_pairs={{0,8},{8,0},{16,24},{24,16},{1,9},{9,1},{17,25},{25,17},{2,10},{10... | collective-permute-start | bytes 393224 | tf_op jit(solution)/shard_map/ppermute | solution.py:322
  24.1 5.6 %collective-permute-start.9 = (bf16[2,2,8,16,128]{4,3,2,1,0:T(8,128)(2,1)S(1)}, bf16[2,2,8,16,128]{4,3,2,1,0:T(8,128)(2,1)S(1)}, u32[]{:S(2)}, u32[]{:S(2)}) collective-permute-start(bf16[2,2,8,16,128]{4,3,2,1,0:T(8,128)(2,1)S(1)} %get-tuple-element.33), channel_id=1, source_target_pairs={{0,16},{8,24},{16,0},{24,8},{1,17},{9,25},{17,1},{25,9},{2,18},{10... | collective-permute-start | bytes 393224 | tf_op jit(solution)/shard_map/ppermute | solution.py:322
  25.0 7.6 %collective-permute-start.8 = (bf16[2,8,16,128]{3,2,1,0:T(8,128)(2,1)S(1)}, bf16[2,8,16,128]{3,2,1,0:T(8,128)(2,1)S(1)}, u32[]{:S(2)}, u32[]{:S(2)}) collective-permute-start(bf16[2,8,16,128]{3,2,1,0:T(8,128)(2,1)S(1)} %get-tuple-element.32), channel_id=1, source_target_pairs={{0,8},{8,0},{16,24},{24,16},{1,9},{9,1},{17,25},{25,17},{2,10},{10... | collective-permute-start | bytes 196616 | tf_op jit(solution)/shard_map/ppermute | solution.py:322
  25.0 12.9 %collective-permute-start.7 = (bf16[8,128,128]{2,1,0:T(8,128)(2,1)S(1)}, bf16[8,128,128]{2,1,0:T(8,128)(2,1)S(1)}, u32[]{:S(2)}, u32[]{:S(2)}) collective-permute-start(bf16[8,128,128]{2,1,0:T(8,128)(2,1)S(1)} %get-tuple-element.30), channel_id=1, source_target_pairs={{0,1},{1,0},{2,3},{3,2},{4,5},{5,4},{6,7},{7,6},{8,9},{9,8},{10,11... | collective-permute-start | bytes 786440 | tf_op jit(solution)/shard_map/ppermute | solution.py:361
  26.9 2.8 %collective-permute-start.17 = (bf16[2,16,16,128]{3,2,1,0:T(8,128)(2,1)S(1)}, bf16[2,16,16,128]{3,2,1,0:T(8,128)(2,1)S(1)}, u32[]{:S(2)}, u32[]{:S(2)}) collective-permute-start(bf16[2,16,16,128]{3,2,1,0:T(8,128)(2,1)S(1)} %slice_bitcast_fusion.2), channel_id=1, source_target_pairs={{0,8},{8,0},{16,24},{24,16},{1,9},{9,1},{17,25},{25,17},{2,10},{10... | collective-permute-start | bytes 393224 | tf_op jit(solution)/shard_map/ppermute | solution.py:322
  29.7 2.9 %collective-permute-start.10 = (bf16[2,8,16,128]{3,2,1,0:T(8,128)(2,1)S(1)}, bf16[2,8,16,128]{3,2,1,0:T(8,128)(2,1)S(1)}, u32[]{:S(2)}, u32[]{:S(2)}) collective-permute-start(bf16[2,8,16,128]{3,2,1,0:T(8,128)(2,1)S(1)} %slice_bitcast_fusion.4), channel_id=1, source_target_pairs={{0,8},{8,0},{16,24},{24,16},{1,9},{9,1},{17,25},{25,17},{2,10},{10... | collective-permute-start | bytes 196616 | tf_op jit(solution)/shard_map/ppermute | solution.py:322
  31.0 17.7 %collective-permute-start.18 = (bf16[2,16,2,2,16,128]{5,4,1,0,3,2:T(8,128)(2,1)S(1)}, bf16[2,16,2,2,16,128]{5,4,1,0,3,2:T(8,128)(2,1)S(1)}, u32[]{:S(2)}, u32[]{:S(2)}) collective-permute-start(bf16[2,16,2,2,16,128]{5,4,1,0,3,2:T(8,128)(2,1)S(1)} %copy.11), channel_id=1, source_target_pairs={{0,1},{1,0},{2,3},{3,2},{4,5},{5,4},{6,7},{7,6},{8,9},{9,8},{10,11... | collective-permute-start | bytes 1572872 | tf_op jit(solution)/shard_map/ppermute | solution.py:338
  33.5 7.7 %collective-permute-start.11 = (bf16[2,8,2,16,128]{4,3,2,1,0:T(8,128)(2,1)S(1)}, bf16[2,8,2,16,128]{4,3,2,1,0:T(8,128)(2,1)S(1)}, u32[]{:S(2)}, u32[]{:S(2)}) collective-permute-start(bf16[2,8,2,16,128]{4,3,2,1,0:T(8,128)(2,1)S(1)} %get-tuple-element.35), channel_id=1, source_target_pairs={{0,2},{1,3},{2,0},{3,1},{4,6},{5,7},{6,4},{7,5},{8,10},{9,11},{10,... | collective-permute-start | bytes 393224 | tf_op jit(solution)/shard_map/ppermute | solution.py:338
  35.1 12.9 %collective-permute-start.12 = (bf16[2,8,2,16,128]{4,3,2,1,0:T(8,128)(2,1)S(1)}, bf16[2,8,2,16,128]{4,3,2,1,0:T(8,128)(2,1)S(1)}, u32[]{:S(2)}, u32[]{:S(2)}) collective-permute-start(bf16[2,8,2,16,128]{4,3,2,1,0:T(8,128)(2,1)S(1)} %get-tuple-element.36), channel_id=1, source_target_pairs={{0,4},{1,5},{2,6},{3,7},{4,0},{5,1},{6,2},{7,3},{8,12},{9,13},{10,... | collective-permute-start | bytes 393224 | tf_op jit(solution)/shard_map/ppermute | solution.py:338
  37.7 10.3 %collective-permute-start.13 = (bf16[2,8,2,16,128]{4,3,2,1,0:T(8,128)(2,1)S(1)}, bf16[2,8,2,16,128]{4,3,2,1,0:T(8,128)(2,1)S(1)}, u32[]{:S(2)}, u32[]{:S(2)}) collective-permute-start(bf16[2,8,2,16,128]{4,3,2,1,0:T(8,128)(2,1)S(1)} %get-tuple-element.37), channel_id=1, source_target_pairs={{0,6},{1,7},{2,4},{3,5},{4,2},{5,3},{6,0},{7,1},{8,14},{9,15},{10,... | collective-permute-start | bytes 393224 | tf_op jit(solution)/shard_map/ppermute | solution.py:338
  48.1 5.7 %collective-permute-start.14 = (bf16[2,8,16,128]{3,2,1,0:T(8,128)(2,1)S(1)}, bf16[2,8,16,128]{3,2,1,0:T(8,128)(2,1)S(1)}, u32[]{:S(2)}, u32[]{:S(2)}) collective-permute-start(bf16[2,8,16,128]{3,2,1,0:T(8,128)(2,1)S(1)} %fusion.8), channel_id=1, source_target_pairs={{0,1},{1,0},{2,3},{3,2},{4,5},{5,4},{6,7},{7,6},{8,9},{9,8},{10,11... | collective-permute-start | bytes 196616 | tf_op jit(solution)/shard_map/ppermute | solution.py:361
  48.9 6.7 %collective-permute-start.19 = (bf16[2,16,16,128]{3,2,1,0:T(8,128)(2,1)S(1)}, bf16[2,16,16,128]{3,2,1,0:T(8,128)(2,1)S(1)}, u32[]{:S(2)}, u32[]{:S(2)}) collective-permute-start(bf16[2,16,16,128]{3,2,1,0:T(8,128)(2,1)S(1)} %get-tuple-element.43), channel_id=1, source_target_pairs={{0,2},{1,3},{2,0},{3,1},{4,6},{5,7},{6,4},{7,5},{8,10},{9,11},{10,... | collective-permute-start | bytes 393224 | tf_op jit(solution)/shard_map/ppermute | solution.py:338
  51.3 11.9 %collective-permute-start.20 = (bf16[2,16,16,128]{3,2,1,0:T(8,128)(2,1)S(1)}, bf16[2,16,16,128]{3,2,1,0:T(8,128)(2,1)S(1)}, u32[]{:S(2)}, u32[]{:S(2)}) collective-permute-start(bf16[2,16,16,128]{3,2,1,0:T(8,128)(2,1)S(1)} %get-tuple-element.45), channel_id=1, source_target_pairs={{0,4},{1,5},{2,6},{3,7},{4,0},{5,1},{6,2},{7,3},{8,12},{9,13},{10,... | collective-permute-start | bytes 393224 | tf_op jit(solution)/shard_map/ppermute | solution.py:338
  52.4 10.8 %collective-permute-start.21 = (bf16[2,16,16,128]{3,2,1,0:T(8,128)(2,1)S(1)}, bf16[2,16,16,128]{3,2,1,0:T(8,128)(2,1)S(1)}, u32[]{:S(2)}, u32[]{:S(2)}) collective-permute-start(bf16[2,16,16,128]{3,2,1,0:T(8,128)(2,1)S(1)} %get-tuple-element.44), channel_id=1, source_target_pairs={{0,6},{1,7},{2,4},{3,5},{4,2},{5,3},{6,0},{7,1},{8,14},{9,15},{10,... | collective-permute-start | bytes 393224 | tf_op jit(solution)/shard_map/ppermute | solution.py:338
  63.3 0.7 %copy-start = (f32[32,16,128]{2,1,0:T(8,128)}, f32[32,16,128]{2,1,0:T(8,128)S(1)}, u32[]{:S(2)}) copy-start(f32[32,16,128]{2,1,0:T(8,128)S(1)} %get-tuple-element.49) | copy-start | bytes 786436
  63.3 0.8 %copy-start.1 = (f32[32,16,128]{2,1,0:T(8,128)}, f32[32,16,128]{2,1,0:T(8,128)S(1)}, u32[]{:S(2)}) copy-start(f32[32,16,128]{2,1,0:T(8,128)S(1)} %get-tuple-element.48) | copy-start | bytes 786436

commit v3 on v2

--- a/solution.py
+++ b/solution.py
@@ -17,7 +17,7 @@
 
 
 def far_masks(groups):
-    return [1] + [mask for even in range(2, groups, 2) for mask in (even, even ^ 1)]
+    return list(range(1, groups))
 
 
 def pick_kernel(cuts, groups, routes, query, grad, keys, values, *rest):
@@ -40,8 +40,7 @@
                     )
                 )
         for index, mask in enumerate(far_masks(groups)):
-            out = outs[(index + 1) // 2]
-            out = out if index == 0 else out.at[(index + 1) % 2]
+            out = outs[index]
             start = pl.multiple_of(routes[group ^ mask, group] * KB, KB)
             for side, rows in enumerate((keys, values)):
                 copies.append(
@@ -51,7 +50,7 @@
                         arrived.at[number, index, side],
                     )
                 )
-        outs = outs[groups // 2 :]
+        outs = outs[groups - 1 :]
     for copy in copies:
         copy.start()
     for copy in copies:
@@ -65,8 +64,8 @@
         heads = heads // 2 if paired else heads
         block = (2, heads, KB, head_dim)
         swap = [(2, heads, tokens, head_dim)] if paired else []
-        shapes += swap + [block] + [(2,) + block] * (groups // 2 - 1)
-        counts.append(len(swap) + groups // 2)
+        shapes += swap + [block] * (groups - 1)
+        counts.append(len(swap) + groups - 1)
     outs = pl.pallas_call(
         functools.partial(pick_kernel, cuts, groups),
         out_shape=[jax.ShapeDtypeStruct(shape, jnp.bfloat16) for shape in shapes],
@@ -85,11 +84,10 @@
 
 
 def slot_specs(groups, step_heads, rows, head_dim):
-    flat = pl.BlockSpec((2, step_heads) + rows + (head_dim,), lambda i, *_: (0, i) + (0,) * (len(rows) + 1))
-    half = pl.BlockSpec(
-        (None, 2, step_heads) + rows + (head_dim,), lambda i, *_: (0, 0, i) + (0,) * (len(rows) + 1)
+    spec = pl.BlockSpec(
+        (2, step_heads) + rows + (head_dim,), lambda i, *_: (0, i) + (0,) * (len(rows) + 1)
     )
-    return [flat] + [half, flat] * (groups // 2 - 1)
+    return [spec] * (groups - 1)
 
 
 def attend_kernel(masks, has_alias, paired, _, query, grad, keys, values, *rest):
@@ -99,10 +97,9 @@
     rest = rest[slots + has_alias + paired :]
     if paired:
         other_out, rest = rest[0], rest[1:]
-    query_out, own_out, near_out = rest[:3]
-    pair_outs = rest[3 : 3 + slots // 2]
-    far_outs = [near_out] + [out.at[half] for out in pair_outs for half in range(2)]
-    score_ref, dweight_ref, half_ref, dscore_ref = rest[3 + slots // 2 :]
+    query_out, own_out = rest[:2]
+    far_outs = rest[2 : 2 + slots]
+    score_ref, dweight_ref, half_ref, dscore_ref = rest[2 + slots :]
     heads, tokens, head_dim = query.shape
     group_keys = keys.shape[1]
     group = lax.axis_index("blk")
@@ -197,11 +194,9 @@
     def pair(count):
         return pl.BlockSpec((2, step_heads, count, head_dim), lambda i, half: (0, i, 0, 0))
 
-    both = pl.BlockSpec((2, 2, step_heads, KB, head_dim), lambda i, half: (0, 0, i, 0, 0))
     block = (2, heads, KB, head_dim)
-    shapes = [query_shape, (2, heads, group_keys, head_dim), block]
-    shapes += [(2,) + block] * (groups // 2 - 1)
-    out_specs = [placed(tokens), pair(group_keys), pair(KB)] + [both] * (groups // 2 - 1)
+    shapes = [query_shape, (2, heads, group_keys, head_dim)] + [block] * len(masks)
+    out_specs = [placed(tokens), pair(group_keys)] + [pair(KB)] * len(masks)
     operands = [half, *rows, *far]
     in_specs = [placed(tokens)] * 2 + [placed(group_keys)] * 2
     in_specs += slot_specs(groups, step_heads, (KB,), head_dim)
@@ -317,15 +312,11 @@
         for first, parts, paired, order in PLAN
     ]
 
-    def exchange(near, pairs):
-        def hop(rows, mask):
-            return lax.ppermute(rows, "blk", [(g, g ^ mask) for g in range(groups)])
-
-        crossed = [hop(pair, 2 * i) for i, pair in enumerate(pairs, 1)]
-        slots = [hop(near, 1)]
-        for pair in crossed:
-            slots += [pair, hop(pair[1], 1)]
-        return slots
+    def exchange(parts):
+        came = []
+        for mask, part in zip(far_masks(groups), parts):
+            came.append(lax.ppermute(part, "blk", [(g, g ^ mask) for g in range(groups)]))
+        return came
 
     def scatter(pieces, stages):
         left = [bit for bit in bits]
@@ -378,13 +369,13 @@
     for swapped, parts in picked:
         if swapped is not None:
             swapped = trade(swapped)
-        fetched.append((swapped, exchange(parts[0], parts[1:])))
+        fetched.append((swapped, exchange(parts)))
     for number, cut in enumerate(cuts):
         swapped, far = fetched[number]
         other, query_out, own, parts = attend(
             half_operand, local_rows, far, swapped, groups, cut, query_rows.shape, query_out
         )
-        back = exchange(parts[0], parts[1:])
+        back = exchange(parts)
         if other is not None:
             others.append((cut, trade(other)))
         wanted = [bit for bit in bits if not (cut[2] and bit == 1)]

time: 64.4 us -> 69.5 us (1.079)
  waiting for transfers between devices: 27.2 us -> 31.5 us
  starting transfers between devices: 22.3 us -> 23.3 us
    ppermute x12, waiting for transfers between devices: 8.56 us -> 13.3 us  [exchange(): lax.ppermute(part, 'blk', [(g, g ^ mask) for g in range(groups)])]
    ppermute x12, starting transfers between devices: 7.74 us -> 9.5 us  [exchange(): lax.ppermute(part, 'blk', [(g, g ^ mask) for g in range(groups)])]
    ppermute x7, starting transfers between devices: 10.9 us -> 9.68 us  [scatter(): lax.ppermute(piece.reshape(shape), 'ulysses', [(r, r ^ mix) for r in rang...]
  transfers between devices with their start and end apart: 22 -> 22, of which waited for: 8 -> 9; matrix products, arithmetic and copies ran while one was open for 2% -> 2% of each run, Pallas kernels for 15% -> 14%
where the time goes in v3:
time: 69.5 us; the launch traced here: 69.2 us
  waiting for transfers between devices  31.5 us (45%)
  starting transfers between devices  23.3 us (34%)
  Pallas kernels  11.7 us (17%)
  local copies, waits for them, and re-layouts  1.66 us (2%)
  between operations  0.78 us (1%)
    ppermute x7, waiting for transfers between devices, scatter(): lax.ppermute(piece.reshape(shape), 'ulysses', [(r, r ^ mix) for r in rang...  18.2 us
    ppermute x12, waiting for transfers between devices, exchange(): lax.ppermute(part, 'blk', [(g, g ^ mask) for g in range(groups)])  13.3 us
    ppermute x7, starting transfers between devices, scatter(): lax.ppermute(piece.reshape(shape), 'ulysses', [(r, r ^ mix) for r in rang...  9.68 us
    ppermute x12, starting transfers between devices, exchange(): lax.ppermute(part, 'blk', [(g, g ^ mask) for g in range(groups)])  9.5 us
    pallas_call x2, Pallas kernels, attend(): pl.pallas_call(functools.partial(attend_kernel, masks, query_out is not N...  7.53 us
    ppermute x3, starting transfers between devices, trade(): return lax.ppermute(rows, 'ulysses', [(r, r ^ 1) for r in range(ranks)])  4.07 us
    pallas_call x2, Pallas kernels, merge(): pl.pallas_call(functools.partial(merge_kernel, masks, bits), out_shape=[j...  2.11 us
    pallas_call x1, Pallas kernels, pick(): pl.pallas_call(functools.partial(pick_kernel, cuts, groups), out_shape=[j...  2.11 us
  transfers between devices with their start and end apart: 22, of which 9 were waited for; matrix products, arithmetic and copies ran while one was open for 2% of the time, Pallas kernels for 14%

profile of v3, /device:TPU:0, one launch (start us, length us, event | category | flops | bytes accessed | tf_op | source)
XLA Modules:
  0.0 69.2 jit_solution(16695155391995611550)
XLA Ops:
  0.6 2.1 %pick.1 = (bf16[2,16,16,128]{3,2,1,0:T(8,128)(2,1)S(1)}, bf16[2,16,16,128]{3,2,1,0:T(8,128)(2,1)S(1)}, bf16[2,16,16,128]{3,2,1,0:T(8,128)(2,1)S(1)}, bf16[2,8,12...) custom-call(s32[4,4]{1,0:T(4,128)} %routes.5, ...), custom_call_target="tpu_custom_call" | custom-call | tf_op jit(solution)/shard_map/pick/pallas_call | solution.py:69
  2.7 3.1 %collective-permute-start.3 = (bf16[2,8,128,128]{3,2,1,0:T(8,128)(2,1)S(1)}, bf16[2,8,128,128]{3,2,1,0:T(8,128)(2,1)S(1)}, u32[]{:S(2)}, u32[]{:S(2)}) collective-permute-start(bf16[2,8,128,128]{3,2,1,0:T(8,128)(2,1)S(1)} %get-tuple-element.30), channel_id=1, source_target_pairs={{0,1},{1,0},{2,3},{3,2},{4,5},{5,4},{6,7},{7,6},{8,9},{9,8},{10,11... | collective-permute-start | bytes 1572872 | tf_op jit(solution)/shard_map/ppermute | solution.py:352
  5.8 0.0 collective-permute-start.4
  5.8 1.5 %collective-permute-start.5 = (bf16[2,16,16,128]{3,2,1,0:T(8,128)(2,1)S(1)}, bf16[2,16,16,128]{3,2,1,0:T(8,128)(2,1)S(1)}, u32[]{:S(2)}, u32[]{:S(2)}) collective-permute-start(bf16[2,16,16,128]{3,2,1,0:T(8,128)(2,1)S(1)} %get-tuple-element.32), channel_id=1, source_target_pairs={{0,16},{8,24},{16,0},{24,8},{1,17},{9,25},{17,1},{25,9},{2,18},{10... | collective-permute-start | bytes 393224 | tf_op jit(solution)/shard_map/ppermute | solution.py:318
  7.3 0.4 collective-permute-start.6
  7.7 0.3 collective-permute-start
  8.0 1.5 %collective-permute-start.1 = (bf16[2,8,16,128]{3,2,1,0:T(8,128)(2,1)S(1)}, bf16[2,8,16,128]{3,2,1,0:T(8,128)(2,1)S(1)}, u32[]{:S(2)}, u32[]{:S(2)}) collective-permute-start(bf16[2,8,16,128]{3,2,1,0:T(8,128)(2,1)S(1)} %get-tuple-element.28), channel_id=1, source_target_pairs={{0,16},{8,24},{16,0},{24,8},{1,17},{9,25},{17,1},{25,9},{2,18},{10... | collective-permute-start | bytes 196616 | tf_op jit(solution)/shard_map/ppermute | solution.py:318
  9.4 2.7 %collective-permute-done.5.rest_1_ = bf16[2,16,16,128]{3,2,1,0:T(8,128)(2,1)S(1)} collective-permute-done((bf16[2,16,16,128]{3,2,1,0:T(8,128)(2,1)S(1)}, bf16[2,16,16,128]{3,2,1,0:T(8,128)(2,1)S(1)}, u32[]{:S(2)}, u32[]{:S(2)}) %collective-permute-start.5) | collective-permute-done | bytes 131104 | tf_op jit(solution)/shard_map/ppermute | solution.py:318
  12.2 1.9 %collective-permute-done.6.rest_2_ = bf16[2,16,16,128]{3,2,1,0:T(8,128)(2,1)S(1)} collective-permute-done((bf16[2,16,16,128]{3,2,1,0:T(8,128)(2,1)S(1)}, bf16[2,16,16,128]{3,2,1,0:T(8,128)(2,1)S(1)}, u32[]{:S(2)}, u32[]{:S(2)}) %collective-permute-start.6) | collective-permute-done | bytes 131104 | tf_op jit(solution)/shard_map/ppermute | solution.py:318
  14.1 4.1 %attend.2 = (bf16[32,128,128]{2,1,0:T(8,128)(2,1)}, bf16[2,16,128,128]{3,2,1,0:T(8,128)(2,1)S(1)}, bf16[2,16,16,128]{3,2,1,0:T(8,128)(2,1)S(1)}, bf16[2,16,16,12...) custom-call(s32[1]{0:T(128)} %bitcast._, bf16[32,128,128]{2,1,0:T(8,128)(2,1)} %query.5, bf16[32,128,128]{2,1,0:T(8,128)(2,1)} %grad.5, ...), custom_call_target="tpu_custom_call" | custom-call | tf_op jit(solution)/shard_map/attend/pallas_call | solution.py:216
  18.2 1.5 %collective-permute-start.16 = (bf16[2,16,16,128]{3,2,1,0:T(8,128)(2,1)S(1)}, bf16[2,16,16,128]{3,2,1,0:T(8,128)(2,1)S(1)}, u32[]{:S(2)}, u32[]{:S(2)}) collective-permute-start(bf16[2,16,16,128]{3,2,1,0:T(8,128)(2,1)S(1)} %get-tuple-element.47), channel_id=1, source_target_pairs={{0,16},{8,24},{16,0},{24,8},{1,17},{9,25},{17,1},{25,9},{2,18},{10... | collective-permute-start | bytes 393224 | tf_op jit(solution)/shard_map/ppermute | solution.py:318
  19.7 0.9 %collective-permute-start.17 = (bf16[2,16,16,128]{3,2,1,0:T(8,128)(2,1)S(1)}, bf16[2,16,16,128]{3,2,1,0:T(8,128)(2,1)S(1)}, u32[]{:S(2)}, u32[]{:S(2)}) collective-permute-start(bf16[2,16,16,128]{3,2,1,0:T(8,128)(2,1)S(1)} %get-tuple-element.48), channel_id=1, source_target_pairs={{0,24},{8,16},{16,8},{24,0},{1,25},{9,17},{17,9},{25,1},{2,26},{10... | collective-permute-start | bytes 393224 | tf_op jit(solution)/shard_map/ppermute | solution.py:318
  20.6 0.0 collective-permute-done.rest_0_
  20.6 0.0 collective-permute-start.15
  20.6 0.0 collective-permute-done.1.rest_1_
  20.6 1.6 %collective-permute-start.2 = (bf16[2,8,16,128]{3,2,1,0:T(8,128)(2,1)S(1)}, bf16[2,8,16,128]{3,2,1,0:T(8,128)(2,1)S(1)}, u32[]{:S(2)}, u32[]{:S(2)}) collective-permute-start(bf16[2,8,16,128]{3,2,1,0:T(8,128)(2,1)S(1)} %get-tuple-element.29), channel_id=1, source_target_pairs={{0,24},{8,16},{16,8},{24,0},{1,25},{9,17},{17,9},{25,1},{2,26},{10... | collective-permute-start | bytes 196616 | tf_op jit(solution)/shard_map/ppermute | solution.py:318
  22.2 6.6 %collective-permute-done.2.rest_2_ = bf16[2,8,16,128]{3,2,1,0:T(8,128)(2,1)S(1)} collective-permute-done((bf16[2,8,16,128]{3,2,1,0:T(8,128)(2,1)S(1)}, bf16[2,8,16,128]{3,2,1,0:T(8,128)(2,1)S(1)}, u32[]{:S(2)}, u32[]{:S(2)}) %collective-permute-start.2) | collective-permute-done | bytes 65568 | tf_op jit(solution)/shard_map/ppermute | solution.py:318
  28.8 3.4 %attend.3 = (bf16[8,128,128]{2,1,0:T(8,128)(2,1)S(1)}, bf16[32,128,128]{2,1,0:T(8,128)(2,1)}, bf16[2,8,128,128]{3,2,1,0:T(8,128)(2,1)S(1)}, bf16[2,8,16,128]{3,2...) custom-call(s32[1]{0:T(128)} %bitcast._, ...), custom_call_target="tpu_custom_call", output_to_operand_aliasing={{1}: (9, {})} | custom-call | tf_op jit(solution)/shard_map/attend/pallas_call | solution.py:216
  32.2 0.0 collective-permute-start.8
  32.2 1.5 %collective-permute-start.9 = (bf16[2,8,16,128]{3,2,1,0:T(8,128)(2,1)S(1)}, bf16[2,8,16,128]{3,2,1,0:T(8,128)(2,1)S(1)}, u32[]{:S(2)}, u32[]{:S(2)}) collective-permute-start(bf16[2,8,16,128]{3,2,1,0:T(8,128)(2,1)S(1)} %get-tuple-element.39), channel_id=1, source_target_pairs={{0,16},{8,24},{16,0},{24,8},{1,17},{9,25},{17,1},{25,9},{2,18},{10... | collective-permute-start | bytes 196616 | tf_op jit(solution)/shard_map/ppermute | solution.py:318
  33.7 0.0 collective-permute-done.16
  33.7 0.3 collective-permute-start.10
  34.1 1.3 %merge.3 = (bf16[2,16,4,16,128]{4,3,2,1,0:T(8,128)(2,1)S(1)}, bf16[2,16,4,16,128]{4,3,2,1,0:T(8,128)(2,1)S(1)}) custom-call(s32[4,4]{1,0:T(4,128)} %routes.5, bf16[2,16,8,16,128]{4,3,2,1,0:T(8,128)(2,1)S(1)} %bitcast.38, bf16[2,16,1,16,128]{4,3,2,1,0:T(8,128)(2,1)S(1)} %bitcast.44, bf16[2,16,1,16,128]{4,3,2,1,0:T(8,128)(2,1)S(1)} %bitcast.42, ...), custom_call_target="tpu_custom_call" | custom-call | tf_op jit(solution)/shard_map/merge/pallas_call | solution.py:277
  35.4 0.3 collective-permute-start.18
  35.7 1.0 %collective-permute-done.9 = bf16[2,8,16,128]{3,2,1,0:T(8,128)(2,1)S(1)} collective-permute-done((bf16[2,8,16,128]{3,2,1,0:T(8,128)(2,1)S(1)}, bf16[2,8,16,128]{3,2,1,0:T(8,128)(2,1)S(1)}, u32[]{:S(2)}, u32[]{:S(2)}) %collective-permute-start.9) | collective-permute-done | bytes 65568 | tf_op jit(solution)/shard_map/ppermute | solution.py:318
  36.7 1.1 %collective-permute-done.10 = bf16[2,8,16,128]{3,2,1,0:T(8,128)(2,1)S(1)} collective-permute-done((bf16[2,8,16,128]{3,2,1,0:T(8,128)(2,1)S(1)}, bf16[2,8,16,128]{3,2,1,0:T(8,128)(2,1)S(1)}, u32[]{:S(2)}, u32[]{:S(2)}) %collective-permute-start.10) | collective-permute-done | bytes 65568 | tf_op jit(solution)/shard_map/ppermute | solution.py:318
  37.8 0.9 %merge.2 = (bf16[2,8,2,16,128]{4,3,2,1,0:T(8,128)(2,1)S(1)}, bf16[2,8,2,16,128]{4,3,2,1,0:T(8,128)(2,1)S(1)}, bf16[2,8,2,16,128]{4,3,2,1,0:T(8,128)(2,1)S(1)}, bf16[2,8,2,16,128]{4,3,2,1,0:T(8,128)(2,1)S(1)}) custom-call(s32[4,4]{1,0:T(4,128)} %routes.5, bf16[2,8,8,16,128]{4,3,2,1,0:T(8,128)(2,1)S(1)} %bitcast.40, bf16[2,8,1,16,128]{4,3,2,1,0:T(8,128)(2,1)S(1)} %bitcast.45, ...), custom_call_target="tpu_custom_call" | custom-call | tf_op jit(solution)/shard_map/merge/pallas_call | solution.py:277
  38.6 1.6 %collective-permute-start.11 = (bf16[2,8,2,16,128]{4,3,2,1,0:T(8,128)(2,1)S(1)}, bf16[2,8,2,16,128]{4,3,2,1,0:T(8,128)(2,1)S(1)}, u32[]{:S(2)}, u32[]{:S(2)}) collective-permute-start(bf16[2,8,2,16,128]{4,3,2,1,0:T(8,128)(2,1)S(1)} %get-tuple-element.42), channel_id=1, source_target_pairs={{0,2},{1,3},{2,0},{3,1},{4,6},{5,7},{6,4},{7,5},{8,10},{9,11},{10,... | collective-permute-start | bytes 393224 | tf_op jit(solution)/shard_map/ppermute | solution.py:329
  40.2 2.6 %collective-permute-start.12 = (bf16[2,8,2,16,128]{4,3,2,1,0:T(8,128)(2,1)S(1)}, bf16[2,8,2,16,128]{4,3,2,1,0:T(8,128)(2,1)S(1)}, u32[]{:S(2)}, u32[]{:S(2)}) collective-permute-start(bf16[2,8,2,16,128]{4,3,2,1,0:T(8,128)(2,1)S(1)} %get-tuple-element.43), channel_id=1, source_target_pairs={{0,4},{1,5},{2,6},{3,7},{4,0},{5,1},{6,2},{7,3},{8,12},{9,13},{10,... | collective-permute-start | bytes 393224 | tf_op jit(solution)/shard_map/ppermute | solution.py:329
  42.8 0.3 collective-permute-start.13
  43.1 0.5 collective-permute-start.7
  43.6 2.7 %collective-permute-done.11 = bf16[2,8,2,16,128]{4,3,2,1,0:T(8,128)(2,1)S(1)} collective-permute-done((bf16[2,8,2,16,128]{4,3,2,1,0:T(8,128)(2,1)S(1)}, bf16[2,8,2,16,128]{4,3,2,1,0:T(8,128)(2,1)S(1)}, u32[]{:S(2)}, u32[]{:S(2)}) %collective-permute-start.11) | collective-permute-done | bytes 131104 | tf_op jit(solution)/shard_map/ppermute | solution.py:329
  46.3 6.8 %collective-permute-done.12 = bf16[2,8,2,16,128]{4,3,2,1,0:T(8,128)(2,1)S(1)} collective-permute-done((bf16[2,8,2,16,128]{4,3,2,1,0:T(8,128)(2,1)S(1)}, bf16[2,8,2,16,128]{4,3,2,1,0:T(8,128)(2,1)S(1)}, u32[]{:S(2)}, u32[]{:S(2)}) %collective-permute-start.12) | collective-permute-done | bytes 131104 | tf_op jit(solution)/shard_map/ppermute | solution.py:329
  53.1 0.1 convert_add_fusion.1
  53.2 0.5 collective-permute-start.14
  53.8 0.1 fusion
  54.0 2.4 %collective-permute-start.19 = (bf16[2,16,16,128]{3,2,1,0:T(8,128)(2,1)S(1)}, bf16[2,16,16,128]{3,2,1,0:T(8,128)(2,1)S(1)}, u32[]{:S(2)}, u32[]{:S(2)}) collective-permute-start(bf16[2,16,16,128]{3,2,1,0:T(8,128)(2,1)S(1)} %get-tuple-element.51), channel_id=1, source_target_pairs={{0,2},{1,3},{2,0},{3,1},{4,6},{5,7},{6,4},{7,5},{8,10},{9,11},{10,... | collective-permute-start | bytes 393224 | tf_op jit(solution)/shard_map/ppermute | solution.py:329
  56.4 1.1 %collective-permute-start.20 = (bf16[2,16,16,128]{3,2,1,0:T(8,128)(2,1)S(1)}, bf16[2,16,16,128]{3,2,1,0:T(8,128)(2,1)S(1)}, u32[]{:S(2)}, u32[]{:S(2)}) collective-permute-start(bf16[2,16,16,128]{3,2,1,0:T(8,128)(2,1)S(1)} %get-tuple-element.53), channel_id=1, source_target_pairs={{0,4},{1,5},{2,6},{3,7},{4,0},{5,1},{6,2},{7,3},{8,12},{9,13},{10,... | collective-permute-start | bytes 393224 | tf_op jit(solution)/shard_map/ppermute | solution.py:329
  57.5 1.4 %collective-permute-start.21 = (bf16[2,16,16,128]{3,2,1,0:T(8,128)(2,1)S(1)}, bf16[2,16,16,128]{3,2,1,0:T(8,128)(2,1)S(1)}, u32[]{:S(2)}, u32[]{:S(2)}) collective-permute-start(bf16[2,16,16,128]{3,2,1,0:T(8,128)(2,1)S(1)} %get-tuple-element.52), channel_id=1, source_target_pairs={{0,6},{1,7},{2,4},{3,5},{4,2},{5,3},{6,0},{7,1},{8,14},{9,15},{10,... | collective-permute-start | bytes 393224 | tf_op jit(solution)/shard_map/ppermute | solution.py:329
  58.9 0.0 collective-permute-done.14
  59.0 0.7 %constant_dynamic-update-slice_fusion = bf16[32,128,128]{2,1,0:T(8,128)(2,1)} fusion(bf16[32,128,128]{2,1,0:T(8,128)(2,1)} %get-tuple-element.35, bf16[8,128,128]{2,1,0:T(8,128)(2,1)S(1)} %collective-permute-done.7, s32[]{:T(128)S(6)} %select_n.111), kind=kLoop, calls=%fused_computation.23 | loop fusion | bytes 524292 | tf_op jit(solution)/shard_map/dynamic_update_slice | solution.py:394
  59.7 1.0 %collective-permute-done.19 = bf16[2,16,16,128]{3,2,1,0:T(8,128)(2,1)S(1)} collective-permute-done((bf16[2,16,16,128]{3,2,1,0:T(8,128)(2,1)S(1)}, bf16[2,16,16,128]{3,2,1,0:T(8,128)(2,1)S(1)}, u32[]{:S(2)}, u32[]{:S(2)}) %collective-permute-start.19) | collective-permute-done | bytes 131104 | tf_op jit(solution)/shard_map/ppermute | solution.py:329
  60.7 7.6 %collective-permute-done.20 = bf16[2,16,16,128]{3,2,1,0:T(8,128)(2,1)S(1)} collective-permute-done((bf16[2,16,16,128]{3,2,1,0:T(8,128)(2,1)S(1)}, bf16[2,16,16,128]{3,2,1,0:T(8,128)(2,1)S(1)}, u32[]{:S(2)}, u32[]{:S(2)}) %collective-permute-start.20) | collective-permute-done | bytes 131104 | tf_op jit(solution)/shard_map/ppermute | solution.py:329
  68.3 0.1 fusion.2
  68.4 0.0 copy-start
  68.4 0.0 copy-start.1
  68.5 0.7 copy-done
  69.1 0.1 copy-done.1
  (17 shorter events, 0.2 us)
Async XLA Ops:
  2.7 26.1 %collective-permute-start.3 = (bf16[2,8,128,128]{3,2,1,0:T(8,128)(2,1)S(1)}, bf16[2,8,128,128]{3,2,1,0:T(8,128)(2,1)S(1)}, u32[]{:S(2)}, u32[]{:S(2)}) collective-permute-start(bf16[2,8,128,128]{3,2,1,0:T(8,128)(2,1)S(1)} %get-tuple-element.30), channel_id=1, source_target_pairs={{0,1},{1,0},{2,3},{3,2},{4,5},{5,4},{6,7},{7,6},{8,9},{9,8},{10,11... | collective-permute-start | bytes 1572872 | tf_op jit(solution)/shard_map/ppermute | solution.py:352
  5.8 2.1 %collective-permute-start.4 = (bf16[2,16,16,128]{3,2,1,0:T(8,128)(2,1)S(1)}, bf16[2,16,16,128]{3,2,1,0:T(8,128)(2,1)S(1)}, u32[]{:S(2)}, u32[]{:S(2)}) collective-permute-start(bf16[2,16,16,128]{3,2,1,0:T(8,128)(2,1)S(1)} %get-tuple-element.31), channel_id=1, source_target_pairs={{0,8},{8,0},{16,24},{24,16},{1,9},{9,1},{17,25},{25,17},{2,10},{10... | collective-permute-start | bytes 393224 | tf_op jit(solution)/shard_map/ppermute | solution.py:318
  5.8 6.4 %collective-permute-start.5 = (bf16[2,16,16,128]{3,2,1,0:T(8,128)(2,1)S(1)}, bf16[2,16,16,128]{3,2,1,0:T(8,128)(2,1)S(1)}, u32[]{:S(2)}, u32[]{:S(2)}) collective-permute-start(bf16[2,16,16,128]{3,2,1,0:T(8,128)(2,1)S(1)} %get-tuple-element.32), channel_id=1, source_target_pairs={{0,16},{8,24},{16,0},{24,8},{1,17},{9,25},{17,1},{25,9},{2,18},{10... | collective-permute-start | bytes 393224 | tf_op jit(solution)/shard_map/ppermute | solution.py:318
  7.3 6.8 %collective-permute-start.6 = (bf16[2,16,16,128]{3,2,1,0:T(8,128)(2,1)S(1)}, bf16[2,16,16,128]{3,2,1,0:T(8,128)(2,1)S(1)}, u32[]{:S(2)}, u32[]{:S(2)}) collective-permute-start(bf16[2,16,16,128]{3,2,1,0:T(8,128)(2,1)S(1)} %get-tuple-element.33), channel_id=1, source_target_pairs={{0,24},{8,16},{16,8},{24,0},{1,25},{9,17},{17,9},{25,1},{2,26},{10... | collective-permute-start | bytes 393224 | tf_op jit(solution)/shard_map/ppermute | solution.py:318
  7.7 13.0 %collective-permute-start = (bf16[2,8,16,128]{3,2,1,0:T(8,128)(2,1)S(1)}, bf16[2,8,16,128]{3,2,1,0:T(8,128)(2,1)S(1)}, u32[]{:S(2)}, u32[]{:S(2)}) collective-permute-start(bf16[2,8,16,128]{3,2,1,0:T(8,128)(2,1)S(1)} %get-tuple-element.27), channel_id=1, source_target_pairs={{0,8},{8,0},{16,24},{24,16},{1,9},{9,1},{17,25},{25,17},{2,10},{10... | collective-permute-start | bytes 196616 | tf_op jit(solution)/shard_map/ppermute | solution.py:318
  8.0 12.7 %collective-permute-start.1 = (bf16[2,8,16,128]{3,2,1,0:T(8,128)(2,1)S(1)}, bf16[2,8,16,128]{3,2,1,0:T(8,128)(2,1)S(1)}, u32[]{:S(2)}, u32[]{:S(2)}) collective-permute-start(bf16[2,8,16,128]{3,2,1,0:T(8,128)(2,1)S(1)} %get-tuple-element.28), channel_id=1, source_target_pairs={{0,16},{8,24},{16,0},{24,8},{1,17},{9,25},{17,1},{25,9},{2,18},{10... | collective-permute-start | bytes 196616 | tf_op jit(solution)/shard_map/ppermute | solution.py:318
  18.2 15.5 %collective-permute-start.16 = (bf16[2,16,16,128]{3,2,1,0:T(8,128)(2,1)S(1)}, bf16[2,16,16,128]{3,2,1,0:T(8,128)(2,1)S(1)}, u32[]{:S(2)}, u32[]{:S(2)}) collective-permute-start(bf16[2,16,16,128]{3,2,1,0:T(8,128)(2,1)S(1)} %get-tuple-element.47), channel_id=1, source_target_pairs={{0,16},{8,24},{16,0},{24,8},{1,17},{9,25},{17,1},{25,9},{2,18},{10... | collective-permute-start | bytes 393224 | tf_op jit(solution)/shard_map/ppermute | solution.py:318
  19.7 14.3 %collective-permute-start.17 = (bf16[2,16,16,128]{3,2,1,0:T(8,128)(2,1)S(1)}, bf16[2,16,16,128]{3,2,1,0:T(8,128)(2,1)S(1)}, u32[]{:S(2)}, u32[]{:S(2)}) collective-permute-start(bf16[2,16,16,128]{3,2,1,0:T(8,128)(2,1)S(1)} %get-tuple-element.48), channel_id=1, source_target_pairs={{0,24},{8,16},{16,8},{24,0},{1,25},{9,17},{17,9},{25,1},{2,26},{10... | collective-permute-start | bytes 393224 | tf_op jit(solution)/shard_map/ppermute | solution.py:318
  20.6 13.4 %collective-permute-start.15 = (bf16[2,16,16,128]{3,2,1,0:T(8,128)(2,1)S(1)}, bf16[2,16,16,128]{3,2,1,0:T(8,128)(2,1)S(1)}, u32[]{:S(2)}, u32[]{:S(2)}) collective-permute-start(bf16[2,16,16,128]{3,2,1,0:T(8,128)(2,1)S(1)} %get-tuple-element.46), channel_id=1, source_target_pairs={{0,8},{8,0},{16,24},{24,16},{1,9},{9,1},{17,25},{25,17},{2,10},{10... | collective-permute-start | bytes 393224 | tf_op jit(solution)/shard_map/ppermute | solution.py:318
  20.6 8.2 %collective-permute-start.2 = (bf16[2,8,16,128]{3,2,1,0:T(8,128)(2,1)S(1)}, bf16[2,8,16,128]{3,2,1,0:T(8,128)(2,1)S(1)}, u32[]{:S(2)}, u32[]{:S(2)}) collective-permute-start(bf16[2,8,16,128]{3,2,1,0:T(8,128)(2,1)S(1)} %get-tuple-element.29), channel_id=1, source_target_pairs={{0,24},{8,16},{16,8},{24,0},{1,25},{9,17},{17,9},{25,1},{2,26},{10... | collective-permute-start | bytes 196616 | tf_op jit(solution)/shard_map/ppermute | solution.py:318
  32.2 3.5 %collective-permute-start.8 = (bf16[2,8,16,128]{3,2,1,0:T(8,128)(2,1)S(1)}, bf16[2,8,16,128]{3,2,1,0:T(8,128)(2,1)S(1)}, u32[]{:S(2)}, u32[]{:S(2)}) collective-permute-start(bf16[2,8,16,128]{3,2,1,0:T(8,128)(2,1)S(1)} %get-tuple-element.38), channel_id=1, source_target_pairs={{0,8},{8,0},{16,24},{24,16},{1,9},{9,1},{17,25},{25,17},{2,10},{10... | collective-permute-start | bytes 196616 | tf_op jit(solution)/shard_map/ppermute | solution.py:318
  32.2 4.5 %collective-permute-start.9 = (bf16[2,8,16,128]{3,2,1,0:T(8,128)(2,1)S(1)}, bf16[2,8,16,128]{3,2,1,0:T(8,128)(2,1)S(1)}, u32[]{:S(2)}, u32[]{:S(2)}) collective-permute-start(bf16[2,8,16,128]{3,2,1,0:T(8,128)(2,1)S(1)} %get-tuple-element.39), channel_id=1, source_target_pairs={{0,16},{8,24},{16,0},{24,8},{1,17},{9,25},{17,1},{25,9},{2,18},{10... | collective-permute-start | bytes 196616 | tf_op jit(solution)/shard_map/ppermute | solution.py:318
  33.7 4.0 %collective-permute-start.10 = (bf16[2,8,16,128]{3,2,1,0:T(8,128)(2,1)S(1)}, bf16[2,8,16,128]{3,2,1,0:T(8,128)(2,1)S(1)}, u32[]{:S(2)}, u32[]{:S(2)}) collective-permute-start(bf16[2,8,16,128]{3,2,1,0:T(8,128)(2,1)S(1)} %get-tuple-element.40), channel_id=1, source_target_pairs={{0,24},{8,16},{16,8},{24,0},{1,25},{9,17},{17,9},{25,1},{2,26},{10... | collective-permute-start | bytes 196616 | tf_op jit(solution)/shard_map/ppermute | solution.py:318
  35.4 18.4 %collective-permute-start.18 = (bf16[2,16,2,2,16,128]{5,4,1,0,3,2:T(8,128)(2,1)S(1)}, bf16[2,16,2,2,16,128]{5,4,1,0,3,2:T(8,128)(2,1)S(1)}, u32[]{:S(2)}, u32[]{:S(2)}) collective-permute-start(bf16[2,16,2,2,16,128]{5,4,1,0,3,2:T(8,128)(2,1)S(1)} %copy.9), channel_id=1, source_target_pairs={{0,1},{1,0},{2,3},{3,2},{4,5},{5,4},{6,7},{7,6},{8,9},{9,8},{10,11... | collective-permute-start | bytes 1572872 | tf_op jit(solution)/shard_map/ppermute | solution.py:329
  38.6 7.7 %collective-permute-start.11 = (bf16[2,8,2,16,128]{4,3,2,1,0:T(8,128)(2,1)S(1)}, bf16[2,8,2,16,128]{4,3,2,1,0:T(8,128)(2,1)S(1)}, u32[]{:S(2)}, u32[]{:S(2)}) collective-permute-start(bf16[2,8,2,16,128]{4,3,2,1,0:T(8,128)(2,1)S(1)} %get-tuple-element.42), channel_id=1, source_target_pairs={{0,2},{1,3},{2,0},{3,1},{4,6},{5,7},{6,4},{7,5},{8,10},{9,11},{10,... | collective-permute-start | bytes 393224 | tf_op jit(solution)/shard_map/ppermute | solution.py:329
  40.2 12.9 %collective-permute-start.12 = (bf16[2,8,2,16,128]{4,3,2,1,0:T(8,128)(2,1)S(1)}, bf16[2,8,2,16,128]{4,3,2,1,0:T(8,128)(2,1)S(1)}, u32[]{:S(2)}, u32[]{:S(2)}) collective-permute-start(bf16[2,8,2,16,128]{4,3,2,1,0:T(8,128)(2,1)S(1)} %get-tuple-element.43), channel_id=1, source_target_pairs={{0,4},{1,5},{2,6},{3,7},{4,0},{5,1},{6,2},{7,3},{8,12},{9,13},{10,... | collective-permute-start | bytes 393224 | tf_op jit(solution)/shard_map/ppermute | solution.py:329
  42.8 10.3 %collective-permute-start.13 = (bf16[2,8,2,16,128]{4,3,2,1,0:T(8,128)(2,1)S(1)}, bf16[2,8,2,16,128]{4,3,2,1,0:T(8,128)(2,1)S(1)}, u32[]{:S(2)}, u32[]{:S(2)}) collective-permute-start(bf16[2,8,2,16,128]{4,3,2,1,0:T(8,128)(2,1)S(1)} %get-tuple-element.44), channel_id=1, source_target_pairs={{0,6},{1,7},{2,4},{3,5},{4,2},{5,3},{6,0},{7,1},{8,14},{9,15},{10,... | collective-permute-start | bytes 393224 | tf_op jit(solution)/shard_map/ppermute | solution.py:329
  43.1 15.9 %collective-permute-start.7 = (bf16[8,128,128]{2,1,0:T(8,128)(2,1)S(1)}, bf16[8,128,128]{2,1,0:T(8,128)(2,1)S(1)}, u32[]{:S(2)}, u32[]{:S(2)}) collective-permute-start(bf16[8,128,128]{2,1,0:T(8,128)(2,1)S(1)} %get-tuple-element.36), channel_id=1, source_target_pairs={{0,1},{1,0},{2,3},{3,2},{4,5},{5,4},{6,7},{7,6},{8,9},{9,8},{10,11... | collective-permute-start | bytes 786440 | tf_op jit(solution)/shard_map/ppermute | solution.py:352
  53.2 5.7 %collective-permute-start.14 = (bf16[2,8,16,128]{3,2,1,0:T(8,128)(2,1)S(1)}, bf16[2,8,16,128]{3,2,1,0:T(8,128)(2,1)S(1)}, u32[]{:S(2)}, u32[]{:S(2)}) collective-permute-start(bf16[2,8,16,128]{3,2,1,0:T(8,128)(2,1)S(1)} %fusion.8), channel_id=1, source_target_pairs={{0,1},{1,0},{2,3},{3,2},{4,5},{5,4},{6,7},{7,6},{8,9},{9,8},{10,11... | collective-permute-start | bytes 196616 | tf_op jit(solution)/shard_map/ppermute | solution.py:352
  54.0 6.7 %collective-permute-start.19 = (bf16[2,16,16,128]{3,2,1,0:T(8,128)(2,1)S(1)}, bf16[2,16,16,128]{3,2,1,0:T(8,128)(2,1)S(1)}, u32[]{:S(2)}, u32[]{:S(2)}) collective-permute-start(bf16[2,16,16,128]{3,2,1,0:T(8,128)(2,1)S(1)} %get-tuple-element.51), channel_id=1, source_target_pairs={{0,2},{1,3},{2,0},{3,1},{4,6},{5,7},{6,4},{7,5},{8,10},{9,11},{10,... | collective-permute-start | bytes 393224 | tf_op jit(solution)/shard_map/ppermute | solution.py:329
  56.4 11.9 %collective-permute-start.20 = (bf16[2,16,16,128]{3,2,1,0:T(8,128)(2,1)S(1)}, bf16[2,16,16,128]{3,2,1,0:T(8,128)(2,1)S(1)}, u32[]{:S(2)}, u32[]{:S(2)}) collective-permute-start(bf16[2,16,16,128]{3,2,1,0:T(8,128)(2,1)S(1)} %get-tuple-element.53), channel_id=1, source_target_pairs={{0,4},{1,5},{2,6},{3,7},{4,0},{5,1},{6,2},{7,3},{8,12},{9,13},{10,... | collective-permute-start | bytes 393224 | tf_op jit(solution)/shard_map/ppermute | solution.py:329
  57.5 10.8 %collective-permute-start.21 = (bf16[2,16,16,128]{3,2,1,0:T(8,128)(2,1)S(1)}, bf16[2,16,16,128]{3,2,1,0:T(8,128)(2,1)S(1)}, u32[]{:S(2)}, u32[]{:S(2)}) collective-permute-start(bf16[2,16,16,128]{3,2,1,0:T(8,128)(2,1)S(1)} %get-tuple-element.52), channel_id=1, source_target_pairs={{0,6},{1,7},{2,4},{3,5},{4,2},{5,3},{6,0},{7,1},{8,14},{9,15},{10,... | collective-permute-start | bytes 393224 | tf_op jit(solution)/shard_map/ppermute | solution.py:329
  68.4 0.7 %copy-start = (f32[32,16,128]{2,1,0:T(8,128)}, f32[32,16,128]{2,1,0:T(8,128)S(1)}, u32[]{:S(2)}) copy-start(f32[32,16,128]{2,1,0:T(8,128)S(1)} %get-tuple-element.57) | copy-start | bytes 786436
  68.4 0.8 %copy-start.1 = (f32[32,16,128]{2,1,0:T(8,128)}, f32[32,16,128]{2,1,0:T(8,128)S(1)}, u32[]{:S(2)}) copy-start(f32[32,16,128]{2,1,0:T(8,128)S(1)} %get-tuple-element.56) | copy-start | bytes 786436

commit v4 on v3

--- a/solution.py
+++ b/solution.py
@@ -10,7 +10,7 @@
 
 
 KB = 16
-PLAN = ((16, 16, False, (1, 2)), (0, 16, True, (2,)))
+PLAN = ((16, 16, False, ((1, 2), (1, 1, 1))), (0, 16, True, (2,)))
 STEP_HEADS = 8
 VMEM_SMALL = 8 << 20
 VMEM_ATTEND = 16 << 20
@@ -241,7 +241,7 @@
     return found
 
 
-def merge_kernel(masks, bits, routes, own, *rest):
+def merge_kernel(masks, firsts, routes, own, *rest):
     slots = len(masks)
     back = rest[:slots]
     outs, total = rest[slots:-1], rest[-1]
@@ -253,34 +253,42 @@
         first = routes[group ^ mask, group] * per_block
         spot = pl.ds(first, per_block)
         total[:, :, spot] = total[:, :, spot] + part[...].astype(jnp.float32)
-    chosen = sum(bits)
-    bases = [index for index in range(own.shape[2]) if index & chosen == 0]
-    for mix, out in zip(mixes(bits), outs):
-        for index, base in enumerate(bases):
-            out[:, :, index] = total[:, :, base + ((rank ^ mix) & chosen)].astype(jnp.bfloat16)
-
-
-def merge(routes, own, back, groups, ranks, bits):
+    outs = list(outs)
+    for side, bits in enumerate(firsts):
+        sides = slice(side, side + 1) if len(firsts) > 1 else slice(0, 2)
+        chosen = sum(bits)
+        bases = [index for index in range(own.shape[2]) if index & chosen == 0]
+        for mix in mixes(bits):
+            out = outs.pop(0)
+            for index, base in enumerate(bases):
+                spot = base + ((rank ^ mix) & chosen)
+                out[:, :, index] = total[sides, :, spot].astype(jnp.bfloat16)
+
+
+def merge(routes, own, back, groups, ranks, firsts):
     _, chunk_heads, group_keys, head_dim = own.shape
     rank_keys = group_keys // ranks
-    step_heads = step_of(chunk_heads)
+    step_heads = math.gcd(16, chunk_heads)
     masks = far_masks(groups)
     rows = (KB // rank_keys, rank_keys)
 
-    def blocks(count):
+    def blocks(sides, count):
         return pl.BlockSpec(
-            (2, step_heads, count, rank_keys, head_dim), lambda i: (0, i, 0, 0, 0)
-        )
-
-    pieces = 1 << len(bits)
-    piece = (2, chunk_heads, ranks // pieces, rank_keys, head_dim)
-    return pl.pallas_call(
-        functools.partial(merge_kernel, masks, bits),
-        out_shape=[jax.ShapeDtypeStruct(piece, jnp.bfloat16)] * pieces,
+            (sides, step_heads, count, rank_keys, head_dim), lambda i: (0, i, 0, 0, 0)
+        )
+
+    sides = 2 // len(firsts)
+    counts = [ranks >> len(bits) for bits in firsts for _ in mixes(bits)]
+    outs = pl.pallas_call(
+        functools.partial(merge_kernel, masks, firsts),
+        out_shape=[
+            jax.ShapeDtypeStruct((sides, chunk_heads, count, rank_keys, head_dim), jnp.bfloat16)
+            for count in counts
+        ],
         grid=(chunk_heads // step_heads,),
-        in_specs=[pl.BlockSpec(memory_space=pltpu.SMEM), blocks(ranks)]
+        in_specs=[pl.BlockSpec(memory_space=pltpu.SMEM), blocks(2, ranks)]
         + slot_specs(groups, step_heads, rows, head_dim),
-        out_specs=[blocks(ranks // pieces)] * pieces,
+        out_specs=[blocks(sides, count) for count in counts],
         scratch_shapes=[
             pltpu.VMEM((2, step_heads, ranks, rank_keys, head_dim), jnp.float32)
         ],
@@ -291,6 +299,11 @@
         own.reshape(2, chunk_heads, ranks, rank_keys, head_dim),
         *(part.reshape(part.shape[:-2] + rows + (head_dim,)) for part in back),
     )
+    pieces = []
+    for bits in firsts:
+        pieces.append(outs[: 1 << len(bits)])
+        outs = outs[1 << len(bits) :]
+    return pieces
 
 
 def body(query_rows, out_grad, key_rows, value_rows, routes):
@@ -322,7 +335,7 @@
         left = [bit for bit in bits]
         for step, stage in enumerate(stages):
             left = [bit for bit in left if bit not in stage]
-            shape = (2, pieces[0].shape[1]) + (2,) * len(left) + (rank_keys, head_dim)
+            shape = pieces[0].shape[:2] + (2,) * len(left) + (rank_keys, head_dim)
             came = []
             for mix, piece in zip(mixes(stage)[1:], pieces[1:]):
                 came.append(
@@ -378,14 +391,21 @@
         back = exchange(parts)
         if other is not None:
             others.append((cut, trade(other)))
-        wanted = [bit for bit in bits if not (cut[2] and bit == 1)]
-        stages = []
-        for size in cut[3] + (1,) * len(bits):
-            if wanted:
-                stages.append(tuple(wanted[:size]))
-                wanted = wanted[size:]
-        pieces = merge(routes, own, back, groups, ranks, stages[0])
-        total = scatter(pieces, stages)
+        split = isinstance(cut[3][0], tuple)
+        plans = []
+        for sizes in cut[3] if split else (cut[3],):
+            wanted = [bit for bit in bits if not (cut[2] and bit == 1)]
+            plans.append([])
+            for size in sizes + (1,) * len(bits):
+                if wanted:
+                    plans[-1].append(tuple(wanted[:size]))
+                    wanted = wanted[size:]
+        pieces = merge(routes, own, back, groups, ranks, [stages[0] for stages in plans])
+        total = [scatter(pieces[i], stages) for i, stages in enumerate(plans)]
+        if split:
+            total = jnp.concatenate(total, axis=0) if cut[2] else [part[0] for part in total]
+        else:
+            total = total[0]
         if cut[2]:
             total = join(total)
         results.append(total)

time: 69.5 us -> 86.7 us (1.25)
  waiting for transfers between devices: 31.5 us -> 41.7 us
  starting transfers between devices: 23.3 us -> 30.4 us
    ppermute x3, waiting for transfers between devices: 0.01 us -> 12.5 us  [trade(): return lax.ppermute(rows, 'ulysses', [(r, r ^ 1) for r in range(ranks)])]
    ppermute x7 -> x10, starting transfers between devices: 9.68 us -> 18.9 us  [scatter(): lax.ppermute(piece.reshape(shape), 'ulysses', [(r, r ^ mix) for r in rang...]
    ppermute x3, starting transfers between devices: 4.07 us -> 2.22 us  [trade(): return lax.ppermute(rows, 'ulysses', [(r, r ^ 1) for r in range(ranks)])]
    ppermute x12, waiting for transfers between devices: 13.3 us -> 12 us  [exchange(): lax.ppermute(part, 'blk', [(g, g ^ mask) for g in range(groups)])]
    ppermute x7 -> x10, waiting for transfers between devices: 18.2 us -> 17.2 us  [scatter(): lax.ppermute(piece.reshape(shape), 'ulysses', [(r, r ^ mix) for r in rang...]
  transfers between devices with their start and end apart: 22 -> 25, of which waited for: 9 -> 10; matrix products, arithmetic and copies ran while one was open for 2% -> 1% of each run, Pallas kernels for 14% -> 5%
where the time goes in v4:
time: 86.7 us; the launch traced here: 86.4 us
  waiting for transfers between devices  41.7 us (48%)
  starting transfers between devices  30.4 us (35%)
  Pallas kernels  11.6 us (13%)
  local copies, waits for them, and re-layouts  1.62 us (2%)
    ppermute x10, starting transfers between devices, scatter(): lax.ppermute(piece.reshape(shape), 'ulysses', [(r, r ^ mix) for r in rang...  18.9 us
    ppermute x10, waiting for transfers between devices, scatter(): lax.ppermute(piece.reshape(shape), 'ulysses', [(r, r ^ mix) for r in rang...  17.2 us
    ppermute x3, waiting for transfers between devices, trade(): return lax.ppermute(rows, 'ulysses', [(r, r ^ 1) for r in range(ranks)])  12.5 us
    ppermute x12, waiting for transfers between devices, exchange(): lax.ppermute(part, 'blk', [(g, g ^ mask) for g in range(groups)])  12 us
    ppermute x12, starting transfers between devices, exchange(): lax.ppermute(part, 'blk', [(g, g ^ mask) for g in range(groups)])  9.29 us
    pallas_call x2, Pallas kernels, attend(): pl.pallas_call(functools.partial(attend_kernel, masks, query_out is not N...  7.53 us
    ppermute x3, starting transfers between devices, trade(): return lax.ppermute(rows, 'ulysses', [(r, r ^ 1) for r in range(ranks)])  2.22 us
    pallas_call x1, Pallas kernels, pick(): pl.pallas_call(functools.partial(pick_kernel, cuts, groups), out_shape=[j...  2.11 us
  transfers between devices with their start and end apart: 25, of which 10 were waited for; matrix products, arithmetic and copies ran while one was open for 1% of the time, Pallas kernels for 5%

profile of v4, /device:TPU:0, one launch (start us, length us, event | category | flops | bytes accessed | tf_op | source)
XLA Modules:
  0.0 86.4 jit_solution(8318710721554661894)
XLA Ops:
  0.6 2.1 %pick.1 = (bf16[2,16,16,128]{3,2,1,0:T(8,128)(2,1)S(1)}, bf16[2,16,16,128]{3,2,1,0:T(8,128)(2,1)S(1)}, bf16[2,16,16,128]{3,2,1,0:T(8,128)(2,1)S(1)}, bf16[2,8,12...) custom-call(s32[4,4]{1,0:T(4,128)} %routes.5, ...), custom_call_target="tpu_custom_call" | custom-call | tf_op jit(solution)/shard_map/pick/pallas_call | solution.py:69
  2.7 0.6 collective-permute-start.4
  3.3 2.6 %collective-permute-start.5 = (bf16[2,16,16,128]{3,2,1,0:T(8,128)(2,1)S(1)}, bf16[2,16,16,128]{3,2,1,0:T(8,128)(2,1)S(1)}, u32[]{:S(2)}, u32[]{:S(2)}) collective-permute-start(bf16[2,16,16,128]{3,2,1,0:T(8,128)(2,1)S(1)} %get-tuple-element.34), channel_id=1, source_target_pairs={{0,16},{8,24},{16,0},{24,8},{1,17},{9,25},{17,1},{25,9},{2,18},{10... | collective-permute-start | bytes 393224 | tf_op jit(solution)/shard_map/ppermute | solution.py:331
  5.9 0.0 collective-permute-start.6
  5.9 0.0 collective-permute-done.4.rest_0_
  5.9 4.3 %collective-permute-done.5.rest_1_ = bf16[2,16,16,128]{3,2,1,0:T(8,128)(2,1)S(1)} collective-permute-done((bf16[2,16,16,128]{3,2,1,0:T(8,128)(2,1)S(1)}, bf16[2,16,16,128]{3,2,1,0:T(8,128)(2,1)S(1)}, u32[]{:S(2)}, u32[]{:S(2)}) %collective-permute-start.5) | collective-permute-done | bytes 131104 | tf_op jit(solution)/shard_map/ppermute | solution.py:331
  10.2 2.3 %collective-permute-done.6.rest_2_ = bf16[2,16,16,128]{3,2,1,0:T(8,128)(2,1)S(1)} collective-permute-done((bf16[2,16,16,128]{3,2,1,0:T(8,128)(2,1)S(1)}, bf16[2,16,16,128]{3,2,1,0:T(8,128)(2,1)S(1)}, u32[]{:S(2)}, u32[]{:S(2)}) %collective-permute-start.6) | collective-permute-done | bytes 131104 | tf_op jit(solution)/shard_map/ppermute | solution.py:331
  12.5 4.1 %attend.2 = (bf16[32,128,128]{2,1,0:T(8,128)(2,1)}, bf16[2,16,128,128]{3,2,1,0:T(8,128)(2,1)S(1)}, bf16[2,16,16,128]{3,2,1,0:T(8,128)(2,1)S(1)}, bf16[2,16,16,12...) custom-call(s32[1]{0:T(128)} %bitcast._, bf16[32,128,128]{2,1,0:T(8,128)(2,1)} %query.5, bf16[32,128,128]{2,1,0:T(8,128)(2,1)} %grad.5, ...), custom_call_target="tpu_custom_call" | custom-call | tf_op jit(solution)/shard_map/attend/pallas_call | solution.py:216
  16.6 1.5 %collective-permute-start.16 = (bf16[2,16,16,128]{3,2,1,0:T(8,128)(2,1)S(1)}, bf16[2,16,16,128]{3,2,1,0:T(8,128)(2,1)S(1)}, u32[]{:S(2)}, u32[]{:S(2)}) collective-permute-start(bf16[2,16,16,128]{3,2,1,0:T(8,128)(2,1)S(1)} %get-tuple-element.49), channel_id=1, source_target_pairs={{0,16},{8,24},{16,0},{24,8},{1,17},{9,25},{17,1},{25,9},{2,18},{10... | collective-permute-start | bytes 393224 | tf_op jit(solution)/shard_map/ppermute | solution.py:331
  18.1 0.7 collective-permute-start.15
  18.8 4.2 %collective-permute-done.16 = bf16[2,16,16,128]{3,2,1,0:T(8,128)(2,1)S(1)} collective-permute-done((bf16[2,16,16,128]{3,2,1,0:T(8,128)(2,1)S(1)}, bf16[2,16,16,128]{3,2,1,0:T(8,128)(2,1)S(1)}, u32[]{:S(2)}, u32[]{:S(2)}) %collective-permute-start.16) | collective-permute-done | bytes 131104 | tf_op jit(solution)/shard_map/ppermute | solution.py:331
  23.0 1.2 %collective-permute-done.17 = bf16[2,16,16,128]{3,2,1,0:T(8,128)(2,1)S(1)} collective-permute-done((bf16[2,16,16,128]{3,2,1,0:T(8,128)(2,1)S(1)}, bf16[2,16,16,128]{3,2,1,0:T(8,128)(2,1)S(1)}, u32[]{:S(2)}, u32[]{:S(2)}) %collective-permute-start.17) | collective-permute-done | bytes 131104 | tf_op jit(solution)/shard_map/ppermute | solution.py:331
  24.2 1.1 %merge.3 = (bf16[1,16,4,16,128]{4,3,2,1,0:T(8,128)(2,1)S(1)}, bf16[1,16,4,16,128]{4,3,2,1,0:T(8,128)(2,1)S(1)}, bf16[1,16,4,16,128]{4,3,2,1,0:T(8,128)(2,1)S(1)}, bf16[1,16,4,16,128]{4,3,2,1,0:T(8,128)(2,1)S(1)}) custom-call(s32[4,4]{1,0:T(4,128)} %routes.5, bf16[2,16,8,16,128]{4,3,2,1,0:T(8,128)(2,1)S(1)} %bitcast.51, ...), custom_call_target="tpu_custom_call" | custom-call | tf_op jit(solution)/shard_map/merge/pallas_call | solution.py:282
  25.3 2.0 %collective-permute-start.22 = (bf16[1,16,2,2,16,128]{5,4,1,2,3,0:T(8,128)(2,1)S(1)}, bf16[1,16,2,2,16,128]{5,4,1,2,3,0:T(8,128)(2,1)S(1)}, u32[]{:S(2)}, u32[]{:S(2)}) collective-permute-start(bf16[1,16,2,2,16,128]{5,4,1,2,3,0:T(8,128)(2,1)S(1)} %copy.11), channel_id=1, source_target_pairs={{0,1},{1,0},{2,3},{3,2},{4,5},{5,4},{6,7},{7,6},{8,9},{9,8},{10,11... | collective-permute-start | bytes 786440 | tf_op jit(solution)/shard_map/ppermute | solution.py:342
  27.3 0.1 collective-permute-start.3
  27.4 0.1 collective-permute-start
  27.5 1.8 %collective-permute-start.1 = (bf16[2,8,16,128]{3,2,1,0:T(8,128)(2,1)S(1)}, bf16[2,8,16,128]{3,2,1,0:T(8,128)(2,1)S(1)}, u32[]{:S(2)}, u32[]{:S(2)}) collective-permute-start(bf16[2,8,16,128]{3,2,1,0:T(8,128)(2,1)S(1)} %get-tuple-element.30), channel_id=1, source_target_pairs={{0,16},{8,24},{16,0},{24,8},{1,17},{9,25},{17,1},{25,9},{2,18},{10... | collective-permute-start | bytes 196616 | tf_op jit(solution)/shard_map/ppermute | solution.py:331
  29.3 0.1 collective-permute-start.2
  29.4 5.1 %collective-permute-done.22 = bf16[1,16,2,2,16,128]{5,4,1,2,3,0:T(8,128)(2,1)S(1)} collective-permute-done((bf16[1,16,2,2,16,128]{5,4,1,2,3,0:T(8,128)(2,1)S(1)}, bf16[1,16,2,2,16,128]{5,4,1,2,3,0:T(8,128)(2,1)S(1)}, u32[]{:S(2)}, u32[]{:S(2)}) %collective-permute-start.22) | collective-permute-done | bytes 262176 | tf_op jit(solution)/shard_map/ppermute | solution.py:342
  34.6 1.9 %collective-permute-start.18 = (bf16[1,16,2,2,16,128]{5,4,1,3,2,0:T(8,128)(2,1)S(1)}, bf16[1,16,2,2,16,128]{5,4,1,3,2,0:T(8,128)(2,1)S(1)}, u32[]{:S(2)}, u32[]{:S(2)}) collective-permute-start(bf16[1,16,2,2,16,128]{5,4,1,3,2,0:T(8,128)(2,1)S(1)} %copy.9), channel_id=1, source_target_pairs={{0,1},{1,0},{2,3},{3,2},{4,5},{5,4},{6,7},{7,6},{8,9},{9,8},{10,11... | collective-permute-start | bytes 786440 | tf_op jit(solution)/shard_map/ppermute | solution.py:342
  36.5 0.1 fusion
  36.6 0.0 collective-permute-done.rest_0_
  36.6 1.6 %collective-permute-start.23 = (bf16[1,16,2,16,128]{4,3,1,2,0:T(8,128)(2,1)S(1)}, bf16[1,16,2,16,128]{4,3,1,2,0:T(8,128)(2,1)S(1)}, u32[]{:S(2)}, u32[]{:S(2)}) collective-permute-start(bf16[1,16,2,16,128]{4,3,1,2,0:T(8,128)(2,1)S(1)} %dynamic-slice_bitcast_fusion), channel_id=1, source_target_pairs={{0,2},{1,3},{2,0},{3,1},{4,6},{5,7},{6,4},{7,5},{8,10},{9,11},{10,... | collective-permute-start | bytes 393224 | tf_op jit(solution)/shard_map/ppermute | solution.py:342
  38.2 0.0 collective-permute-done.2.rest_2_
  38.2 7.6 %collective-permute-done.3.rest_3_ = bf16[2,8,128,128]{3,2,1,0:T(8,128)(2,1)S(1)} collective-permute-done((bf16[2,8,128,128]{3,2,1,0:T(8,128)(2,1)S(1)}, bf16[2,8,128,128]{3,2,1,0:T(8,128)(2,1)S(1)}, u32[]{:S(2)}, u32[]{:S(2)}) %collective-permute-start.3) | collective-permute-done | bytes 524320 | tf_op jit(solution)/shard_map/ppermute | solution.py:365
  45.8 3.4 %attend.3 = (bf16[8,128,128]{2,1,0:T(8,128)(2,1)S(1)}, bf16[32,128,128]{2,1,0:T(8,128)(2,1)}, bf16[2,8,128,128]{3,2,1,0:T(8,128)(2,1)S(1)}, bf16[2,8,16,128]{3,2...) custom-call(s32[1]{0:T(128)} %bitcast._, ...), custom_call_target="tpu_custom_call", output_to_operand_aliasing={{1}: (9, {})} | custom-call | tf_op jit(solution)/shard_map/attend/pallas_call | solution.py:216
  49.2 1.9 %collective-permute-start.9 = (bf16[2,8,16,128]{3,2,1,0:T(8,128)(2,1)S(1)}, bf16[2,8,16,128]{3,2,1,0:T(8,128)(2,1)S(1)}, u32[]{:S(2)}, u32[]{:S(2)}) collective-permute-start(bf16[2,8,16,128]{3,2,1,0:T(8,128)(2,1)S(1)} %get-tuple-element.41), channel_id=1, source_target_pairs={{0,16},{8,24},{16,0},{24,8},{1,17},{9,25},{17,1},{25,9},{2,18},{10... | collective-permute-start | bytes 196616 | tf_op jit(solution)/shard_map/ppermute | solution.py:331
  51.1 0.1 collective-permute-start.10
  51.2 0.1 fusion.1
  51.3 1.9 %collective-permute-start.19 = (bf16[1,16,16,128]{3,2,1,0:T(8,128)(2,1)S(1)}, bf16[1,16,16,128]{3,2,1,0:T(8,128)(2,1)S(1)}, u32[]{:S(2)}, u32[]{:S(2)}) collective-permute-start(bf16[1,16,16,128]{3,2,1,0:T(8,128)(2,1)S(1)} %get-tuple-element.59), channel_id=1, source_target_pairs={{0,2},{1,3},{2,0},{3,1},{4,6},{5,7},{6,4},{7,5},{8,10},{9,11},{10,... | collective-permute-start | bytes 196616 | tf_op jit(solution)/shard_map/ppermute | solution.py:342
  53.2 2.6 %collective-permute-start.20 = (bf16[1,16,16,128]{3,2,1,0:T(8,128)(2,1)S(1)}, bf16[1,16,16,128]{3,2,1,0:T(8,128)(2,1)S(1)}, u32[]{:S(2)}, u32[]{:S(2)}) collective-permute-start(bf16[1,16,16,128]{3,2,1,0:T(8,128)(2,1)S(1)} %get-tuple-element.61), channel_id=1, source_target_pairs={{0,4},{1,5},{2,6},{3,7},{4,0},{5,1},{6,2},{7,3},{8,12},{9,13},{10,... | collective-permute-start | bytes 196616 | tf_op jit(solution)/shard_map/ppermute | solution.py:342
  55.8 0.9 merge.2
  56.6 0.9 %collective-permute-start.11 = (bf16[2,8,2,16,128]{4,3,2,1,0:T(8,128)(2,1)S(1)}, bf16[2,8,2,16,128]{4,3,2,1,0:T(8,128)(2,1)S(1)}, u32[]{:S(2)}, u32[]{:S(2)}) collective-permute-start(bf16[2,8,2,16,128]{4,3,2,1,0:T(8,128)(2,1)S(1)} %get-tuple-element.44), channel_id=1, source_target_pairs={{0,2},{1,3},{2,0},{3,1},{4,6},{5,7},{6,4},{7,5},{8,10},{9,11},{10,... | collective-permute-start | bytes 393224 | tf_op jit(solution)/shard_map/ppermute | solution.py:342
  57.5 2.7 %collective-permute-start.12 = (bf16[2,8,2,16,128]{4,3,2,1,0:T(8,128)(2,1)S(1)}, bf16[2,8,2,16,128]{4,3,2,1,0:T(8,128)(2,1)S(1)}, u32[]{:S(2)}, u32[]{:S(2)}) collective-permute-start(bf16[2,8,2,16,128]{4,3,2,1,0:T(8,128)(2,1)S(1)} %get-tuple-element.45), channel_id=1, source_target_pairs={{0,4},{1,5},{2,6},{3,7},{4,0},{5,1},{6,2},{7,3},{8,12},{9,13},{10,... | collective-permute-start | bytes 393224 | tf_op jit(solution)/shard_map/ppermute | solution.py:342
  60.2 0.9 %collective-permute-start.13 = (bf16[2,8,2,16,128]{4,3,2,1,0:T(8,128)(2,1)S(1)}, bf16[2,8,2,16,128]{4,3,2,1,0:T(8,128)(2,1)S(1)}, u32[]{:S(2)}, u32[]{:S(2)}) collective-permute-start(bf16[2,8,2,16,128]{4,3,2,1,0:T(8,128)(2,1)S(1)} %get-tuple-element.46), channel_id=1, source_target_pairs={{0,6},{1,7},{2,4},{3,5},{4,2},{5,3},{6,0},{7,1},{8,14},{9,15},{10,... | collective-permute-start | bytes 393224 | tf_op jit(solution)/shard_map/ppermute | solution.py:342
  61.2 3.2 %collective-permute-done.11 = bf16[2,8,2,16,128]{4,3,2,1,0:T(8,128)(2,1)S(1)} collective-permute-done((bf16[2,8,2,16,128]{4,3,2,1,0:T(8,128)(2,1)S(1)}, bf16[2,8,2,16,128]{4,3,2,1,0:T(8,128)(2,1)S(1)}, u32[]{:S(2)}, u32[]{:S(2)}) %collective-permute-start.11) | collective-permute-done | bytes 131104 | tf_op jit(solution)/shard_map/ppermute | solution.py:342
  64.4 2.7 %collective-permute-start.21 = (bf16[1,16,16,128]{3,2,1,0:T(8,128)(2,1)S(1)}, bf16[1,16,16,128]{3,2,1,0:T(8,128)(2,1)S(1)}, u32[]{:S(2)}, u32[]{:S(2)}) collective-permute-start(bf16[1,16,16,128]{3,2,1,0:T(8,128)(2,1)S(1)} %get-tuple-element.60), channel_id=1, source_target_pairs={{0,6},{1,7},{2,4},{3,5},{4,2},{5,3},{6,0},{7,1},{8,14},{9,15},{10,... | collective-permute-start | bytes 196616 | tf_op jit(solution)/shard_map/ppermute | solution.py:342
  67.1 4.8 %collective-permute-done.12 = bf16[2,8,2,16,128]{4,3,2,1,0:T(8,128)(2,1)S(1)} collective-permute-done((bf16[2,8,2,16,128]{4,3,2,1,0:T(8,128)(2,1)S(1)}, bf16[2,8,2,16,128]{4,3,2,1,0:T(8,128)(2,1)S(1)}, u32[]{:S(2)}, u32[]{:S(2)}) %collective-permute-start.12) | collective-permute-done | bytes 131104 | tf_op jit(solution)/shard_map/ppermute | solution.py:342
  71.9 1.5 %collective-permute-start.7 = (bf16[8,128,128]{2,1,0:T(8,128)(2,1)S(1)}, bf16[8,128,128]{2,1,0:T(8,128)(2,1)S(1)}, u32[]{:S(2)}, u32[]{:S(2)}) collective-permute-start(bf16[8,128,128]{2,1,0:T(8,128)(2,1)S(1)} %get-tuple-element.38), channel_id=1, source_target_pairs={{0,1},{1,0},{2,3},{3,2},{4,5},{5,4},{6,7},{7,6},{8,9},{9,8},{10,11... | collective-permute-start | bytes 786440 | tf_op jit(solution)/shard_map/ppermute | solution.py:365
  73.4 0.1 convert_add_fusion.1
  73.5 0.6 collective-permute-start.14
  74.1 4.9 %collective-permute-done.14 = bf16[2,8,16,128]{3,2,1,0:T(8,128)(2,1)S(1)} collective-permute-done((bf16[2,8,16,128]{3,2,1,0:T(8,128)(2,1)S(1)}, bf16[2,8,16,128]{3,2,1,0:T(8,128)(2,1)S(1)}, u32[]{:S(2)}, u32[]{:S(2)}) %collective-permute-start.14) | collective-permute-done | bytes 65568 | tf_op jit(solution)/shard_map/ppermute | solution.py:365
  79.0 1.8 %collective-permute-start.24 = (bf16[1,16,16,128]{3,2,1,0:T(8,128)(2,1)S(1)}, bf16[1,16,16,128]{3,2,1,0:T(8,128)(2,1)S(1)}, u32[]{:S(2)}, u32[]{:S(2)}) collective-permute-start(bf16[1,16,16,128]{3,2,1,0:T(8,128)(2,1)S(1)} %dynamic-slice_bitcast_fusion.1), channel_id=1, source_target_pairs={{0,4},{1,5},{2,6},{3,7},{4,0},{5,1},{6,2},{7,3},{8,12},{9,13},{10,... | collective-permute-start | bytes 196616 | tf_op jit(solution)/shard_map/ppermute | solution.py:342
  80.8 4.0 %collective-permute-done.24 = bf16[1,16,16,128]{3,2,1,0:T(8,128)(2,1)S(1)} collective-permute-done((bf16[1,16,16,128]{3,2,1,0:T(8,128)(2,1)S(1)}, bf16[1,16,16,128]{3,2,1,0:T(8,128)(2,1)S(1)}, u32[]{:S(2)}, u32[]{:S(2)}) %collective-permute-start.24) | collective-permute-done | bytes 65568 | tf_op jit(solution)/shard_map/ppermute | solution.py:342
  84.8 0.0 copy-start.1
  84.9 0.8 constant_dynamic-update-slice_fusion
  85.7 0.0 copy-start
  85.7 0.7 copy-done
  (28 shorter events, 0.3 us)
Async XLA Ops:
  2.7 3.2 %collective-permute-start.4 = (bf16[2,16,16,128]{3,2,1,0:T(8,128)(2,1)S(1)}, bf16[2,16,16,128]{3,2,1,0:T(8,128)(2,1)S(1)}, u32[]{:S(2)}, u32[]{:S(2)}) collective-permute-start(bf16[2,16,16,128]{3,2,1,0:T(8,128)(2,1)S(1)} %get-tuple-element.33), channel_id=1, source_target_pairs={{0,8},{8,0},{16,24},{24,16},{1,9},{9,1},{17,25},{25,17},{2,10},{10... | collective-permute-start | bytes 393224 | tf_op jit(solution)/shard_map/ppermute | solution.py:331
  3.3 6.9 %collective-permute-start.5 = (bf16[2,16,16,128]{3,2,1,0:T(8,128)(2,1)S(1)}, bf16[2,16,16,128]{3,2,1,0:T(8,128)(2,1)S(1)}, u32[]{:S(2)}, u32[]{:S(2)}) collective-permute-start(bf16[2,16,16,128]{3,2,1,0:T(8,128)(2,1)S(1)} %get-tuple-element.34), channel_id=1, source_target_pairs={{0,16},{8,24},{16,0},{24,8},{1,17},{9,25},{17,1},{25,9},{2,18},{10... | collective-permute-start | bytes 393224 | tf_op jit(solution)/shard_map/ppermute | solution.py:331
  5.9 6.6 %collective-permute-start.6 = (bf16[2,16,16,128]{3,2,1,0:T(8,128)(2,1)S(1)}, bf16[2,16,16,128]{3,2,1,0:T(8,128)(2,1)S(1)}, u32[]{:S(2)}, u32[]{:S(2)}) collective-permute-start(bf16[2,16,16,128]{3,2,1,0:T(8,128)(2,1)S(1)} %get-tuple-element.35), channel_id=1, source_target_pairs={{0,24},{8,16},{16,8},{24,0},{1,25},{9,17},{17,9},{25,1},{2,26},{10... | collective-permute-start | bytes 393224 | tf_op jit(solution)/shard_map/ppermute | solution.py:331
  16.6 6.4 %collective-permute-start.16 = (bf16[2,16,16,128]{3,2,1,0:T(8,128)(2,1)S(1)}, bf16[2,16,16,128]{3,2,1,0:T(8,128)(2,1)S(1)}, u32[]{:S(2)}, u32[]{:S(2)}) collective-permute-start(bf16[2,16,16,128]{3,2,1,0:T(8,128)(2,1)S(1)} %get-tuple-element.49), channel_id=1, source_target_pairs={{0,16},{8,24},{16,0},{24,8},{1,17},{9,25},{17,1},{25,9},{2,18},{10... | collective-permute-start | bytes 393224 | tf_op jit(solution)/shard_map/ppermute | solution.py:331
  18.1 6.1 %collective-permute-start.17 = (bf16[2,16,16,128]{3,2,1,0:T(8,128)(2,1)S(1)}, bf16[2,16,16,128]{3,2,1,0:T(8,128)(2,1)S(1)}, u32[]{:S(2)}, u32[]{:S(2)}) collective-permute-start(bf16[2,16,16,128]{3,2,1,0:T(8,128)(2,1)S(1)} %get-tuple-element.50), channel_id=1, source_target_pairs={{0,24},{8,16},{16,8},{24,0},{1,25},{9,17},{17,9},{25,1},{2,26},{10... | collective-permute-start | bytes 393224 | tf_op jit(solution)/shard_map/ppermute | solution.py:331
  18.1 6.1 %collective-permute-start.15 = (bf16[2,16,16,128]{3,2,1,0:T(8,128)(2,1)S(1)}, bf16[2,16,16,128]{3,2,1,0:T(8,128)(2,1)S(1)}, u32[]{:S(2)}, u32[]{:S(2)}) collective-permute-start(bf16[2,16,16,128]{3,2,1,0:T(8,128)(2,1)S(1)} %get-tuple-element.48), channel_id=1, source_target_pairs={{0,8},{8,0},{16,24},{24,16},{1,9},{9,1},{17,25},{25,17},{2,10},{10... | collective-permute-start | bytes 393224 | tf_op jit(solution)/shard_map/ppermute | solution.py:331
  25.3 9.2 %collective-permute-start.22 = (bf16[1,16,2,2,16,128]{5,4,1,2,3,0:T(8,128)(2,1)S(1)}, bf16[1,16,2,2,16,128]{5,4,1,2,3,0:T(8,128)(2,1)S(1)}, u32[]{:S(2)}, u32[]{:S(2)}) collective-permute-start(bf16[1,16,2,2,16,128]{5,4,1,2,3,0:T(8,128)(2,1)S(1)} %copy.11), channel_id=1, source_target_pairs={{0,1},{1,0},{2,3},{3,2},{4,5},{5,4},{6,7},{7,6},{8,9},{9,8},{10,11... | collective-permute-start | bytes 786440 | tf_op jit(solution)/shard_map/ppermute | solution.py:342
  27.3 18.5 %collective-permute-start.3 = (bf16[2,8,128,128]{3,2,1,0:T(8,128)(2,1)S(1)}, bf16[2,8,128,128]{3,2,1,0:T(8,128)(2,1)S(1)}, u32[]{:S(2)}, u32[]{:S(2)}) collective-permute-start(bf16[2,8,128,128]{3,2,1,0:T(8,128)(2,1)S(1)} %get-tuple-element.32), channel_id=1, source_target_pairs={{0,1},{1,0},{2,3},{3,2},{4,5},{5,4},{6,7},{7,6},{8,9},{9,8},{10,11... | collective-permute-start | bytes 1572872 | tf_op jit(solution)/shard_map/ppermute | solution.py:365
  27.4 9.1 %collective-permute-start = (bf16[2,8,16,128]{3,2,1,0:T(8,128)(2,1)S(1)}, bf16[2,8,16,128]{3,2,1,0:T(8,128)(2,1)S(1)}, u32[]{:S(2)}, u32[]{:S(2)}) collective-permute-start(bf16[2,8,16,128]{3,2,1,0:T(8,128)(2,1)S(1)} %get-tuple-element.29), channel_id=1, source_target_pairs={{0,8},{8,0},{16,24},{24,16},{1,9},{9,1},{17,25},{25,17},{2,10},{10... | collective-permute-start | bytes 196616 | tf_op jit(solution)/shard_map/ppermute | solution.py:331
  27.5 10.7 %collective-permute-start.1 = (bf16[2,8,16,128]{3,2,1,0:T(8,128)(2,1)S(1)}, bf16[2,8,16,128]{3,2,1,0:T(8,128)(2,1)S(1)}, u32[]{:S(2)}, u32[]{:S(2)}) collective-permute-start(bf16[2,8,16,128]{3,2,1,0:T(8,128)(2,1)S(1)} %get-tuple-element.30), channel_id=1, source_target_pairs={{0,16},{8,24},{16,0},{24,8},{1,17},{9,25},{17,1},{25,9},{2,18},{10... | collective-permute-start | bytes 196616 | tf_op jit(solution)/shard_map/ppermute | solution.py:331
  29.3 8.9 %collective-permute-start.2 = (bf16[2,8,16,128]{3,2,1,0:T(8,128)(2,1)S(1)}, bf16[2,8,16,128]{3,2,1,0:T(8,128)(2,1)S(1)}, u32[]{:S(2)}, u32[]{:S(2)}) collective-permute-start(bf16[2,8,16,128]{3,2,1,0:T(8,128)(2,1)S(1)} %get-tuple-element.31), channel_id=1, source_target_pairs={{0,24},{8,16},{16,8},{24,0},{1,25},{9,17},{17,9},{25,1},{2,26},{10... | collective-permute-start | bytes 196616 | tf_op jit(solution)/shard_map/ppermute | solution.py:331
  34.6 16.6 %collective-permute-start.18 = (bf16[1,16,2,2,16,128]{5,4,1,3,2,0:T(8,128)(2,1)S(1)}, bf16[1,16,2,2,16,128]{5,4,1,3,2,0:T(8,128)(2,1)S(1)}, u32[]{:S(2)}, u32[]{:S(2)}) collective-permute-start(bf16[1,16,2,2,16,128]{5,4,1,3,2,0:T(8,128)(2,1)S(1)} %copy.9), channel_id=1, source_target_pairs={{0,1},{1,0},{2,3},{3,2},{4,5},{5,4},{6,7},{7,6},{8,9},{9,8},{10,11... | collective-permute-start | bytes 786440 | tf_op jit(solution)/shard_map/ppermute | solution.py:342
  36.6 23.6 %collective-permute-start.23 = (bf16[1,16,2,16,128]{4,3,1,2,0:T(8,128)(2,1)S(1)}, bf16[1,16,2,16,128]{4,3,1,2,0:T(8,128)(2,1)S(1)}, u32[]{:S(2)}, u32[]{:S(2)}) collective-permute-start(bf16[1,16,2,16,128]{4,3,1,2,0:T(8,128)(2,1)S(1)} %dynamic-slice_bitcast_fusion), channel_id=1, source_target_pairs={{0,2},{1,3},{2,0},{3,1},{4,6},{5,7},{6,4},{7,5},{8,10},{9,11},{10,... | collective-permute-start | bytes 393224 | tf_op jit(solution)/shard_map/ppermute | solution.py:342
  49.2 4.0 %collective-permute-start.8 = (bf16[2,8,16,128]{3,2,1,0:T(8,128)(2,1)S(1)}, bf16[2,8,16,128]{3,2,1,0:T(8,128)(2,1)S(1)}, u32[]{:S(2)}, u32[]{:S(2)}) collective-permute-start(bf16[2,8,16,128]{3,2,1,0:T(8,128)(2,1)S(1)} %get-tuple-element.40), channel_id=1, source_target_pairs={{0,8},{8,0},{16,24},{24,16},{1,9},{9,1},{17,25},{25,17},{2,10},{10... | collective-permute-start | bytes 196616 | tf_op jit(solution)/shard_map/ppermute | solution.py:331
  49.2 6.6 %collective-permute-start.9 = (bf16[2,8,16,128]{3,2,1,0:T(8,128)(2,1)S(1)}, bf16[2,8,16,128]{3,2,1,0:T(8,128)(2,1)S(1)}, u32[]{:S(2)}, u32[]{:S(2)}) collective-permute-start(bf16[2,8,16,128]{3,2,1,0:T(8,128)(2,1)S(1)} %get-tuple-element.41), channel_id=1, source_target_pairs={{0,16},{8,24},{16,0},{24,8},{1,17},{9,25},{17,1},{25,9},{2,18},{10... | collective-permute-start | bytes 196616 | tf_op jit(solution)/shard_map/ppermute | solution.py:331
  51.1 4.7 %collective-permute-start.10 = (bf16[2,8,16,128]{3,2,1,0:T(8,128)(2,1)S(1)}, bf16[2,8,16,128]{3,2,1,0:T(8,128)(2,1)S(1)}, u32[]{:S(2)}, u32[]{:S(2)}) collective-permute-start(bf16[2,8,16,128]{3,2,1,0:T(8,128)(2,1)S(1)} %get-tuple-element.42), channel_id=1, source_target_pairs={{0,24},{8,16},{16,8},{24,0},{1,25},{9,17},{17,9},{25,1},{2,26},{10... | collective-permute-start | bytes 196616 | tf_op jit(solution)/shard_map/ppermute | solution.py:331
  51.3 34.3 %collective-permute-start.19 = (bf16[1,16,16,128]{3,2,1,0:T(8,128)(2,1)S(1)}, bf16[1,16,16,128]{3,2,1,0:T(8,128)(2,1)S(1)}, u32[]{:S(2)}, u32[]{:S(2)}) collective-permute-start(bf16[1,16,16,128]{3,2,1,0:T(8,128)(2,1)S(1)} %get-tuple-element.59), channel_id=1, source_target_pairs={{0,2},{1,3},{2,0},{3,1},{4,6},{5,7},{6,4},{7,5},{8,10},{9,11},{10,... | collective-permute-start | bytes 196616 | tf_op jit(solution)/shard_map/ppermute | solution.py:342
  53.2 32.5 %collective-permute-start.20 = (bf16[1,16,16,128]{3,2,1,0:T(8,128)(2,1)S(1)}, bf16[1,16,16,128]{3,2,1,0:T(8,128)(2,1)S(1)}, u32[]{:S(2)}, u32[]{:S(2)}) collective-permute-start(bf16[1,16,16,128]{3,2,1,0:T(8,128)(2,1)S(1)} %get-tuple-element.61), channel_id=1, source_target_pairs={{0,4},{1,5},{2,6},{3,7},{4,0},{5,1},{6,2},{7,3},{8,12},{9,13},{10,... | collective-permute-start | bytes 196616 | tf_op jit(solution)/shard_map/ppermute | solution.py:342
  56.6 7.7 %collective-permute-start.11 = (bf16[2,8,2,16,128]{4,3,2,1,0:T(8,128)(2,1)S(1)}, bf16[2,8,2,16,128]{4,3,2,1,0:T(8,128)(2,1)S(1)}, u32[]{:S(2)}, u32[]{:S(2)}) collective-permute-start(bf16[2,8,2,16,128]{4,3,2,1,0:T(8,128)(2,1)S(1)} %get-tuple-element.44), channel_id=1, source_target_pairs={{0,2},{1,3},{2,0},{3,1},{4,6},{5,7},{6,4},{7,5},{8,10},{9,11},{10,... | collective-permute-start | bytes 393224 | tf_op jit(solution)/shard_map/ppermute | solution.py:342
  57.5 14.3 %collective-permute-start.12 = (bf16[2,8,2,16,128]{4,3,2,1,0:T(8,128)(2,1)S(1)}, bf16[2,8,2,16,128]{4,3,2,1,0:T(8,128)(2,1)S(1)}, u32[]{:S(2)}, u32[]{:S(2)}) collective-permute-start(bf16[2,8,2,16,128]{4,3,2,1,0:T(8,128)(2,1)S(1)} %get-tuple-element.45), channel_id=1, source_target_pairs={{0,4},{1,5},{2,6},{3,7},{4,0},{5,1},{6,2},{7,3},{8,12},{9,13},{10,... | collective-permute-start | bytes 393224 | tf_op jit(solution)/shard_map/ppermute | solution.py:342
  60.2 13.2 %collective-permute-start.13 = (bf16[2,8,2,16,128]{4,3,2,1,0:T(8,128)(2,1)S(1)}, bf16[2,8,2,16,128]{4,3,2,1,0:T(8,128)(2,1)S(1)}, u32[]{:S(2)}, u32[]{:S(2)}) collective-permute-start(bf16[2,8,2,16,128]{4,3,2,1,0:T(8,128)(2,1)S(1)} %get-tuple-element.46), channel_id=1, source_target_pairs={{0,6},{1,7},{2,4},{3,5},{4,2},{5,3},{6,0},{7,1},{8,14},{9,15},{10,... | collective-permute-start | bytes 393224 | tf_op jit(solution)/shard_map/ppermute | solution.py:342
  64.4 21.3 %collective-permute-start.21 = (bf16[1,16,16,128]{3,2,1,0:T(8,128)(2,1)S(1)}, bf16[1,16,16,128]{3,2,1,0:T(8,128)(2,1)S(1)}, u32[]{:S(2)}, u32[]{:S(2)}) collective-permute-start(bf16[1,16,16,128]{3,2,1,0:T(8,128)(2,1)S(1)} %get-tuple-element.60), channel_id=1, source_target_pairs={{0,6},{1,7},{2,4},{3,5},{4,2},{5,3},{6,0},{7,1},{8,14},{9,15},{10,... | collective-permute-start | bytes 196616 | tf_op jit(solution)/shard_map/ppermute | solution.py:342
  71.9 13.0 %collective-permute-start.7 = (bf16[8,128,128]{2,1,0:T(8,128)(2,1)S(1)}, bf16[8,128,128]{2,1,0:T(8,128)(2,1)S(1)}, u32[]{:S(2)}, u32[]{:S(2)}) collective-permute-start(bf16[8,128,128]{2,1,0:T(8,128)(2,1)S(1)} %get-tuple-element.38), channel_id=1, source_target_pairs={{0,1},{1,0},{2,3},{3,2},{4,5},{5,4},{6,7},{7,6},{8,9},{9,8},{10,11... | collective-permute-start | bytes 786440 | tf_op jit(solution)/shard_map/ppermute | solution.py:365
  73.5 5.4 %collective-permute-start.14 = (bf16[2,8,16,128]{3,2,1,0:T(8,128)(2,1)S(1)}, bf16[2,8,16,128]{3,2,1,0:T(8,128)(2,1)S(1)}, u32[]{:S(2)}, u32[]{:S(2)}) collective-permute-start(bf16[2,8,16,128]{3,2,1,0:T(8,128)(2,1)S(1)} %fusion.12), channel_id=1, source_target_pairs={{0,1},{1,0},{2,3},{3,2},{4,5},{5,4},{6,7},{7,6},{8,9},{9,8},{10,11... | collective-permute-start | bytes 196616 | tf_op jit(solution)/shard_map/ppermute | solution.py:365
  79.0 5.9 %collective-permute-start.24 = (bf16[1,16,16,128]{3,2,1,0:T(8,128)(2,1)S(1)}, bf16[1,16,16,128]{3,2,1,0:T(8,128)(2,1)S(1)}, u32[]{:S(2)}, u32[]{:S(2)}) collective-permute-start(bf16[1,16,16,128]{3,2,1,0:T(8,128)(2,1)S(1)} %dynamic-slice_bitcast_fusion.1), channel_id=1, source_target_pairs={{0,4},{1,5},{2,6},{3,7},{4,0},{5,1},{6,2},{7,3},{8,12},{9,13},{10,... | collective-permute-start | bytes 196616 | tf_op jit(solution)/shard_map/ppermute | solution.py:342
  84.8 0.8 copy-start.1
  85.7 0.7 copy-start
